TPU v7x, 256 devices: a whole 4x4x8 slice. The times are simulated.
256 devices in a mesh: section: 8 (over y, z_hi), expert: 32 (over x, z_lo, core).
Axes of the slice: x: 4, y: 4, z: 8 (z_hi: 2, z_lo: 4; z = z_hi * 4 + z_lo), core: 2. Of those that a mesh axis runs over, the one named last changes fastest.
Arguments:
- embedded: bfloat16 [4096, 3584], P('expert'), may hold values from -6 to 6
- forward_held: bfloat16 [8, 4096, 3584], P('section', 'expert'), may hold values from -6 to 6
- forward_route: int32 [8, 4096, 1], P('section', 'expert'), may hold values from 0 to 7; in each aligned block of 128 rows (0 to 127, 128 to 255, ..., all dimensions but the last counted through in order) at most 24 rows name the same one
- forward_weight: float32 [8, 4096], P('section', 'expert'), may hold values from 0.2 to 1
- loss_cotangent: bfloat16 [4096, 3584], P('expert'), may hold values from -6 to 6
- backward_held: bfloat16 [8, 4096, 3584], P('section', 'expert'), may hold values from -6 to 6
- backward_route: int32 [8, 4096, 1], P('section', 'expert'), may hold values from 0 to 7; in each aligned block of 128 rows (0 to 127, 128 to 255, ..., all dimensions but the last counted through in order) at most 24 rows name the same one
- backward_weight: float32 [8, 4096], P('section', 'expert'), may hold values from 0.2 to 1
- saved_gate: bfloat16 [8, 768, 8192], P('section', None, 'expert'), may hold values from -6 to 6
- saved_up: bfloat16 [8, 768, 8192], P('section', None, 'expert'), may hold values from -6 to 6
- gate_weight: bfloat16 [8, 3584, 8192], P('section', None, 'expert'), may hold values from -0.09375 to 0.09375
- up_weight: bfloat16 [8, 3584, 8192], P('section', None, 'expert'), may hold values from -0.09375 to 0.09375
- down_weight: bfloat16 [8, 8192, 3584], P('section', 'expert'), may hold values from -0.1875 to 0.1875
- steering: float32 [8, 3584], P('section'), may hold values from -6 to 6
Outputs:
- forward_out: bfloat16 [8, 4096, 3584], P('section', 'expert')
- forward_coefficient: float32 [8, 4096], P('section', 'expert')
- backward_out: bfloat16 [8, 4096, 3584], P('section', 'expert')
Inputs may be any that keep to these rules, and one draw needn't show every extreme that they name: `forward_route`: in each aligned block of 128 tokens of a layer (the tokens of one device) no expert is chosen more than 24 times, and some expert is chosen exactly 24 times in some block. `backward_route`: in each aligned block of 128 tokens of a layer (the tokens of one device) no expert is chosen more than 24 times, and some expert is chosen exactly 24 times in some block.
All inputs are finite; a program needn't handle non-finite values.
Results may differ from a plain program's by a relative error of at most 0.0058.
Values may be sent and summed in bfloat16 or wider, within the bound.
A program may use at most 64 MiB of HBM per device.

v0:
```python
import jax
import jax.numpy as jnp
from jax import lax
from jax.sharding import PartitionSpec as P

H = 1024


def shifted(value, axis, by):
    devices = lax.axis_size(axis)
    pairs = [(i, i + by) for i in range(devices) if 0 <= i + by < devices]
    return lax.ppermute(value, axis, pairs)


def dispatch_layout(expert_ids, expert_count, capacity):
    onehot = (expert_ids[:, None] == jnp.arange(expert_count, dtype=jnp.int32)[None, :]).astype(
        jnp.int32
    )
    earlier = jnp.cumsum(onehot, axis=0) - onehot
    position = jnp.sum(earlier * onehot, axis=1)
    target = expert_ids * capacity + position
    return (
        jnp.arange(expert_count * capacity, dtype=jnp.int32)[:, None] == target[None, :]
    ).astype(jnp.bfloat16)


def spread_rows(layout, tokens, holder_count, capacity):
    chosen = jnp.dot(layout, tokens, preferred_element_type=jnp.float32).astype(jnp.bfloat16)
    feature_count = tokens.shape[1]
    grouped = chosen.reshape(-1, 1, capacity, feature_count)
    copies = jnp.broadcast_to(grouped, (grouped.shape[0], holder_count, capacity, feature_count))
    return copies.reshape(-1, capacity, feature_count)


def merge_holders(arrived, expert_count, holder_count):
    capacity = arrived.shape[1]
    feature_count = arrived.shape[2]
    grouped = arrived.reshape(expert_count, holder_count, capacity, feature_count).astype(
        jnp.float32
    )
    return (
        jnp.sum(grouped, axis=1)
        .astype(jnp.bfloat16)
        .reshape(expert_count * capacity, feature_count)
    )


def expert_forward(slot_rows, weights):
    gate_cols, up_cols, down_rows = weights
    gate_pre = jnp.dot(slot_rows, gate_cols, preferred_element_type=jnp.float32)
    up_pre = jnp.dot(slot_rows, up_cols, preferred_element_type=jnp.float32)
    hidden = (jax.nn.silu(gate_pre) * up_pre).astype(jnp.bfloat16)
    return jnp.dot(hidden, down_rows, preferred_element_type=jnp.float32).astype(jnp.bfloat16)


def expert_backward(slot_rows, gate_saved, up_saved, weights):
    gate_cols, up_cols, down_rows = weights
    contract = (((1,), (1,)), ((), ()))
    grad_hidden = lax.dot_general(
        slot_rows, down_rows, contract, preferred_element_type=jnp.float32
    )
    gate_pre = gate_saved.astype(jnp.float32)
    up_pre = up_saved.astype(jnp.float32)
    sigmoid_gate = jax.nn.sigmoid(gate_pre)
    grad_gate = (
        grad_hidden * up_pre * sigmoid_gate * (1.0 + gate_pre * (1.0 - sigmoid_gate))
    ).astype(jnp.bfloat16)
    grad_up = (grad_hidden * gate_pre * sigmoid_gate).astype(jnp.bfloat16)
    grad_part = lax.dot_general(grad_gate, gate_cols, contract, preferred_element_type=jnp.float32)
    grad_part = grad_part + lax.dot_general(
        grad_up, up_cols, contract, preferred_element_type=jnp.float32
    )
    return grad_part.astype(jnp.bfloat16)


def over_slots(compute, inputs, feature_count):
    device_count = inputs[0].shape[0]
    capacity = inputs[0].shape[1]
    flattened = tuple(
        (member.reshape(device_count * capacity, member.shape[2]) for member in inputs)
    )
    return compute(*flattened).reshape(device_count, capacity, feature_count)


def body(
    embedded,
    forward_held,
    forward_route,
    forward_weight,
    loss_cotangent,
    backward_held,
    backward_route,
    backward_weight,
    saved_gate,
    saved_up,
    gate_weight,
    up_weight,
    down_weight,
    steering,
):
    section_count = lax.axis_size("section")
    section_index = lax.axis_index("section")
    device_count = lax.axis_size("expert")
    local_hidden = gate_weight.shape[2]
    holder_count = H // local_hidden
    expert_count = device_count // holder_count
    capacity = saved_gate.shape[1] // device_count
    feature_count = embedded.shape[1]
    arriving = shifted(forward_held, "section", 1)[0]
    forward_in = jnp.where(section_index == 0, embedded, arriving)
    returning = shifted(backward_held, "section", -1)[0]
    backward_in = jnp.where(section_index == section_count - 1, loss_cotangent, returning)
    direction = steering[0]
    unit_dir = direction / jnp.sqrt(jnp.sum(direction * direction) + 1e-06)
    weights = (gate_weight[0], up_weight[0], down_weight[0])
    forward_layout = dispatch_layout(forward_route[0, :, 0], expert_count, capacity)
    forward_send = spread_rows(forward_layout, forward_in, holder_count, capacity)
    backward_dy = backward_in.astype(jnp.float32)
    along_dir = jnp.sum(backward_dy * unit_dir[None, :], axis=1)
    sent_rows = (
        backward_weight[0][:, None] * (backward_dy - along_dir[:, None] * unit_dir[None, :])
    ).astype(jnp.bfloat16)
    backward_layout = dispatch_layout(backward_route[0, :, 0], expert_count, capacity)
    backward_send = spread_rows(backward_layout, sent_rows, holder_count, capacity)
    gate_saved = saved_gate[0].reshape(device_count, capacity, local_hidden)
    up_saved = saved_up[0].reshape(device_count, capacity, local_hidden)

    def forward_compute(slot_rows):
        return expert_forward(slot_rows, weights)

    def backward_compute(slot_rows, gate_rows, up_rows):
        return expert_backward(slot_rows, gate_rows, up_rows, weights)

    forward_arrived = lax.all_to_all(
        forward_send, "expert", split_axis=0, concat_axis=0, tiled=True
    )
    forward_part = over_slots(forward_compute, (forward_arrived,), feature_count)
    forward_back = lax.all_to_all(forward_part, "expert", split_axis=0, concat_axis=0, tiled=True)
    backward_arrived = lax.all_to_all(
        backward_send, "expert", split_axis=0, concat_axis=0, tiled=True
    )
    backward_part = over_slots(
        backward_compute, (backward_arrived, gate_saved, up_saved), feature_count
    )
    backward_back = lax.all_to_all(backward_part, "expert", split_axis=0, concat_axis=0, tiled=True)
    contract = (((0,), (0,)), ((), ()))
    forward_rows = merge_holders(forward_back, expert_count, holder_count)
    picked = lax.dot_general(
        forward_layout, forward_rows, contract, preferred_element_type=jnp.float32
    )
    mixed_rows = forward_weight[0][:, None] * picked
    coefficient = jnp.sum(mixed_rows * unit_dir[None, :], axis=1)
    forward_out = (
        forward_in.astype(jnp.float32) + mixed_rows - coefficient[:, None] * unit_dir[None, :]
    ).astype(jnp.bfloat16)
    backward_rows = merge_holders(backward_back, expert_count, holder_count)
    returned = lax.dot_general(
        backward_layout, backward_rows, contract, preferred_element_type=jnp.float32
    )
    backward_out = (backward_dy + returned).astype(jnp.bfloat16)
    return (forward_out[None], coefficient[None], backward_out[None])


def solution(mesh):
    in_specs = (
        P("expert", None),
        P("section", "expert", None),
        P("section", "expert", None),
        P("section", "expert"),
        P("expert", None),
        P("section", "expert", None),
        P("section", "expert", None),
        P("section", "expert"),
        P("section", None, "expert"),
        P("section", None, "expert"),
        P("section", None, "expert"),
        P("section", None, "expert"),
        P("section", "expert", None),
        P("section", None),
    )
    out_specs = (P("section", "expert", None), P("section", "expert"), P("section", "expert", None))
    return jax.shard_map(body, mesh=mesh, in_specs=in_specs, out_specs=out_specs, check_vma=False)
```

profile of v0, /device:TPU:24, one launch (start us, length us, event | category | flops | bytes accessed | tf_op | source)
XLA Modules:
  0.0 642.6 jit_solution(6075756311747875402)
XLA Ops:
  0.6 9.2 %collective-permute-start = (bf16[1,128,3584]{2,1,0:T(8,128)(2,1)}, bf16[1,128,3584]{2,1,0:T(8,128)(2,1)S(1)}, u32[]{:S(2)}, u32[]{:S(2)}) collective-permute-start(bf16[1,128,3584]{2,1,0:T(8,128)(2,1)} %param.15), channel_id=1, source_target_pairs={{0,32},{32,64},{64,96},{96,128},{128,160},{160,192},{192,224},{1,3... | collective-permute-start | bytes 2752520 | tf_op jit(solution)/shard_map/ppermute | solution.py:12
  9.9 0.7 fusion.51
  10.6 0.2 reduce_window_sum.17
  10.8 0.8 select_reduce_fusion.1
  11.6 0.7 multiply_add_fusion.1
  12.3 23.2 %collective-permute-done = bf16[1,128,3584]{2,1,0:T(8,128)(2,1)S(1)} collective-permute-done((bf16[1,128,3584]{2,1,0:T(8,128)(2,1)}, bf16[1,128,3584]{2,1,0:T(8,128)(2,1)S(1)}, u32[]{:S(2)}, u32[]{:S(2)}) %collective-permute-start) | collective-permute-done | bytes 917536 | tf_op jit(solution)/shard_map/ppermute | solution.py:12
  35.5 0.5 convolution_convert_fusion.2
  36.0 0.4 broadcast_in_dim.15
  36.4 146.5 %all_to_all.20 = bf16[32,24,3584]{2,1,0:T(8,128)(2,1)S(1)} all-to-all(bf16[32,24,3584]{2,1,0:T(8,128)(2,1)S(1)} %bitcast.76), channel_id=1, replica_groups=mesh['section'=8,'expert'=32] {'expert'}, dimensions={0} | all-to-all | bytes 11010048 | tf_op jit(solution)/shard_map/all_to_all | solution.py:134
  182.9 2.5 copy-done.1
  185.4 1.6 fusion.13
  187.0 11.3 %convolution_convert_fusion = bf16[768,3584]{1,0:T(8,128)(2,1)} fusion(bf16[1,256,3584]{2,1,0:T(8,128)(2,1)} %param.26, bf16[768,3584]{1,0:T(8,128)(2,1)} %bitcast.80, bf16[1,3584,256]{2,1,0:T(8,128)(2,1)S(1)} %copy-done, f32[768,256]{1,0:T(8,128)S(1)} %fusion.13), kind=kOutput, calls=%fused_computation.1 | convolution fusion | flops 2822504448 | bytes 15466496 | tf_op jit(solution)/shard_map/dot_general | solution.py:53
  198.3 5.0 all-to-all-start.1
  203.3 4.6 collective-permute-start.1
  208.0 0.6 multiply_reduce_fusion.1
  209.3 0.2 reduce_window_sum.18
  209.5 0.2 select_reduce_fusion
  209.7 156.4 %all-to-all-done.1 = bf16[32,24,3584]{2,1,0:T(8,128)(2,1)} async-done(((bf16[32,24,3584]{2,1,0:T(8,128)(2,1)}), bf16[32,24,3584]{2,1,0:T(8,128)(2,1)}, u32[]{:S(2)}, u32[]{:S(2)}) %all-to-all-start.1) | async-done | bytes 5505056 | tf_op jit(solution)/shard_map/all_to_all | solution.py:138
  366.1 3.4 bitcast_reduce_fusion.1
  369.6 0.9 copy-done.7
  370.5 3.2 fusion.2
  373.7 0.6 convolution_convert_fusion.1
  374.3 0.4 broadcast_in_dim.19
  374.7 127.2 %all_to_all.21 = bf16[32,24,3584]{2,1,0:T(8,128)(2,1)S(1)} all-to-all(bf16[32,24,3584]{2,1,0:T(8,128)(2,1)S(1)} %bitcast.77), channel_id=1, replica_groups=mesh['section'=8,'expert'=32] {'expert'}, dimensions={0} | all-to-all | bytes 11010048 | tf_op jit(solution)/shard_map/all_to_all | solution.py:139
  501.9 1.6 fusion.5
  503.6 1.8 fusion.11
  505.4 4.2 add_convert_fusion
  509.5 4.9 all-to-all-start.3
  514.4 3.1 fusion.23
  517.5 120.4 %all-to-all-done.3 = bf16[32,24,3584]{2,1,0:T(8,128)(2,1)} async-done(((bf16[32,24,3584]{2,1,0:T(8,128)(2,1)}), bf16[32,24,3584]{2,1,0:T(8,128)(2,1)}, u32[]{:S(2)}, u32[]{:S(2)}) %all-to-all-start.3) | async-done | bytes 5505056 | tf_op jit(solution)/shard_map/all_to_all | solution.py:145
  637.9 3.3 bitcast_reduce_fusion
  641.3 1.4 fusion.1
  (32 shorter events, 0.2 us)
Async XLA Ops:
  0.6 186.3 %copy-start = (bf16[1,3584,256]{2,1,0:T(8,128)(2,1)S(1)}, bf16[1,3584,256]{2,1,0:T(8,128)(2,1)}, u32[]{:S(2)}) copy-start(bf16[1,3584,256]{2,1,0:T(8,128)(2,1)} %param.25) | copy-start | bytes 5505028
  0.6 34.8 %collective-permute-start = (bf16[1,128,3584]{2,1,0:T(8,128)(2,1)}, bf16[1,128,3584]{2,1,0:T(8,128)(2,1)S(1)}, u32[]{:S(2)}, u32[]{:S(2)}) collective-permute-start(bf16[1,128,3584]{2,1,0:T(8,128)(2,1)} %param.15), channel_id=1, source_target_pairs={{0,32},{32,64},{64,96},{96,128},{128,160},{160,192},{192,224},{1,3... | collective-permute-start | bytes 2752520 | tf_op jit(solution)/shard_map/ppermute | solution.py:12
  35.5 0.9 copy-start.2
  36.4 149.0 %copy-start.3 = (bf16[1,3584,256]{2,1,0:T(8,128)(2,1)S(1)}, bf16[1,3584,256]{2,1,0:T(8,128)(2,1)}, u32[]{:S(2)}) copy-start(bf16[1,3584,256]{2,1,0:T(8,128)(2,1)} %param.24) | copy-start | bytes 5505028
  182.9 2.5 copy-start.1
  198.3 9.6 %copy-start.10 = (s32[1,128,1]{1,2,0:T(1,128)S(1)}, s32[1,128,1]{1,2,0:T(1,128)}, u32[]{:S(2)}) copy-start(s32[1,128,1]{1,2,0:T(1,128)} %param.20) | copy-start | bytes 1540
  198.3 9.7 %copy-start.9 = (f32[1,3584]{1,0:T(1,128)S(1)}, f32[1,3584]{1,0:T(1,128)}, u32[]{:S(2)}) copy-start(f32[1,3584]{1,0:T(1,128)} %param.27) | copy-start | bytes 43012
  198.3 167.9 %all-to-all-start.1 = ((bf16[32,24,3584]{2,1,0:T(8,128)(2,1)}), bf16[32,24,3584]{2,1,0:T(8,128)(2,1)}, u32[]{:S(2)}, u32[]{:S(2)}) async-start(bf16[32,24,3584]{2,1,0:T(8,128)(2,1)} %bitcast.78), calls=%async_computation.1 | async-start | bytes 11010048 | tf_op jit(solution)/shard_map/all_to_all | solution.py:138
  203.3 166.2 %collective-permute-start.1 = (bf16[1,128,3584]{2,1,0:T(8,128)(2,1)}, bf16[1,128,3584]{2,1,0:T(8,128)(2,1)S(1)}, u32[]{:S(2)}, u32[]{:S(2)}) collective-permute-start(bf16[1,128,3584]{2,1,0:T(8,128)(2,1)} %param.19), channel_id=1, source_target_pairs={{32,0},{64,32},{96,64},{128,96},{160,128},{192,160},{224,192},{33,... | collective-permute-start | bytes 2752520 | tf_op jit(solution)/shard_map/ppermute | solution.py:12
  209.7 160.8 %copy-start.12 = (f32[1,128]{1,0:T(1,128)S(1)}, f32[1,128]{1,0:T(1,128)}, u32[]{:S(2)}) copy-start(f32[1,128]{1,0:T(1,128)} %param.17) | copy-start | bytes 1540
  366.1 4.4 copy-start.6
  369.6 0.9 copy-start.7
  370.5 3.2 copy-start.13
  373.7 140.7 %copy-start.11 = (f32[128]{0:T(128)}, f32[128]{0:T(128)S(1)}, u32[]{:S(2)}) copy-start(f32[128]{0:T(128)S(1)} %get-tuple-element.4) | copy-start | bytes 1540
  374.7 127.2 %copy-start.14 = (bf16[1,256,3584]{2,1,0:T(8,128)(2,1)S(1)}, bf16[1,256,3584]{2,1,0:T(8,128)(2,1)}, u32[]{:S(2)}) copy-start(bf16[1,256,3584]{2,1,0:T(8,128)(2,1)} %param.26) | copy-start | bytes 5505028
  501.9 1.6 copy-start.4
  501.9 1.6 copy-start.5
  501.9 1.7 copy-start.8
  509.5 128.4 %all-to-all-start.3 = ((bf16[32,24,3584]{2,1,0:T(8,128)(2,1)}), bf16[32,24,3584]{2,1,0:T(8,128)(2,1)}, u32[]{:S(2)}, u32[]{:S(2)}) async-start(bf16[32,24,3584]{2,1,0:T(8,128)(2,1)} %bitcast.75), calls=%async_computation.3 | async-start | bytes 11010048 | tf_op jit(solution)/shard_map/all_to_all | solution.py:145
where the time goes:
time: 643 us
  waiting for transfers between devices  300 us (47%)
  blocking collectives  274 us (43%)
  matrix products  26.1 us (4%)
  starting transfers between devices  23.7 us (4%)
  other arithmetic  13.3 us (2%)
    all_to_all x1, waiting for transfers between devices, body(): lax.all_to_all(forward_part, 'expert', split_axis=0, concat_axis=0, tiled...  156 us
    all_to_all x1, blocking collectives, body(): lax.all_to_all(forward_send, 'expert', split_axis=0, concat_axis=0, tiled...  147 us
    all_to_all x1, blocking collectives, body(): lax.all_to_all(backward_send, 'expert', split_axis=0, concat_axis=0, tile...  127 us
    all_to_all x1, waiting for transfers between devices, body(): lax.all_to_all(backward_part, 'expert', split_axis=0, concat_axis=0, tile...  120 us
    ppermute x2, waiting for transfers between devices, shifted(): return lax.ppermute(value, axis, pairs)  23.2 us
    ppermute x2, starting transfers between devices, shifted(): return lax.ppermute(value, axis, pairs)  13.8 us
  transfers between devices with their start and end apart: 4, of which 3 were waited for; matrix products, arithmetic and copies ran while one was open for 2% of the time, Pallas kernels for 0%

commit v1 on v0

v1 whole, which is shorter than its diff:
```python
import jax
import jax.numpy as jnp
import numpy as np
from jax import lax
from jax.sharding import Mesh
from jax.sharding import PartitionSpec as P

H = 1024
EXPERT_AXES = ("ex", "em", "ep", "ec")
GROUP = ("ex", "em")
HOLDERS = ("ep", "ec")


def shifted(value, axis, by):
    devices = lax.axis_size(axis)
    pairs = [(i, i + by) for i in range(devices) if 0 <= i + by < devices]
    return lax.ppermute(value, axis, pairs)


def dispatch_layout(expert_ids, expert_count, capacity):
    onehot = (expert_ids[:, None] == jnp.arange(expert_count, dtype=jnp.int32)[None, :]).astype(
        jnp.int32
    )
    earlier = jnp.cumsum(onehot, axis=0) - onehot
    position = jnp.sum(earlier * onehot, axis=1)
    target = expert_ids * capacity + position
    return (
        jnp.arange(expert_count * capacity, dtype=jnp.int32)[:, None] == target[None, :]
    ).astype(jnp.bfloat16)


def expert_forward(slot_rows, weights):
    gate_cols, up_cols, down_rows = weights
    gate_pre = jnp.dot(slot_rows, gate_cols, preferred_element_type=jnp.float32)
    up_pre = jnp.dot(slot_rows, up_cols, preferred_element_type=jnp.float32)
    hidden = (jax.nn.silu(gate_pre) * up_pre).astype(jnp.bfloat16)
    return jnp.dot(hidden, down_rows, preferred_element_type=jnp.float32).astype(jnp.bfloat16)


def expert_backward(slot_rows, gate_saved, up_saved, weights):
    gate_cols, up_cols, down_rows = weights
    contract = (((1,), (1,)), ((), ()))
    grad_hidden = lax.dot_general(
        slot_rows, down_rows, contract, preferred_element_type=jnp.float32
    )
    gate_pre = gate_saved.astype(jnp.float32)
    up_pre = up_saved.astype(jnp.float32)
    sigmoid_gate = jax.nn.sigmoid(gate_pre)
    grad_gate = (
        grad_hidden * up_pre * sigmoid_gate * (1.0 + gate_pre * (1.0 - sigmoid_gate))
    ).astype(jnp.bfloat16)
    grad_up = (grad_hidden * gate_pre * sigmoid_gate).astype(jnp.bfloat16)
    grad_part = lax.dot_general(grad_gate, gate_cols, contract, preferred_element_type=jnp.float32)
    grad_part = grad_part + lax.dot_general(
        grad_up, up_cols, contract, preferred_element_type=jnp.float32
    )
    return grad_part.astype(jnp.bfloat16)


def combine_holders(parts):
    swapped = lax.all_to_all(parts, "ec", split_axis=2, concat_axis=2, tiled=True)
    pair = swapped[:, :, 0].astype(jnp.float32) + swapped[:, :, 1].astype(jnp.float32)
    me = lax.axis_index("ep")
    mine = jnp.where(me == 0, pair[:, 0], pair[:, 1])
    other = jnp.where(me == 0, pair[:, 1], pair[:, 0]).astype(jnp.bfloat16)
    arrived = lax.ppermute(other, "ep", [(0, 1), (1, 0)])
    return (mine + arrived.astype(jnp.float32)).astype(jnp.bfloat16)


def body(
    embedded,
    forward_held,
    forward_route,
    forward_weight,
    loss_cotangent,
    backward_held,
    backward_route,
    backward_weight,
    saved_gate,
    saved_up,
    gate_weight,
    up_weight,
    down_weight,
    steering,
):
    section_count = lax.axis_size("section")
    section_index = lax.axis_index("section")
    group_count = lax.axis_size(GROUP)
    holder_count = lax.axis_size(HOLDERS)
    local_hidden = gate_weight.shape[2]
    expert_count = group_count
    device_count = group_count * holder_count
    capacity = saved_gate.shape[1] // device_count
    feature_count = embedded.shape[1]
    arriving = shifted(forward_held, "section", 1)[0]
    forward_in = jnp.where(section_index == 0, embedded, arriving)
    returning = shifted(backward_held, "section", -1)[0]
    backward_in = jnp.where(section_index == section_count - 1, loss_cotangent, returning)
    direction = steering[0]
    unit_dir = direction / jnp.sqrt(jnp.sum(direction * direction) + 1e-06)
    weights = (gate_weight[0], up_weight[0], down_weight[0])

    forward_layout = dispatch_layout(forward_route[0, :, 0], expert_count, capacity)
    forward_send = jnp.dot(forward_layout, forward_in, preferred_element_type=jnp.float32).astype(
        jnp.bfloat16
    )
    backward_dy = backward_in.astype(jnp.float32)
    along_dir = jnp.sum(backward_dy * unit_dir[None, :], axis=1)
    sent_rows = (
        backward_weight[0][:, None] * (backward_dy - along_dir[:, None] * unit_dir[None, :])
    ).astype(jnp.bfloat16)
    backward_layout = dispatch_layout(backward_route[0, :, 0], expert_count, capacity)
    backward_send = jnp.dot(backward_layout, sent_rows, preferred_element_type=jnp.float32).astype(
        jnp.bfloat16
    )
    send = jnp.stack([forward_send, backward_send]).reshape(2, expert_count, capacity, feature_count)
    by_group = lax.all_to_all(send, GROUP, split_axis=1, concat_axis=1, tiled=True)
    gathered = lax.all_gather(by_group, HOLDERS, axis=1, tiled=False)
    rows = gathered.reshape(2, device_count * capacity, feature_count)

    def reorder(saved):
        return (
            saved[0]
            .reshape(group_count, holder_count, capacity, local_hidden)
            .transpose(1, 0, 2, 3)
            .reshape(device_count * capacity, local_hidden)
        )

    forward_part = expert_forward(rows[0], weights)
    backward_part = expert_backward(rows[1], reorder(saved_gate), reorder(saved_up), weights)
    parts = jnp.stack([forward_part, backward_part]).reshape(
        2, 2, 2, group_count, capacity, feature_count
    )
    summed = combine_holders(parts)
    back = lax.all_to_all(summed, GROUP, split_axis=1, concat_axis=1, tiled=True)
    back = back.reshape(2, expert_count * capacity, feature_count)

    contract = (((0,), (0,)), ((), ()))
    picked = lax.dot_general(forward_layout, back[0], contract, preferred_element_type=jnp.float32)
    mixed_rows = forward_weight[0][:, None] * picked
    coefficient = jnp.sum(mixed_rows * unit_dir[None, :], axis=1)
    forward_out = (
        forward_in.astype(jnp.float32) + mixed_rows - coefficient[:, None] * unit_dir[None, :]
    ).astype(jnp.bfloat16)
    returned = lax.dot_general(
        backward_layout, back[1], contract, preferred_element_type=jnp.float32
    )
    backward_out = (backward_dy + returned).astype(jnp.bfloat16)
    return (forward_out[None], coefficient[None], backward_out[None])


def solution(mesh):
    sections = mesh.shape["section"]
    experts = mesh.shape["expert"]
    fine = Mesh(
        np.asarray(mesh.devices).reshape(sections, experts // 8, 2, 2, 2),
        ("section",) + EXPERT_AXES,
    )
    E = EXPERT_AXES
    in_specs = (
        P(E, None),
        P("section", E, None),
        P("section", E, None),
        P("section", E),
        P(E, None),
        P("section", E, None),
        P("section", E, None),
        P("section", E),
        P("section", None, E),
        P("section", None, E),
        P("section", None, E),
        P("section", None, E),
        P("section", E, None),
        P("section", None),
    )
    out_specs = (P("section", E, None), P("section", E), P("section", E, None))
    return jax.shard_map(body, mesh=fine, in_specs=in_specs, out_specs=out_specs, check_vma=False)
```

time: 643 us -> 485 us (0.75)
  blocking collectives: 274 us -> 175 us
  waiting for transfers between devices: 300 us -> 209 us
  between operations: 1.58 us -> 15 us
  starting transfers between devices: 23.7 us -> 12.1 us
  local copies, waits for them, and re-layouts: 4.24 us -> 14.4 us
  matrix products: 26.1 us -> 35.6 us
  other arithmetic: 13.3 us -> 22 us
    all_to_all x2 -> x0, waiting for transfers between devices: 277 us -> none  [the longest x1 156 us: body(): lax.all_to_all(forward_part, 'expert', split_axis=0, concat_axis=0, tiled...]
    all_gather x0 -> x1, waiting for transfers between devices: none -> 101 us  [body(): gathered = lax.all_gather(by_group, HOLDERS, axis=1, tiled=False)]
    all_to_all x2 -> x3, blocking collectives: 274 us -> 175 us  [the longest x1 89.2 us: body(): lax.all_to_all(send, GROUP, split_axis=1, concat_axis=1, tiled=True)]
    ppermute x0 -> x1, waiting for transfers between devices: none -> 61.3 us  [combine_holders(): arrived = lax.ppermute(other, 'ep', [(0, 1), (1, 0)])]
    ppermute x2, waiting for transfers between devices: 23.2 us -> 47.3 us  [shifted(): return lax.ppermute(value, axis, pairs)]
    all_to_all x2 -> x0, starting transfers between devices: 9.91 us -> none  [the longest x1 5.03 us: body(): lax.all_to_all(forward_part, 'expert', split_axis=0, concat_axis=0, tiled...]
    slice x0 -> x2, local copies, waits for them, and re-layouts: none -> 9.19 us  [the longest x1 9 us: body(): forward_part = expert_forward(rows[0], weights)]
  transfers between devices with their start and end apart: 4 -> 4, of which waited for: 3 -> 4; matrix products, arithmetic and copies ran while one was open for 2% -> 2% of each run, Pallas kernels for 0% -> 0%
where the time goes in v1:
time: 485 us; the launch traced here: 483 us
  waiting for transfers between devices  209 us (43%)
  blocking collectives  175 us (36%)
  matrix products  35.6 us (7%)
  other arithmetic  22 us (5%)
  between operations  15 us (3%)
  local copies, waits for them, and re-layouts  14.4 us (3%)
  starting transfers between devices  12.1 us (2%)
    all_gather x1, waiting for transfers between devices, body(): gathered = lax.all_gather(by_group, HOLDERS, axis=1, tiled=False)  101 us
    all_to_all x1, blocking collectives, body(): lax.all_to_all(send, GROUP, split_axis=1, concat_axis=1, tiled=True)  89.2 us
    all_to_all x1, blocking collectives, body(): lax.all_to_all(summed, GROUP, split_axis=1, concat_axis=1, tiled=True)  69.8 us
    ppermute x1, waiting for transfers between devices, combine_holders(): arrived = lax.ppermute(other, 'ep', [(0, 1), (1, 0)])  61.3 us
    ppermute x2, waiting for transfers between devices, shifted(): return lax.ppermute(value, axis, pairs)  47.3 us
    all_to_all x1, blocking collectives, combine_holders(): lax.all_to_all(parts, 'ec', split_axis=2, concat_axis=2, tiled=True)  15.8 us
    ppermute x2, starting transfers between devices, shifted(): return lax.ppermute(value, axis, pairs)  11.5 us
    dot_general x1, matrix products, expert_forward(): jnp.dot(hidden, down_rows, preferred_element_type=jnp.float32)  11.3 us
  transfers between devices with their start and end apart: 4, of which 4 were waited for; matrix products, arithmetic and copies ran while one was open for 2% of the time, Pallas kernels for 0%

profile of v1, /device:TPU:24, one launch (start us, length us, event | category | flops | bytes accessed | tf_op | source)
XLA Modules:
  0.0 483.1 jit_solution(16857197294877407817)
XLA Ops:
  7.2 9.4 %collective-permute-start.1 = (bf16[1,128,3584]{2,1,0:T(8,128)(2,1)}, bf16[1,128,3584]{2,1,0:T(8,128)(2,1)}, u32[]{:S(2)}, u32[]{:S(2)}) collective-permute-start(bf16[1,128,3584]{2,1,0:T(8,128)(2,1)} %param.19), channel_id=1, source_target_pairs={{32,0},{64,32},{96,64},{128,96},{160,128},{192,160},{224,192},{33,... | collective-permute-start | bytes 2752520 | tf_op jit(solution)/shard_map/ppermute | solution.py:17
  16.7 2.1 collective-permute-start
  18.7 0.7 fusion.47
  19.6 0.9 select_reduce_fusion
  20.5 1.4 multiply_reduce_fusion.1
  22.6 0.8 divide_reduce_fusion
  24.0 0.7 fusion.48
  24.9 0.8 select_reduce_fusion.1
  26.4 31.0 %collective-permute-done.1 = bf16[1,128,3584]{2,1,0:T(8,128)(2,1)} collective-permute-done((bf16[1,128,3584]{2,1,0:T(8,128)(2,1)}, bf16[1,128,3584]{2,1,0:T(8,128)(2,1)}, u32[]{:S(2)}, u32[]{:S(2)}) %collective-permute-start.1) | collective-permute-done | bytes 917536 | tf_op jit(solution)/shard_map/ppermute | solution.py:17
  57.5 1.6 fusion.6
  59.7 16.3 %collective-permute-done = bf16[1,128,3584]{2,1,0:T(8,128)(2,1)} collective-permute-done((bf16[1,128,3584]{2,1,0:T(8,128)(2,1)}, bf16[1,128,3584]{2,1,0:T(8,128)(2,1)}, u32[]{:S(2)}, u32[]{:S(2)}) %collective-permute-start) | collective-permute-done | bytes 917536 | tf_op jit(solution)/shard_map/ppermute | solution.py:17
  76.0 1.7 convolution_convert_fusion.2
  77.9 89.2 %all_to_all.15 = bf16[2,8,24,3584]{3,2,0,1:T(8,128)(2,1)} all-to-all(bf16[2,8,24,3584]{3,2,0,1:T(8,128)(2,1)S(1)} %pad_maximum_fusion.1), channel_id=1, replica_groups=mesh['section'=8,'ex'=4,'em'=2,'ep'=2,'ec'=2] {'ex','em'}, dimensions={1} | all-to-all | bytes 5505024 | tf_op jit(solution)/shard_map/all_to_all | solution.py:117
  167.2 1.0 copy-done.8
  168.2 1.1 copy.37
  169.3 100.7 %all-gather.3.cloned.1.call-done = bf16[2,32,24,3584]{3,2,0,1:T(8,128)(2,1)} async-done(((bf16[2,8,24,3584]{3,2,0,1:T(8,128)(2,1)}), bf16[2,32,24,3584]{3,2,0,1:T(8,128)(2,1)}) %all-gather.3.cloned.1.call-update) | async-done | bytes 11010064 | tf_op jit(solution)/shard_map/all_gather | solution.py:118
  270.0 9.0 %fusion.54 = (bf16[1,32,24,3584]{3,2,0,1:T(8,128)(2,1)}, bf16[1,32,24,3584]{3,2,0,1:T(8,128)(2,1)}) fusion(bf16[2,32,24,3584]{3,2,0,1:T(8,128)(2,1)} %all-gather.3.cloned.1.call-done), kind=kLoop, calls=%fused_computation.78 | loop fusion | bytes 22020096 | tf_op jit(solution)/shard_map/slice | solution.py:129
  279.0 5.7 %fusion.17 = f32[768,256]{1,0:T(8,128)} fusion(bf16[768,3584]{1,0:T(8,128)(2,1)} %bitcast.127, bf16[1,3584,256]{2,1,0:T(8,128)(2,1)} %param.24), kind=kOutput, calls=%fused_computation.30 | convolution fusion | flops 1409286144 | bytes 8126464 | tf_op jit(solution)/shard_map/dot_general | solution.py:34
  284.7 2.5 fusion.40
  287.3 5.8 %fusion.15 = f32[768,3584]{1,0:T(8,128)} fusion(bf16[768,256]{1,0:T(8,128)(2,1)S(1)} %get-tuple-element.10, bf16[1,3584,256]{2,1,0:T(8,128)(2,1)S(1)} %copy-done.7), kind=kOutput, calls=%fused_computation.28 | convolution fusion | flops 1409286144 | bytes 13238272 | tf_op jit(solution)/shard_map/dot_general | solution.py:53
  293.1 11.3 %convolution_convert_fusion = bf16[768,3584]{1,0:T(8,128)(2,1)} fusion(bf16[1,256,3584]{2,1,0:T(8,128)(2,1)} %param.26, bf16[768,3584]{1,0:T(8,128)(2,1)} %bitcast.128, bf16[1,3584,256]{2,1,0:T(8,128)(2,1)S(1)} %copy-done, f32[768,256]{1,0:T(8,128)S(1)} %copy-done.14), kind=kOutput, calls=%fused_computation.3 | convolution fusion | flops 2822504448 | bytes 15466496 | tf_op jit(solution)/shard_map/dot_general | solution.py:37
  304.4 5.9 %add_convert_fusion = bf16[768,3584]{1,0:T(8,128)(2,1)S(1)} fusion(f32[768,3584]{1,0:T(8,128)} %fusion.15, bf16[768,256]{1,0:T(8,128)(2,1)S(1)} %copy-done.9, bf16[1,3584,256]{2,1,0:T(8,128)(2,1)S(1)} %copy-done), kind=kOutput, calls=%fused_computation.2 | convolution fusion | flops 1414791168 | bytes 18743296 | tf_op jit(solution)/shard_map/dot_general | solution.py:54
  310.4 1.1 pad_maximum_fusion
  311.5 1.8 copy.45
  313.3 15.8 %all_to_all.16 = bf16[2,2,2,8,24,3584]{5,4,3,1,0,2:T(8,128)(2,1)} all-to-all(bf16[2,2,2,8,24,3584]{5,4,3,1,0,2:T(8,128)(2,1)S(1)} %copy.45), channel_id=1, replica_groups=mesh['section'=8,'ex'=4,'em'=2,'ep'=2,'ec'=2] {'ec'}, dimensions={2} | all-to-all | bytes 22020096 | tf_op jit(solution)/shard_map/all_to_all | solution.py:61
  329.1 5.9 %add_bitcast_fusion = f32[2,2,8,24,3584]{4,3,2,1,0:T(8,128)S(1)} fusion(bf16[2,2,2,8,24,3584]{5,4,3,1,0,2:T(8,128)(2,1)} %all_to_all.16), kind=kLoop, calls=%fused_computation.1 | loop fusion | flops 8257536 | bytes 22020096 | tf_op jit(solution)/shard_map/add | solution.py:62
  336.0 61.3 %collective-permute-done.2 = bf16[2,8,24,3584]{3,2,1,0:T(8,128)(2,1)} collective-permute-done((bf16[2,8,24,3584]{3,2,1,0:T(8,128)(2,1)S(1)}, bf16[2,8,24,3584]{3,2,1,0:T(8,128)(2,1)}, u32[]{:S(2)}, u32[]{:S(2)}) %collective-permute-start.2) | collective-permute-done | bytes 2752544 | tf_op jit(solution)/shard_map/ppermute | solution.py:66
  397.4 3.2 fusion.2
  400.8 69.8 %all_to_all.17 = bf16[2,8,24,3584]{3,2,0,1:T(8,128)(2,1)S(1)} all-to-all(bf16[2,8,24,3584]{3,2,0,1:T(8,128)(2,1)S(1)} %copy.44), channel_id=1, replica_groups=mesh['section'=8,'ex'=4,'em'=2,'ep'=2,'ec'=2] {'ex','em'}, dimensions={1} | all-to-all | bytes 5505024 | tf_op jit(solution)/shard_map/all_to_all | solution.py:135
  470.7 1.0 copy-done.3
  471.7 1.4 fusion.4
  473.7 2.5 fusion.27
  (47 shorter events, 4.8 us)
Async XLA Ops:
  7.2 285.9 %copy-start = (bf16[1,3584,256]{2,1,0:T(8,128)(2,1)S(1)}, bf16[1,3584,256]{2,1,0:T(8,128)(2,1)}, u32[]{:S(2)}) copy-start(bf16[1,3584,256]{2,1,0:T(8,128)(2,1)} %param.25) | copy-start | bytes 5505028
  7.2 51.9 %copy-start.11 = (f32[1,128]{1,0:T(1,128)S(1)}, f32[1,128]{1,0:T(1,128)}, u32[]{:S(2)}) copy-start(f32[1,128]{1,0:T(1,128)} %param.21) | copy-start | bytes 1540
  7.2 262.8 %all-gather.3.cloned.1.call-start = ((), (), s32[]{:S(2)}) async-start(), calls=%async_computation.3 | async-start | bytes 13762560 | tf_op jit(solution)/shard_map/all_gather | solution.py:118
  7.2 50.2 %collective-permute-start.1 = (bf16[1,128,3584]{2,1,0:T(8,128)(2,1)}, bf16[1,128,3584]{2,1,0:T(8,128)(2,1)}, u32[]{:S(2)}, u32[]{:S(2)}) collective-permute-start(bf16[1,128,3584]{2,1,0:T(8,128)(2,1)} %param.19), channel_id=1, source_target_pairs={{32,0},{64,32},{96,64},{128,96},{160,128},{192,160},{224,192},{33,... | collective-permute-start | bytes 2752520 | tf_op jit(solution)/shard_map/ppermute | solution.py:17
  16.7 59.3 %collective-permute-start = (bf16[1,128,3584]{2,1,0:T(8,128)(2,1)}, bf16[1,128,3584]{2,1,0:T(8,128)(2,1)}, u32[]{:S(2)}, u32[]{:S(2)}) collective-permute-start(bf16[1,128,3584]{2,1,0:T(8,128)(2,1)} %param.15), channel_id=1, source_target_pairs={{0,32},{32,64},{64,96},{96,128},{128,160},{160,192},{192,224},{1,3... | collective-permute-start | bytes 2752520 | tf_op jit(solution)/shard_map/ppermute | solution.py:17
  19.6 56.3 %copy-start.5 = (bf16[128,3584]{1,0:T(8,128)(2,1)S(1)}, bf16[128,3584]{1,0:T(8,128)(2,1)}, u32[]{:S(2)}) copy-start(bf16[128,3584]{1,0:T(8,128)(2,1)} %param.14) | copy-start | bytes 2752516
  59.1 18.6 %copy-start.2 = (bf16[128,3584]{1,0:T(8,128)(2,1)}, bf16[128,3584]{1,0:T(8,128)(2,1)S(1)}, u32[]{:S(2)}) copy-start(bf16[128,3584]{1,0:T(8,128)(2,1)S(1)} %get-tuple-element.4) | copy-start | bytes 2752516
  167.1 1.0 copy-start.8
  279.0 5.7 %copy-start.4 = (bf16[1,32,24,3584]{3,2,0,1:T(8,128)(2,1)S(1)}, bf16[1,32,24,3584]{3,2,0,1:T(8,128)(2,1)}, u32[]{:S(2)}) copy-start(bf16[1,32,24,3584]{3,2,0,1:T(8,128)(2,1)} %get-tuple-element.6) | copy-start | bytes 16515076
  279.0 5.7 %copy-start.13 = (bf16[1,256,3584]{2,1,0:T(8,128)(2,1)S(1)}, bf16[1,256,3584]{2,1,0:T(8,128)(2,1)}, u32[]{:S(2)}) copy-start(bf16[1,256,3584]{2,1,0:T(8,128)(2,1)} %param.26) | copy-start | bytes 5505028
  284.7 2.5 copy-start.7
  287.3 5.8 %copy-start.14 = (f32[768,256]{1,0:T(8,128)S(1)}, f32[768,256]{1,0:T(8,128)}, u32[]{:S(2)}) copy-start(f32[768,256]{1,0:T(8,128)} %fusion.17) | copy-start | bytes 2359300
  293.1 11.3 %copy-start.9 = (bf16[768,256]{1,0:T(8,128)(2,1)S(1)}, bf16[768,256]{1,0:T(8,128)(2,1)}, u32[]{:S(2)}) copy-start(bf16[768,256]{1,0:T(8,128)(2,1)} %get-tuple-element.9) | copy-start | bytes 1179652
  304.4 5.9 %slice-start = ((s8[5505024]{0:T(1024)(128)(4,1)}), s8[4194304]{0:T(1024)(128)(4,1)S(1)}, s32[]{:S(2)}) async-start(s8[5505024]{0:T(1024)(128)(4,1)} %bitcast.130), calls=%async_computation.4 | async-start | bytes 8388608
  304.4 5.9 %slice-start.1 = ((s8[5505024]{0:T(1024)(128)(4,1)}), s8[1310720]{0:T(1024)(128)(4,1)S(1)}, s32[]{:S(2)}) async-start(s8[5505024]{0:T(1024)(128)(4,1)} %bitcast.130), calls=%async_computation.5 | async-start | bytes 2621440
  335.5 61.9 %collective-permute-start.2 = (bf16[2,8,24,3584]{3,2,1,0:T(8,128)(2,1)S(1)}, bf16[2,8,24,3584]{3,2,1,0:T(8,128)(2,1)}, u32[]{:S(2)}, u32[]{:S(2)}) collective-permute-start(bf16[2,8,24,3584]{3,2,1,0:T(8,128)(2,1)S(1)} %fusion.5), channel_id=1, source_target_pairs={{0,2},{2,0},{1,3},{3,1},{4,6},{6,4},{5,7},{7,5},{8,10},{10,8},{9,1... | collective-permute-start | bytes 8257544 | tf_op jit(solution)/shard_map/ppermute | solution.py:66
  470.5 1.2 copy-start.3
  470.7 2.4 copy-start.12
  471.7 2.0 copy-start.6
  473.1 3.1 copy-start.1
  473.6 2.6 copy-start.10
Sparse Core Ops, SparseCore 0:
  167.3 102.6 all-gather.2

commit v2 on v1

--- a/solution.py
+++ b/solution.py
@@ -57,14 +57,23 @@
     return grad_part.astype(jnp.bfloat16)
 
 
-def combine_holders(parts):
-    swapped = lax.all_to_all(parts, "ec", split_axis=2, concat_axis=2, tiled=True)
-    pair = swapped[:, :, 0].astype(jnp.float32) + swapped[:, :, 1].astype(jnp.float32)
-    me = lax.axis_index("ep")
-    mine = jnp.where(me == 0, pair[:, 0], pair[:, 1])
-    other = jnp.where(me == 0, pair[:, 1], pair[:, 0]).astype(jnp.bfloat16)
-    arrived = lax.ppermute(other, "ep", [(0, 1), (1, 0)])
-    return (mine + arrived.astype(jnp.float32)).astype(jnp.bfloat16)
+def swap_pair(value):
+    return lax.ppermute(value, "ep", [(0, 1), (1, 0)])
+
+
+def spread_to_holders(send):
+    own = lax.all_to_all(send, GROUP, split_axis=0, concat_axis=0, tiled=True)
+    other = swap_pair(own)
+    pair = jnp.stack([own, other])
+    return lax.all_gather(pair, "ec", axis=0, tiled=False)
+
+
+def collect_from_holders(parts):
+    swapped = lax.all_to_all(parts, "ec", split_axis=0, concat_axis=0, tiled=True)
+    pair = swapped[0].astype(jnp.float32) + swapped[1].astype(jnp.float32)
+    arrived = swap_pair(pair[1].astype(jnp.bfloat16))
+    summed = (pair[0] + arrived.astype(jnp.float32)).astype(jnp.bfloat16)
+    return lax.all_to_all(summed, GROUP, split_axis=0, concat_axis=0, tiled=True)
 
 
 def body(
@@ -92,6 +101,7 @@
     device_count = group_count * holder_count
     capacity = saved_gate.shape[1] // device_count
     feature_count = embedded.shape[1]
+    rows_shape = (device_count * capacity, feature_count)
     arriving = shifted(forward_held, "section", 1)[0]
     forward_in = jnp.where(section_index == 0, embedded, arriving)
     returning = shifted(backward_held, "section", -1)[0]
@@ -104,6 +114,8 @@
     forward_send = jnp.dot(forward_layout, forward_in, preferred_element_type=jnp.float32).astype(
         jnp.bfloat16
     )
+    forward_rows = spread_to_holders(forward_send.reshape(expert_count, capacity, feature_count))
+
     backward_dy = backward_in.astype(jnp.float32)
     along_dir = jnp.sum(backward_dy * unit_dir[None, :], axis=1)
     sent_rows = (
@@ -113,37 +125,35 @@
     backward_send = jnp.dot(backward_layout, sent_rows, preferred_element_type=jnp.float32).astype(
         jnp.bfloat16
     )
-    send = jnp.stack([forward_send, backward_send]).reshape(2, expert_count, capacity, feature_count)
-    by_group = lax.all_to_all(send, GROUP, split_axis=1, concat_axis=1, tiled=True)
-    gathered = lax.all_gather(by_group, HOLDERS, axis=1, tiled=False)
-    rows = gathered.reshape(2, device_count * capacity, feature_count)
+    backward_rows = spread_to_holders(backward_send.reshape(expert_count, capacity, feature_count))
+
+    flip = lax.axis_index("ep") == 1
 
     def reorder(saved):
-        return (
-            saved[0]
-            .reshape(group_count, holder_count, capacity, local_hidden)
-            .transpose(1, 0, 2, 3)
-            .reshape(device_count * capacity, local_hidden)
-        )
+        grouped = saved[0].reshape(group_count, 2, 2, capacity, local_hidden).transpose(2, 1, 0, 3, 4)
+        grouped = jnp.where(flip, grouped[:, ::-1], grouped)
+        return grouped.reshape(device_count * capacity, local_hidden)
 
-    forward_part = expert_forward(rows[0], weights)
-    backward_part = expert_backward(rows[1], reorder(saved_gate), reorder(saved_up), weights)
-    parts = jnp.stack([forward_part, backward_part]).reshape(
-        2, 2, 2, group_count, capacity, feature_count
+    forward_part = expert_forward(forward_rows.reshape(rows_shape), weights)
+    forward_back = collect_from_holders(
+        forward_part.reshape(2, 2, group_count, capacity, feature_count)
+    ).reshape(expert_count * capacity, feature_count)
+    backward_part = expert_backward(
+        backward_rows.reshape(rows_shape), reorder(saved_gate), reorder(saved_up), weights
     )
-    summed = combine_holders(parts)
-    back = lax.all_to_all(summed, GROUP, split_axis=1, concat_axis=1, tiled=True)
-    back = back.reshape(2, expert_count * capacity, feature_count)
+    backward_back = collect_from_holders(
+        backward_part.reshape(2, 2, group_count, capacity, feature_count)
+    ).reshape(expert_count * capacity, feature_count)
 
     contract = (((0,), (0,)), ((), ()))
-    picked = lax.dot_general(forward_layout, back[0], contract, preferred_element_type=jnp.float32)
+    picked = lax.dot_general(forward_layout, forward_back, contract, preferred_element_type=jnp.float32)
     mixed_rows = forward_weight[0][:, None] * picked
     coefficient = jnp.sum(mixed_rows * unit_dir[None, :], axis=1)
     forward_out = (
         forward_in.astype(jnp.float32) + mixed_rows - coefficient[:, None] * unit_dir[None, :]
     ).astype(jnp.bfloat16)
     returned = lax.dot_general(
-        backward_layout, back[1], contract, preferred_element_type=jnp.float32
+        backward_layout, backward_back, contract, preferred_element_type=jnp.float32
     )
     backward_out = (backward_dy + returned).astype(jnp.bfloat16)
     return (forward_out[None], coefficient[None], backward_out[None])

time: 485 us -> 487 us (level)
  waiting for transfers between devices: 209 us -> 277 us
  blocking collectives: 175 us -> 110 us
  starting transfers between devices: 12.1 us -> 31.4 us
  local copies, waits for them, and re-layouts: 14.4 us -> 3.94 us
  other arithmetic: 22 us -> 16.2 us
    all_gather x1 -> x2, waiting for transfers between devices: 101 us -> 34 us  [spread_to_holders(): return lax.all_gather(pair, 'ec', axis=0, tiled=False)]
    all_to_all x3 -> x4, blocking collectives: 175 us -> 110 us  [the longest x2 92.6 us: spread_to_holders(): own = lax.all_to_all(send, GROUP, split_axis=0, concat_axis=0, tiled=True)]
    ppermute x1 -> x4, waiting for transfers between devices: 61.3 us -> 123 us  [swap_pair(): return lax.ppermute(value, 'ep', [(0, 1), (1, 0)])]
    all_to_all x0 -> x2, waiting for transfers between devices: none -> 46.6 us  [collect_from_holders(): lax.all_to_all(summed, GROUP, split_axis=0, concat_axis=0, tiled=True)]
    ppermute x2, waiting for transfers between devices: 47.3 us -> 73.5 us  [shifted(): return lax.ppermute(value, axis, pairs)]
    all_to_all x0 -> x2, starting transfers between devices: none -> 12.7 us  [collect_from_holders(): lax.all_to_all(summed, GROUP, split_axis=0, concat_axis=0, tiled=True)]
    slice x2 -> x0, local copies, waits for them, and re-layouts: 9.19 us -> none  [the longest x1 9 us: body(): forward_part = expert_forward(rows[0], weights)]
    dot_general x2, matrix products: 1.93 us -> 6.89 us  [the longest x1 4.18 us: body(): lax.dot_general(forward_layout, forward_back, contract, preferred_element...]
  transfers between devices with their start and end apart: 4 -> 10, of which waited for: 4 -> 10; matrix products, arithmetic and copies ran while one was open for 2% -> 2% of each run, Pallas kernels for 0% -> 0%
where the time goes in v2:
time: 487 us; the launch traced here: 486 us
  waiting for transfers between devices  277 us (57%)
  blocking collectives  110 us (23%)
  matrix products  32.5 us (7%)
  starting transfers between devices  31.4 us (6%)
  other arithmetic  16.2 us (3%)
  between operations  15 us (3%)
    ppermute x4, waiting for transfers between devices, swap_pair(): return lax.ppermute(value, 'ep', [(0, 1), (1, 0)])  123 us
    all_to_all x2, blocking collectives, spread_to_holders(): own = lax.all_to_all(send, GROUP, split_axis=0, concat_axis=0, tiled=True)  92.6 us
    ppermute x2, waiting for transfers between devices, shifted(): return lax.ppermute(value, axis, pairs)  73.5 us
    all_to_all x2, waiting for transfers between devices, collect_from_holders(): lax.all_to_all(summed, GROUP, split_axis=0, concat_axis=0, tiled=True)  46.6 us
    all_gather x2, waiting for transfers between devices, spread_to_holders(): return lax.all_gather(pair, 'ec', axis=0, tiled=False)  34 us
    all_to_all x2, blocking collectives, collect_from_holders(): lax.all_to_all(parts, 'ec', split_axis=0, concat_axis=0, tiled=True)  17.8 us
    ppermute x2, starting transfers between devices, shifted(): return lax.ppermute(value, axis, pairs)  15.3 us
    all_to_all x2, starting transfers between devices, collect_from_holders(): lax.all_to_all(summed, GROUP, split_axis=0, concat_axis=0, tiled=True)  12.7 us
  transfers between devices with their start and end apart: 10, of which 10 were waited for; matrix products, arithmetic and copies ran while one was open for 2% of the time, Pallas kernels for 0%

profile of v2, /device:TPU:24, one launch (start us, length us, event | category | flops | bytes accessed | tf_op | source)
XLA Modules:
  0.0 486.4 jit_solution(16126653054294378699)
XLA Ops:
  7.2 9.2 %collective-permute-start = (bf16[1,128,3584]{2,1,0:T(8,128)(2,1)}, bf16[1,128,3584]{2,1,0:T(8,128)(2,1)S(1)}, u32[]{:S(2)}, u32[]{:S(2)}) collective-permute-start(bf16[1,128,3584]{2,1,0:T(8,128)(2,1)} %param.15), channel_id=1, source_target_pairs={{0,32},{32,64},{64,96},{96,128},{128,160},{160,192},{192,224},{1,3... | collective-permute-start | bytes 2752520 | tf_op jit(solution)/shard_map/ppermute | solution.py:17
  18.9 23.2 %collective-permute-done = bf16[1,128,3584]{2,1,0:T(8,128)(2,1)S(1)} collective-permute-done((bf16[1,128,3584]{2,1,0:T(8,128)(2,1)}, bf16[1,128,3584]{2,1,0:T(8,128)(2,1)S(1)}, u32[]{:S(2)}, u32[]{:S(2)}) %collective-permute-start) | collective-permute-done | bytes 917536 | tf_op jit(solution)/shard_map/ppermute | solution.py:17
  42.6 55.8 %all_to_all.30 = bf16[8,24,3584]{2,1,0:T(8,128)(2,1)S(1)} all-to-all(bf16[8,24,3584]{2,1,0:T(8,128)(2,1)S(1)} %bitcast.91), channel_id=1, replica_groups=mesh['section'=8,'ex'=4,'em'=2,'ep'=2,'ec'=2] {'ex','em'}, dimensions={0} | all-to-all | bytes 2752512 | tf_op jit(solution)/shard_map/all_to_all | solution.py:65
  98.4 31.1 %collective-permute-done.1 = bf16[8,24,3584]{2,1,0:T(8,128)(2,1)S(1)} collective-permute-done((bf16[8,24,3584]{2,1,0:T(8,128)(2,1)S(1)}, bf16[8,24,3584]{2,1,0:T(8,128)(2,1)S(1)}, u32[]{:S(2)}, u32[]{:S(2)}) %collective-permute-start.1) | collective-permute-done | bytes 1376288 | tf_op jit(solution)/shard_map/ppermute | solution.py:61
  129.6 1.8 pad_maximum_fusion
  131.4 18.4 %all-gather.5.cloned.1.call-done = bf16[4,8,24,3584]{3,2,1,0:T(8,128)(2,1)} async-done(((bf16[2,8,24,3584]{3,2,1,0:T(8,128)(2,1)}), bf16[4,8,24,3584]{3,2,1,0:T(8,128)(2,1)}) %all-gather.5.cloned.1.call-update) | async-done | bytes 5505040 | tf_op jit(solution)/shard_map/all_gather | solution.py:68
  149.8 4.7 fusion.17
  154.5 11.4 %convolution_convert_fusion = bf16[768,3584]{1,0:T(8,128)(2,1)} fusion(bf16[1,256,3584]{2,1,0:T(8,128)(2,1)} %param.26, bf16[768,3584]{1,0:T(8,128)(2,1)} %bitcast.110, bf16[1,3584,256]{2,1,0:T(8,128)(2,1)S(1)} %copy-done, f32[768,256]{1,0:T(8,128)S(1)} %fusion.17), kind=kOutput, calls=%fused_computation.1 | convolution fusion | flops 2822504448 | bytes 15466496 | tf_op jit(solution)/shard_map/dot_general | solution.py:37
  165.9 9.6 %all_to_all.31 = bf16[2,2,8,24,3584]{4,3,2,1,0:T(8,128)(2,1)S(1)} all-to-all(bf16[2,2,8,24,3584]{4,3,2,1,0:T(8,128)(2,1)} %bitcast.86), channel_id=1, replica_groups=mesh['section'=8,'ex'=4,'em'=2,'ep'=2,'ec'=2] {'ec'}, dimensions={0} | all-to-all | bytes 11010048 | tf_op jit(solution)/shard_map/all_to_all | solution.py:72
  176.4 1.6 collective-permute-start.2
  178.1 30.7 %collective-permute-done.2 = bf16[8,24,3584]{2,1,0:T(8,128)(2,1)S(1)} collective-permute-done((bf16[8,24,3584]{2,1,0:T(8,128)(2,1)S(1)}, bf16[8,24,3584]{2,1,0:T(8,128)(2,1)S(1)}, u32[]{:S(2)}, u32[]{:S(2)}) %collective-permute-start.2) | collective-permute-done | bytes 1376288 | tf_op jit(solution)/shard_map/ppermute | solution.py:61
  208.8 1.4 fusion.5
  210.2 6.4 %all-to-all-start.2 = ((bf16[8,24,3584]{2,1,0:T(8,128)(2,1)}), bf16[8,24,3584]{2,1,0:T(8,128)(2,1)S(1)}, u32[]{:S(2)}, u32[]{:S(2)}) async-start(bf16[8,24,3584]{2,1,0:T(8,128)(2,1)} %fusion.5), calls=%async_computation.2 | async-start | bytes 2752512 | tf_op jit(solution)/shard_map/all_to_all | solution.py:76
  216.6 6.1 %collective-permute-start.3 = (bf16[1,128,3584]{2,1,0:T(8,128)(2,1)}, bf16[1,128,3584]{2,1,0:T(8,128)(2,1)}, u32[]{:S(2)}, u32[]{:S(2)}) collective-permute-start(bf16[1,128,3584]{2,1,0:T(8,128)(2,1)} %param.19), channel_id=1, source_target_pairs={{32,0},{64,32},{96,64},{128,96},{160,128},{192,160},{224,192},{33,... | collective-permute-start | bytes 2752520 | tf_op jit(solution)/shard_map/ppermute | solution.py:17
  224.6 50.3 %collective-permute-done.3 = bf16[1,128,3584]{2,1,0:T(8,128)(2,1)} collective-permute-done((bf16[1,128,3584]{2,1,0:T(8,128)(2,1)}, bf16[1,128,3584]{2,1,0:T(8,128)(2,1)}, u32[]{:S(2)}, u32[]{:S(2)}) %collective-permute-start.3) | collective-permute-done | bytes 917536 | tf_op jit(solution)/shard_map/ppermute | solution.py:17
  275.0 15.3 %all-to-all-done.2 = bf16[8,24,3584]{2,1,0:T(8,128)(2,1)S(1)} async-done(((bf16[8,24,3584]{2,1,0:T(8,128)(2,1)}), bf16[8,24,3584]{2,1,0:T(8,128)(2,1)S(1)}, u32[]{:S(2)}, u32[]{:S(2)}) %all-to-all-start.2) | async-done | bytes 1376288 | tf_op jit(solution)/shard_map/all_to_all | solution.py:76
  291.3 4.2 fusion.6
  296.1 36.8 %all_to_all.32 = bf16[8,24,3584]{2,1,0:T(8,128)(2,1)S(1)} all-to-all(bf16[8,24,3584]{2,1,0:T(8,128)(2,1)S(1)} %bitcast.90), channel_id=1, replica_groups=mesh['section'=8,'ex'=4,'em'=2,'ep'=2,'ec'=2] {'ex','em'}, dimensions={0} | all-to-all | bytes 2752512 | tf_op jit(solution)/shard_map/all_to_all | solution.py:65
  332.9 30.4 %collective-permute-done.4 = bf16[8,24,3584]{2,1,0:T(8,128)(2,1)S(1)} collective-permute-done((bf16[8,24,3584]{2,1,0:T(8,128)(2,1)S(1)}, bf16[8,24,3584]{2,1,0:T(8,128)(2,1)S(1)}, u32[]{:S(2)}, u32[]{:S(2)}) %collective-permute-start.4) | collective-permute-done | bytes 1376288 | tf_op jit(solution)/shard_map/ppermute | solution.py:61
  363.4 1.8 pad_maximum_fusion.1
  367.7 1.6 reverse_select_fusion
  369.3 15.5 %all-gather.7.cloned.1.call-done = bf16[4,8,24,3584]{3,2,1,0:T(8,128)(2,1)} async-done(((bf16[2,8,24,3584]{3,2,1,0:T(8,128)(2,1)}), bf16[4,8,24,3584]{3,2,1,0:T(8,128)(2,1)}) %all-gather.7.cloned.1.call-update) | async-done | bytes 5505040 | tf_op jit(solution)/shard_map/all_gather | solution.py:68
  384.8 4.9 %fusion.9 = f32[768,256]{1,0:T(8,128)S(1)} fusion(bf16[768,3584]{1,0:T(8,128)(2,1)} %bitcast.108, bf16[1,256,3584]{2,1,0:T(8,128)(2,1)} %param.26), kind=kOutput, calls=%fused_computation.25 | convolution fusion | flops 1409286144 | bytes 8126464 | tf_op jit(solution)/shard_map/dot_general | solution.py:43
  389.7 1.8 fusion.15
  391.5 1.7 add_convert_fusion
  393.2 8.2 %all_to_all.33 = bf16[2,2,8,24,3584]{4,3,2,1,0:T(8,128)(2,1)S(1)} all-to-all(bf16[2,2,8,24,3584]{4,3,2,1,0:T(8,128)(2,1)S(1)} %bitcast.85), channel_id=1, replica_groups=mesh['section'=8,'ex'=4,'em'=2,'ep'=2,'ec'=2] {'ec'}, dimensions={0} | all-to-all | bytes 11010048 | tf_op jit(solution)/shard_map/all_to_all | solution.py:72
  402.3 1.6 collective-permute-start.5
  404.0 30.7 %collective-permute-done.5 = bf16[8,24,3584]{2,1,0:T(8,128)(2,1)S(1)} collective-permute-done((bf16[8,24,3584]{2,1,0:T(8,128)(2,1)S(1)}, bf16[8,24,3584]{2,1,0:T(8,128)(2,1)S(1)}, u32[]{:S(2)}, u32[]{:S(2)}) %collective-permute-start.5) | collective-permute-done | bytes 1376288 | tf_op jit(solution)/shard_map/ppermute | solution.py:61
  436.1 6.4 %all-to-all-start.5 = ((bf16[8,24,3584]{2,1,0:T(8,128)(2,1)}), bf16[8,24,3584]{2,1,0:T(8,128)(2,1)}, u32[]{:S(2)}, u32[]{:S(2)}) async-start(bf16[8,24,3584]{2,1,0:T(8,128)(2,1)} %fusion.3), calls=%async_computation.5 | async-start | bytes 2752512 | tf_op jit(solution)/shard_map/all_to_all | solution.py:76
  442.5 3.1 fusion.29
  445.5 31.4 %all-to-all-done.5 = bf16[8,24,3584]{2,1,0:T(8,128)(2,1)} async-done(((bf16[8,24,3584]{2,1,0:T(8,128)(2,1)}), bf16[8,24,3584]{2,1,0:T(8,128)(2,1)}, u32[]{:S(2)}, u32[]{:S(2)}) %all-to-all-start.5) | async-done | bytes 1376288 | tf_op jit(solution)/shard_map/all_to_all | solution.py:76
  476.9 2.7 fusion.1
  (51 shorter events, 11.7 us)
Async XLA Ops:
  7.2 147.3 %copy-start = (bf16[1,3584,256]{2,1,0:T(8,128)(2,1)S(1)}, bf16[1,3584,256]{2,1,0:T(8,128)(2,1)}, u32[]{:S(2)}) copy-start(bf16[1,3584,256]{2,1,0:T(8,128)(2,1)} %param.25) | copy-start | bytes 5505028
  7.2 142.6 %all-gather.5.cloned.1.call-start = ((), (), s32[]{:S(2)}) async-start(), calls=%async_computation.6 | async-start | bytes 8257536 | tf_op jit(solution)/shard_map/all_gather | solution.py:68
  7.2 34.8 %collective-permute-start = (bf16[1,128,3584]{2,1,0:T(8,128)(2,1)}, bf16[1,128,3584]{2,1,0:T(8,128)(2,1)S(1)}, u32[]{:S(2)}, u32[]{:S(2)}) collective-permute-start(bf16[1,128,3584]{2,1,0:T(8,128)(2,1)} %param.15), channel_id=1, source_target_pairs={{0,32},{32,64},{64,96},{96,128},{128,160},{160,192},{192,224},{1,3... | collective-permute-start | bytes 2752520 | tf_op jit(solution)/shard_map/ppermute | solution.py:17
  42.1 56.4 %copy-start.2 = (bf16[1,128,3584]{2,1,0:T(8,128)(2,1)}, bf16[1,128,3584]{2,1,0:T(8,128)(2,1)S(1)}, u32[]{:S(2)}) copy-start(bf16[1,128,3584]{2,1,0:T(8,128)(2,1)S(1)} %collective-permute-done) | copy-start | bytes 2752516
  98.4 31.1 %collective-permute-start.1 = (bf16[8,24,3584]{2,1,0:T(8,128)(2,1)S(1)}, bf16[8,24,3584]{2,1,0:T(8,128)(2,1)S(1)}, u32[]{:S(2)}, u32[]{:S(2)}) collective-permute-start(bf16[8,24,3584]{2,1,0:T(8,128)(2,1)S(1)} %all_to_all.30), channel_id=1, source_target_pairs={{0,2},{2,0},{1,3},{3,1},{4,6},{6,4},{5,7},{7,5},{8,10},{10,8},{9,1... | collective-permute-start | bytes 4128776 | tf_op jit(solution)/shard_map/ppermute | solution.py:61
  176.4 32.3 %collective-permute-start.2 = (bf16[8,24,3584]{2,1,0:T(8,128)(2,1)S(1)}, bf16[8,24,3584]{2,1,0:T(8,128)(2,1)S(1)}, u32[]{:S(2)}, u32[]{:S(2)}) collective-permute-start(bf16[8,24,3584]{2,1,0:T(8,128)(2,1)S(1)} %fusion.19), channel_id=1, source_target_pairs={{0,2},{2,0},{1,3},{3,1},{4,6},{6,4},{5,7},{7,5},{8,10},{10,8},{9,1... | collective-permute-start | bytes 4128776 | tf_op jit(solution)/shard_map/ppermute | solution.py:61
  210.2 12.6 %copy-start.6 = (f32[1,3584]{1,0:T(1,128)S(1)}, f32[1,3584]{1,0:T(1,128)}, u32[]{:S(2)}) copy-start(f32[1,3584]{1,0:T(1,128)} %param.27) | copy-start | bytes 43012
  210.2 13.9 %copy-start.7 = (s32[1,128,1]{1,2,0:T(1,128)S(1)}, s32[1,128,1]{1,2,0:T(1,128)}, u32[]{:S(2)}) copy-start(s32[1,128,1]{1,2,0:T(1,128)} %param.20) | copy-start | bytes 1540
  210.2 81.1 %copy-start.11 = (f32[1,128]{1,0:T(1,128)S(1)}, f32[1,128]{1,0:T(1,128)}, u32[]{:S(2)}) copy-start(f32[1,128]{1,0:T(1,128)} %param.17) | copy-start | bytes 1540
  210.2 80.0 %all-to-all-start.2 = ((bf16[8,24,3584]{2,1,0:T(8,128)(2,1)}), bf16[8,24,3584]{2,1,0:T(8,128)(2,1)S(1)}, u32[]{:S(2)}, u32[]{:S(2)}) async-start(bf16[8,24,3584]{2,1,0:T(8,128)(2,1)} %fusion.5), calls=%async_computation.2 | async-start | bytes 2752512 | tf_op jit(solution)/shard_map/all_to_all | solution.py:76
  216.6 168.3 %all-gather.7.cloned.1.call-start = ((), (), s32[]{:S(2)}) async-start(), calls=%async_computation.7 | async-start | bytes 8257536 | tf_op jit(solution)/shard_map/all_gather | solution.py:68
  216.6 58.3 %collective-permute-start.3 = (bf16[1,128,3584]{2,1,0:T(8,128)(2,1)}, bf16[1,128,3584]{2,1,0:T(8,128)(2,1)}, u32[]{:S(2)}, u32[]{:S(2)}) collective-permute-start(bf16[1,128,3584]{2,1,0:T(8,128)(2,1)} %param.19), channel_id=1, source_target_pairs={{32,0},{64,32},{96,64},{128,96},{160,128},{192,160},{224,192},{33,... | collective-permute-start | bytes 2752520 | tf_op jit(solution)/shard_map/ppermute | solution.py:17
  224.6 70.9 %copy-start.9 = (s32[128]{0:T(128)}, s32[128]{0:T(128)S(1)}, u32[]{:S(2)}) copy-start(s32[128]{0:T(128)S(1)} %multiply_add_fusion) | copy-start | bytes 1540
  290.2 1.1 copy-start.1
  291.3 4.2 copy-start.12
  332.9 30.4 %collective-permute-start.4 = (bf16[8,24,3584]{2,1,0:T(8,128)(2,1)S(1)}, bf16[8,24,3584]{2,1,0:T(8,128)(2,1)S(1)}, u32[]{:S(2)}, u32[]{:S(2)}) collective-permute-start(bf16[8,24,3584]{2,1,0:T(8,128)(2,1)S(1)} %all_to_all.32), channel_id=1, source_target_pairs={{0,2},{2,0},{1,3},{3,1},{4,6},{6,4},{5,7},{7,5},{8,10},{10,8},{9,1... | collective-permute-start | bytes 4128776 | tf_op jit(solution)/shard_map/ppermute | solution.py:61
  365.1 1.0 copy-start.4
  365.1 1.8 copy-start.5
  384.8 4.9 %copy-start.3 = (bf16[1,3584,256]{2,1,0:T(8,128)(2,1)S(1)}, bf16[1,3584,256]{2,1,0:T(8,128)(2,1)}, u32[]{:S(2)}) copy-start(bf16[1,3584,256]{2,1,0:T(8,128)(2,1)} %param.24) | copy-start | bytes 5505028
  402.3 32.3 %collective-permute-start.5 = (bf16[8,24,3584]{2,1,0:T(8,128)(2,1)S(1)}, bf16[8,24,3584]{2,1,0:T(8,128)(2,1)S(1)}, u32[]{:S(2)}, u32[]{:S(2)}) collective-permute-start(bf16[8,24,3584]{2,1,0:T(8,128)(2,1)S(1)} %fusion.20), channel_id=1, source_target_pairs={{0,2},{2,0},{1,3},{3,1},{4,6},{6,4},{5,7},{7,5},{8,10},{10,8},{9,1... | collective-permute-start | bytes 4128776 | tf_op jit(solution)/shard_map/ppermute | solution.py:61
  436.1 6.4 %copy-start.8 = (f32[128]{0:T(128)S(1)}, f32[128]{0:T(128)}, u32[]{:S(2)}) copy-start(f32[128]{0:T(128)} %get-tuple-element.4) | copy-start | bytes 1540
  436.1 40.8 %all-to-all-start.5 = ((bf16[8,24,3584]{2,1,0:T(8,128)(2,1)}), bf16[8,24,3584]{2,1,0:T(8,128)(2,1)}, u32[]{:S(2)}, u32[]{:S(2)}) async-start(bf16[8,24,3584]{2,1,0:T(8,128)(2,1)} %fusion.3), calls=%async_computation.5 | async-start | bytes 2752512 | tf_op jit(solution)/shard_map/all_to_all | solution.py:76
  442.4 34.4 %copy-start.10 = (s32[128]{0:T(128)S(1)}, s32[128]{0:T(128)}, u32[]{:S(2)}) copy-start(s32[128]{0:T(128)} %copy-done.9) | copy-start | bytes 1540
Sparse Core Ops, SparseCore 0:
  131.5 18.2 all-gather.4
  365.3 19.5 all-gather.6

commit v3 on v2

--- a/solution.py
+++ b/solution.py
@@ -1,7 +1,11 @@
+import functools
+
 import jax
 import jax.numpy as jnp
 import numpy as np
 from jax import lax
+from jax.experimental import pallas as pl
+from jax.experimental.pallas import tpu as pltpu
 from jax.sharding import Mesh
 from jax.sharding import PartitionSpec as P
 
@@ -9,6 +13,7 @@
 EXPERT_AXES = ("ex", "em", "ep", "ec")
 GROUP = ("ex", "em")
 HOLDERS = ("ep", "ec")
+MESH_IDS = pl.DeviceIdType.MESH
 
 
 def shifted(value, axis, by):
@@ -61,11 +66,128 @@
     return lax.ppermute(value, "ep", [(0, 1), (1, 0)])
 
 
-def spread_to_holders(send):
-    own = lax.all_to_all(send, GROUP, split_axis=0, concat_axis=0, tiled=True)
-    other = swap_pair(own)
-    pair = jnp.stack([own, other])
-    return lax.all_gather(pair, "ec", axis=0, tiled=False)
+def spread_kernel(groups, *refs):
+    streams = (len(refs) - 6) // 2
+    sends = refs[:streams]
+    rows = refs[streams : 2 * streams]
+    first_recv, first_send, pair_recv, pair_send, near_recv, near_send = refs[2 * streams : 2 * streams + 6]
+    section = lax.axis_index("section")
+    ex = lax.axis_index("ex")
+    em = lax.axis_index("em")
+    ep = lax.axis_index("ep")
+    ec = lax.axis_index("ec")
+    me = ex * 2 + em
+    partner = (section, ex, em, 1 - ep, ec)
+    sibling = (section, ex, em, ep, 1 - ec)
+
+    def peer(g):
+        return (section, g // 2, g % 2, ep, ec)
+
+    barrier = pltpu.get_barrier_semaphore()
+    for d in range(1, groups):
+        pl.semaphore_signal(barrier, inc=1, device_id=peer((me + d) % groups), device_id_type=MESH_IDS)
+    pl.semaphore_signal(barrier, inc=1, device_id=partner, device_id_type=MESH_IDS)
+    pl.semaphore_signal(barrier, inc=1, device_id=sibling, device_id_type=MESH_IDS)
+    pl.semaphore_wait(barrier, groups + 1)
+
+    def first_copy(s, g, target):
+        return pltpu.make_async_remote_copy(
+            src_ref=sends[s].at[g],
+            dst_ref=rows[s].at[ec, 0, me],
+            send_sem=first_send.at[s, g],
+            recv_sem=first_recv.at[s, me],
+            device_id=target,
+            device_id_type=MESH_IDS,
+        )
+
+    def arrived(s, g):
+        return pltpu.make_async_remote_copy(
+            src_ref=sends[s].at[g],
+            dst_ref=rows[s].at[ec, 0, g],
+            send_sem=first_send.at[s, g],
+            recv_sem=first_recv.at[s, g],
+            device_id=peer(g),
+            device_id_type=MESH_IDS,
+        )
+
+    def relay(s, q, g, target, recv, send, slot):
+        return pltpu.make_async_remote_copy(
+            src_ref=rows[s].at[ec, q, g],
+            dst_ref=rows[s].at[ec, slot, g],
+            send_sem=send.at[s, q, g],
+            recv_sem=recv.at[s, q, g],
+            device_id=target,
+            device_id_type=MESH_IDS,
+        )
+
+    local = []
+    for s in range(streams):
+        copy = pltpu.make_async_copy(sends[s].at[me], rows[s].at[ec, 0, me], first_recv.at[s, me])
+        copy.start()
+        local.append(copy)
+        for d in range(1, groups):
+            g = (me + d) % groups
+            first_copy(s, g, peer(g)).start()
+    outgoing = []
+    for s in range(streams):
+        local[s].wait()
+        for d in range(groups):
+            g = (me + groups - d) % groups
+            if d > 0:
+                arrived(s, g).wait_recv()
+            for target, recv, send, slot in (
+                (partner, pair_recv, pair_send, 1),
+                (sibling, near_recv, near_send, 0),
+            ):
+                copy = relay(s, 0, g, target, recv, send, slot)
+                copy.start()
+                outgoing.append(copy)
+    for s in range(streams):
+        for d in range(groups):
+            g = (me + groups - d) % groups
+            relay(s, 0, g, partner, pair_recv, pair_send, 1).wait_recv()
+            copy = relay(s, 1, g, sibling, near_recv, near_send, 1)
+            copy.start()
+            outgoing.append(copy)
+    for s in range(streams):
+        for q in range(2):
+            for g in range(groups):
+                pltpu.make_async_remote_copy(
+                    src_ref=rows[s].at[1 - ec, q, g],
+                    dst_ref=rows[s].at[1 - ec, q, g],
+                    send_sem=near_send.at[s, q, g],
+                    recv_sem=near_recv.at[s, q, g],
+                    device_id=sibling,
+                    device_id_type=MESH_IDS,
+                ).wait_recv()
+    for s in range(streams):
+        for d in range(1, groups):
+            g = (me + d) % groups
+            first_copy(s, g, peer(g)).wait_send()
+    for copy in outgoing:
+        copy.wait_send()
+
+
+def spread_to_holders(*sends):
+    groups, capacity, features = sends[0].shape
+    streams = len(sends)
+    rows = jax.ShapeDtypeStruct((2, 2, groups, capacity, features), sends[0].dtype)
+    any_spec = pl.BlockSpec(memory_space=pl.ANY)
+    return pl.pallas_call(
+        functools.partial(spread_kernel, groups),
+        out_shape=[rows] * streams,
+        in_specs=[any_spec] * streams,
+        out_specs=[any_spec] * streams,
+        scratch_shapes=[
+            pltpu.SemaphoreType.DMA((streams, groups)),
+            pltpu.SemaphoreType.DMA((streams, groups)),
+            pltpu.SemaphoreType.DMA((streams, 2, groups)),
+            pltpu.SemaphoreType.DMA((streams, 2, groups)),
+            pltpu.SemaphoreType.DMA((streams, 2, groups)),
+            pltpu.SemaphoreType.DMA((streams, 2, groups)),
+        ],
+        compiler_params=pltpu.CompilerParams(collective_id=0, has_side_effects=True),
+    )(*sends)
 
 
 def collect_from_holders(parts):
@@ -114,7 +236,6 @@
     forward_send = jnp.dot(forward_layout, forward_in, preferred_element_type=jnp.float32).astype(
         jnp.bfloat16
     )
-    forward_rows = spread_to_holders(forward_send.reshape(expert_count, capacity, feature_count))
 
     backward_dy = backward_in.astype(jnp.float32)
     along_dir = jnp.sum(backward_dy * unit_dir[None, :], axis=1)
@@ -125,7 +246,10 @@
     backward_send = jnp.dot(backward_layout, sent_rows, preferred_element_type=jnp.float32).astype(
         jnp.bfloat16
     )
-    backward_rows = spread_to_holders(backward_send.reshape(expert_count, capacity, feature_count))
+    forward_rows, backward_rows = spread_to_holders(
+        forward_send.reshape(expert_count, capacity, feature_count),
+        backward_send.reshape(expert_count, capacity, feature_count),
+    )
 
     flip = lax.axis_index("ep") == 1
 

time: 487 us -> 372 us (0.76)
  waiting for transfers between devices: 277 us -> 145 us
  Pallas kernels: 0 us -> 120 us
  blocking collectives: 110 us -> 9.33 us
  between operations: 15 us -> 1.7 us
  local copies, waits for them, and re-layouts: 3.94 us -> 10.6 us
    pallas_call x0 -> x1, Pallas kernels: none -> 120 us  [spread_to_holders(): pl.pallas_call(functools.partial(spread_kernel, groups), out_shape=[rows]...]
    all_to_all x2 -> x0, blocking collectives: 92.6 us -> none  [spread_to_holders(): own = lax.all_to_all(send, GROUP, split_axis=0, concat_axis=0, tiled=True)]
    ppermute x4 -> x2, waiting for transfers between devices: 123 us -> 62.8 us  [swap_pair(): return lax.ppermute(value, 'ep', [(0, 1), (1, 0)])]
    all_gather x2 -> x0, waiting for transfers between devices: 34 us -> none  [spread_to_holders(): return lax.all_gather(pair, 'ec', axis=0, tiled=False)]
    ppermute x2, waiting for transfers between devices: 73.5 us -> 50.1 us  [shifted(): return lax.ppermute(value, axis, pairs)]
    all_to_all x2, waiting for transfers between devices: 46.6 us -> 32.2 us  [collect_from_holders(): lax.all_to_all(summed, GROUP, split_axis=0, concat_axis=0, tiled=True)]
    all_to_all x2 -> x1, blocking collectives: 17.8 us -> 9.33 us  [collect_from_holders(): lax.all_to_all(parts, 'ec', split_axis=0, concat_axis=0, tiled=True)]
    all_to_all x0 -> x1, starting transfers between devices: none -> 6.15 us  [collect_from_holders(): lax.all_to_all(parts, 'ec', split_axis=0, concat_axis=0, tiled=True)]
  transfers between devices with their start and end apart: 10 -> 7, of which waited for: 10 -> 4; matrix products, arithmetic and copies ran while one was open for 2% -> 7% of each run, Pallas kernels for 0% -> 0%
where the time goes in v3:
time: 372 us; the launch traced here: 367 us
  waiting for transfers between devices  145 us (39%)
  Pallas kernels  120 us (32%)
  matrix products  33.1 us (9%)
  starting transfers between devices  26.6 us (7%)
  other arithmetic  20.5 us (6%)
  local copies, waits for them, and re-layouts  10.6 us (3%)
  blocking collectives  9.33 us (3%)
    pallas_call x1, Pallas kernels, spread_to_holders(): pl.pallas_call(functools.partial(spread_kernel, groups), out_shape=[rows]...  120 us
    ppermute x2, waiting for transfers between devices, swap_pair(): return lax.ppermute(value, 'ep', [(0, 1), (1, 0)])  62.8 us
    ppermute x2, waiting for transfers between devices, shifted(): return lax.ppermute(value, axis, pairs)  50.1 us
    all_to_all x2, waiting for transfers between devices, collect_from_holders(): lax.all_to_all(summed, GROUP, split_axis=0, concat_axis=0, tiled=True)  32.2 us
    dot_general x1, matrix products, expert_forward(): jnp.dot(hidden, down_rows, preferred_element_type=jnp.float32)  11.5 us
    ppermute x2, starting transfers between devices, shifted(): return lax.ppermute(value, axis, pairs)  11.3 us
    all_to_all x1, blocking collectives, collect_from_holders(): lax.all_to_all(parts, 'ec', split_axis=0, concat_axis=0, tiled=True)  9.33 us
  transfers between devices with their start and end apart: 7, of which 4 were waited for; matrix products, arithmetic and copies ran while one was open for 7% of the time, Pallas kernels for 0%

profile of v3, /device:TPU:24, one launch (start us, length us, event | category | flops | bytes accessed | tf_op | source)
XLA Modules:
  0.0 366.6 jit_solution(17801763406019372600)
XLA Ops:
  0.7 9.2 %collective-permute-start = (bf16[1,128,3584]{2,1,0:T(8,128)(2,1)}, bf16[1,128,3584]{2,1,0:T(8,128)(2,1)}, u32[]{:S(2)}, u32[]{:S(2)}) collective-permute-start(bf16[1,128,3584]{2,1,0:T(8,128)(2,1)} %param.15), channel_id=1, source_target_pairs={{0,32},{32,64},{64,96},{96,128},{128,160},{160,192},{192,224},{1,3... | collective-permute-start | bytes 2752520 | tf_op jit(solution)/shard_map/ppermute | solution.py:22
  9.9 2.1 collective-permute-start.1
  12.0 1.3 multiply_reduce_fusion.1
  19.3 50.1 %collective-permute-done.1 = bf16[1,128,3584]{2,1,0:T(8,128)(2,1)} collective-permute-done((bf16[1,128,3584]{2,1,0:T(8,128)(2,1)}, bf16[1,128,3584]{2,1,0:T(8,128)(2,1)}, u32[]{:S(2)}, u32[]{:S(2)}) %collective-permute-start.1) | collective-permute-done | bytes 917536 | tf_op jit(solution)/shard_map/ppermute | solution.py:22
  69.4 1.6 fusion.6
  71.0 1.8 convolution_convert_fusion.1
  72.8 2.8 convolution_convert_fusion.2
  75.6 119.6 %shard_map.157 = (bf16[2,2,8,24,3584]{4,3,2,1,0:T(8,128)(2,1)}, bf16[2,2,8,24,3584]{4,3,2,1,0:T(8,128)(2,1)}) custom-call(bf16[8,24,3584]{2,1,0:T(8,128)(2,1)} %bitcast.86, bf16[8,24,3584]{2,1,0:T(8,128)(2,1)} %bitcast.85), custom_call_target="tpu_custom_call" | custom-call | tf_op jit(solution)/shard_map/pallas_call | solution.py:176
  195.2 5.8 %fusion.9 = f32[768,256]{1,0:T(8,128)} fusion(bf16[768,3584]{1,0:T(8,128)(2,1)} %bitcast.103, bf16[1,256,3584]{2,1,0:T(8,128)(2,1)} %param.26), kind=kOutput, calls=%fused_computation.23 | convolution fusion | flops 1409286144 | bytes 8126464 | tf_op jit(solution)/shard_map/dot_general | solution.py:48
  201.0 2.5 fusion.17
  203.5 11.5 %convolution_convert_fusion = bf16[768,3584]{1,0:T(8,128)(2,1)} fusion(bf16[1,256,3584]{2,1,0:T(8,128)(2,1)} %param.26, bf16[768,3584]{1,0:T(8,128)(2,1)} %bitcast.101, bf16[1,3584,256]{2,1,0:T(8,128)(2,1)S(1)} %copy-done, f32[768,256]{1,0:T(8,128)} %fusion.17), kind=kOutput, calls=%fused_computation.1 | convolution fusion | flops 2822504448 | bytes 15466496 | tf_op jit(solution)/shard_map/dot_general | solution.py:42
  215.0 3.6 fusion.15
  218.6 1.9 add_convert_fusion
  220.5 9.3 %all_to_all.20 = bf16[2,2,8,24,3584]{4,3,2,1,0:T(8,128)(2,1)} all-to-all(bf16[2,2,8,24,3584]{4,3,2,1,0:T(8,128)(2,1)S(1)} %bitcast.81), channel_id=1, replica_groups=mesh['section'=8,'ex'=4,'em'=2,'ep'=2,'ec'=2] {'ec'}, dimensions={0} | all-to-all | bytes 11010048 | tf_op jit(solution)/shard_map/all_to_all | solution.py:194
  229.8 6.2 %all-to-all-start = ((bf16[2,2,8,24,3584]{4,3,2,1,0:T(8,128)(2,1)}), bf16[2,2,8,24,3584]{4,3,2,1,0:T(8,128)(2,1)}, u32[]{:S(2)}, u32[]{:S(2)}) async-start(bf16[2,2,8,24,3584]{4,3,2,1,0:T(8,128)(2,1)} %bitcast.83), calls=%async_computation | async-start | bytes 11010048 | tf_op jit(solution)/shard_map/all_to_all | solution.py:194
  236.0 3.4 convert_add_fusion
  239.4 2.5 copy-done.2
  241.9 1.2 fusion.20
  243.1 3.6 convert_add_fusion.1
  246.7 2.4 copy-done.4
  249.1 1.3 fusion.19
  250.4 2.0 collective-permute-start.2
  252.4 23.9 %collective-permute-done.3 = bf16[8,24,3584]{2,1,0:T(8,128)(2,1)S(1)} collective-permute-done((bf16[8,24,3584]{2,1,0:T(8,128)(2,1)}, bf16[8,24,3584]{2,1,0:T(8,128)(2,1)S(1)}, u32[]{:S(2)}, u32[]{:S(2)}) %collective-permute-start.3) | collective-permute-done | bytes 1376288 | tf_op jit(solution)/shard_map/ppermute | solution.py:66
  276.3 1.4 fusion.3
  277.8 3.6 all-to-all-start.3
  281.3 38.9 %collective-permute-done.2 = bf16[8,24,3584]{2,1,0:T(8,128)(2,1)} collective-permute-done((bf16[8,24,3584]{2,1,0:T(8,128)(2,1)}, bf16[8,24,3584]{2,1,0:T(8,128)(2,1)}, u32[]{:S(2)}, u32[]{:S(2)}) %collective-permute-start.2) | collective-permute-done | bytes 1376288 | tf_op jit(solution)/shard_map/ppermute | solution.py:66
  320.3 3.5 fusion.5
  323.8 1.1 copy-done.5
  324.8 3.6 all-to-all-start.1
  328.5 2.7 fusion.1
  331.2 32.2 %all-to-all-done.1 = bf16[8,24,3584]{2,1,0:T(8,128)(2,1)S(1)} async-done(((bf16[8,24,3584]{2,1,0:T(8,128)(2,1)}), bf16[8,24,3584]{2,1,0:T(8,128)(2,1)S(1)}, u32[]{:S(2)}, u32[]{:S(2)}) %all-to-all-start.1) | async-done | bytes 1376288 | tf_op jit(solution)/shard_map/all_to_all | solution.py:198
  364.0 2.7 fusion.29
  (56 shorter events, 5.7 us)
Async XLA Ops:
  0.6 202.8 %copy-start = (bf16[1,3584,256]{2,1,0:T(8,128)(2,1)S(1)}, bf16[1,3584,256]{2,1,0:T(8,128)(2,1)}, u32[]{:S(2)}) copy-start(bf16[1,3584,256]{2,1,0:T(8,128)(2,1)} %param.25) | copy-start | bytes 5505028
  0.6 18.4 %copy-start.10 = (f32[1,3584]{1,0:T(1,128)S(1)}, f32[1,3584]{1,0:T(1,128)}, u32[]{:S(2)}) copy-start(f32[1,3584]{1,0:T(1,128)} %param.27) | copy-start | bytes 43012
  0.7 18.3 %copy-start.11 = (s32[1,128,1]{1,2,0:T(1,128)S(1)}, s32[1,128,1]{1,2,0:T(1,128)}, u32[]{:S(2)}) copy-start(s32[1,128,1]{1,2,0:T(1,128)} %param.16) | copy-start | bytes 1540
  0.7 18.1 %copy-start.12 = (s32[1,128,1]{1,2,0:T(1,128)S(1)}, s32[1,128,1]{1,2,0:T(1,128)}, u32[]{:S(2)}) copy-start(s32[1,128,1]{1,2,0:T(1,128)} %param.20) | copy-start | bytes 1540
  0.7 72.1 %collective-permute-start = (bf16[1,128,3584]{2,1,0:T(8,128)(2,1)}, bf16[1,128,3584]{2,1,0:T(8,128)(2,1)}, u32[]{:S(2)}, u32[]{:S(2)}) collective-permute-start(bf16[1,128,3584]{2,1,0:T(8,128)(2,1)} %param.15), channel_id=1, source_target_pairs={{0,32},{32,64},{64,96},{96,128},{128,160},{160,192},{192,224},{1,3... | collective-permute-start | bytes 2752520 | tf_op jit(solution)/shard_map/ppermute | solution.py:22
  9.9 59.5 %collective-permute-start.1 = (bf16[1,128,3584]{2,1,0:T(8,128)(2,1)}, bf16[1,128,3584]{2,1,0:T(8,128)(2,1)}, u32[]{:S(2)}, u32[]{:S(2)}) collective-permute-start(bf16[1,128,3584]{2,1,0:T(8,128)(2,1)} %param.19), channel_id=1, source_target_pairs={{32,0},{64,32},{96,64},{128,96},{160,128},{192,160},{224,192},{33,... | collective-permute-start | bytes 2752520 | tf_op jit(solution)/shard_map/ppermute | solution.py:22
  19.0 53.8 %copy-start.13 = (s32[128]{0:T(128)}, s32[128]{0:T(128)S(1)}, u32[]{:S(2)}) copy-start(s32[128]{0:T(128)S(1)} %multiply_add_fusion.1) | copy-start | bytes 1540
  19.1 52.0 %copy-start.16 = (s32[128]{0:T(128)}, s32[128]{0:T(128)S(1)}, u32[]{:S(2)}) copy-start(s32[128]{0:T(128)S(1)} %multiply_add_fusion) | copy-start | bytes 1540
  19.1 51.9 %copy-start.18 = (f32[1,128]{1,0:T(1,128)S(1)}, f32[1,128]{1,0:T(1,128)}, u32[]{:S(2)}) copy-start(f32[1,128]{1,0:T(1,128)} %param.21) | copy-start | bytes 1540
  71.0 1.8 copy-start.6
  195.2 5.8 %copy-start.9 = (bf16[1,3584,256]{2,1,0:T(8,128)(2,1)S(1)}, bf16[1,3584,256]{2,1,0:T(8,128)(2,1)}, u32[]{:S(2)}) copy-start(bf16[1,3584,256]{2,1,0:T(8,128)(2,1)} %param.24) | copy-start | bytes 5505028
  195.2 5.8 %copy-start.20 = (bf16[2,2,8,24,3584]{4,3,2,1,0:T(8,128)(2,1)S(1)}, bf16[2,2,8,24,3584]{4,3,2,1,0:T(8,128)(2,1)}, u32[]{:S(2)}) copy-start(bf16[2,2,8,24,3584]{4,3,2,1,0:T(8,128)(2,1)} %get-tuple-element.5) | copy-start | bytes 16515076
  215.0 3.6 copy-start.8
  229.8 13.3 %all-to-all-start = ((bf16[2,2,8,24,3584]{4,3,2,1,0:T(8,128)(2,1)}), bf16[2,2,8,24,3584]{4,3,2,1,0:T(8,128)(2,1)}, u32[]{:S(2)}, u32[]{:S(2)}) async-start(bf16[2,2,8,24,3584]{4,3,2,1,0:T(8,128)(2,1)} %bitcast.83), calls=%async_computation | async-start | bytes 11010048 | tf_op jit(solution)/shard_map/all_to_all | solution.py:194
  239.4 2.5 copy-start.2
  243.1 33.2 %collective-permute-start.3 = (bf16[8,24,3584]{2,1,0:T(8,128)(2,1)}, bf16[8,24,3584]{2,1,0:T(8,128)(2,1)S(1)}, u32[]{:S(2)}, u32[]{:S(2)}) collective-permute-start(bf16[8,24,3584]{2,1,0:T(8,128)(2,1)} %fusion.20), channel_id=1, source_target_pairs={{0,2},{2,0},{1,3},{3,1},{4,6},{6,4},{5,7},{7,5},{8,10},{10,8},{9,1... | collective-permute-start | bytes 4128776 | tf_op jit(solution)/shard_map/ppermute | solution.py:66
  243.1 33.2 %copy-start.3 = (f32[1,2,8,24,3584]{4,3,2,1,0:T(8,128)S(1)}, f32[1,2,8,24,3584]{4,3,2,1,0:T(8,128)}, u32[]{:S(2)}) copy-start(f32[1,2,8,24,3584]{4,3,2,1,0:T(8,128)} %copy-done.2) | copy-start | bytes 16515076
  246.7 2.4 copy-start.4
  250.4 69.8 %collective-permute-start.2 = (bf16[8,24,3584]{2,1,0:T(8,128)(2,1)}, bf16[8,24,3584]{2,1,0:T(8,128)(2,1)}, u32[]{:S(2)}, u32[]{:S(2)}) collective-permute-start(bf16[8,24,3584]{2,1,0:T(8,128)(2,1)} %fusion.19), channel_id=1, source_target_pairs={{0,2},{2,0},{1,3},{3,1},{4,6},{6,4},{5,7},{7,5},{8,10},{10,8},{9,1... | collective-permute-start | bytes 4128776 | tf_op jit(solution)/shard_map/ppermute | solution.py:66
  277.8 46.0 %all-to-all-start.3 = ((bf16[8,24,3584]{2,1,0:T(8,128)(2,1)}), bf16[8,24,3584]{2,1,0:T(8,128)(2,1)S(1)}, u32[]{:S(2)}, u32[]{:S(2)}) async-start(bf16[8,24,3584]{2,1,0:T(8,128)(2,1)} %fusion.3), calls=%async_computation.3 | async-start | bytes 2752512 | tf_op jit(solution)/shard_map/all_to_all | solution.py:198
  323.7 4.7 %copy-start.17 = (s32[128]{0:T(128)S(1)}, s32[128]{0:T(128)}, u32[]{:S(2)}) copy-start(s32[128]{0:T(128)} %copy-done.16) | copy-start | bytes 1540
  323.8 1.1 copy-start.5
  324.8 38.5 %all-to-all-start.1 = ((bf16[8,24,3584]{2,1,0:T(8,128)(2,1)}), bf16[8,24,3584]{2,1,0:T(8,128)(2,1)S(1)}, u32[]{:S(2)}, u32[]{:S(2)}) async-start(bf16[8,24,3584]{2,1,0:T(8,128)(2,1)} %fusion.5), calls=%async_computation.1 | async-start | bytes 2752512 | tf_op jit(solution)/shard_map/all_to_all | solution.py:198
  328.4 34.9 %copy-start.14 = (s32[128]{0:T(128)S(1)}, s32[128]{0:T(128)}, u32[]{:S(2)}) copy-start(s32[128]{0:T(128)} %copy-done.13) | copy-start | bytes 1540
  328.4 34.9 %copy-start.19 = (f32[1,128]{1,0:T(1,128)S(1)}, f32[1,128]{1,0:T(1,128)}, u32[]{:S(2)}) copy-start(f32[1,128]{1,0:T(1,128)} %param.17) | copy-start | bytes 1540
  331.2 32.8 %copy-start.7 = (bf16[128,3584]{1,0:T(8,128)(2,1)S(1)}, bf16[128,3584]{1,0:T(8,128)(2,1)}, u32[]{:S(2)}) copy-start(bf16[128,3584]{1,0:T(8,128)(2,1)} %param.14) | copy-start | bytes 2752516
  363.9 2.7 copy-start.15
  363.9 2.7 copy-start.1

commit v4 on v3

--- a/solution.py
+++ b/solution.py
@@ -190,12 +190,108 @@
     )(*sends)
 
 
-def collect_from_holders(parts):
-    swapped = lax.all_to_all(parts, "ec", split_axis=0, concat_axis=0, tiled=True)
-    pair = swapped[0].astype(jnp.float32) + swapped[1].astype(jnp.float32)
-    arrived = swap_pair(pair[1].astype(jnp.bfloat16))
-    summed = (pair[0] + arrived.astype(jnp.float32)).astype(jnp.bfloat16)
-    return lax.all_to_all(summed, GROUP, split_axis=0, concat_axis=0, tiled=True)
+def collect_kernel(groups, mine, other, back, landed, summed, swap_recv, swap_send, back_recv, back_send):
+    streams = mine.shape[0]
+    section = lax.axis_index("section")
+    ex = lax.axis_index("ex")
+    em = lax.axis_index("em")
+    ep = lax.axis_index("ep")
+    ec = lax.axis_index("ec")
+    me = ex * 2 + em
+    partner = (section, ex, em, 1 - ep, ec)
+
+    def peer(g):
+        return (section, g // 2, g % 2, ep, ec)
+
+    barrier = pltpu.get_barrier_semaphore()
+    for d in range(1, groups):
+        pl.semaphore_signal(barrier, inc=1, device_id=peer((me + d) % groups), device_id_type=MESH_IDS)
+    pl.semaphore_signal(barrier, inc=1, device_id=partner, device_id_type=MESH_IDS)
+    pl.semaphore_wait(barrier, groups)
+
+    def swap(s, g):
+        return pltpu.make_async_remote_copy(
+            src_ref=other.at[s, g],
+            dst_ref=landed.at[s, g],
+            send_sem=swap_send.at[s, g],
+            recv_sem=swap_recv.at[s, g],
+            device_id=partner,
+            device_id_type=MESH_IDS,
+        )
+
+    def reply(s, g):
+        return pltpu.make_async_remote_copy(
+            src_ref=summed.at[s, g],
+            dst_ref=back.at[s, me],
+            send_sem=back_send.at[s, g],
+            recv_sem=back_recv.at[s, me],
+            device_id=peer(g),
+            device_id_type=MESH_IDS,
+        )
+
+    def incoming(s, g):
+        return pltpu.make_async_remote_copy(
+            src_ref=summed.at[s, g],
+            dst_ref=back.at[s, g],
+            send_sem=back_send.at[s, g],
+            recv_sem=back_recv.at[s, g],
+            device_id=peer(g),
+            device_id_type=MESH_IDS,
+        )
+
+    for s in range(streams):
+        for d in range(1, groups + 1):
+            swap(s, (me + d) % groups).start()
+    local = []
+    for s in range(streams):
+        for d in range(1, groups + 1):
+            g = (me + d) % groups
+            swap(s, g).wait_recv()
+            summed[s, g] = (mine[s, g] + landed[s, g].astype(jnp.float32)).astype(summed.dtype)
+            if d < groups:
+                reply(s, g).start()
+            else:
+                copy = pltpu.make_async_copy(summed.at[s, g], back.at[s, me], back_recv.at[s, me])
+                copy.start()
+                local.append(copy)
+    for s in range(streams):
+        local[s].wait()
+        for d in range(1, groups):
+            incoming(s, (me + d) % groups).wait_recv()
+    for s in range(streams):
+        for d in range(1, groups + 1):
+            swap(s, (me + d) % groups).wait_send()
+        for d in range(1, groups):
+            reply(s, (me + d) % groups).wait_send()
+
+
+def collect_from_holders(*parts):
+    mine, other = [], []
+    for part in parts:
+        swapped = lax.all_to_all(part, "ec", split_axis=0, concat_axis=0, tiled=True)
+        pair = swapped[0].astype(jnp.float32) + swapped[1].astype(jnp.float32)
+        mine.append(pair[0])
+        other.append(pair[1].astype(jnp.bfloat16))
+    mine = jnp.stack(mine)
+    other = jnp.stack(other)
+    streams, groups = mine.shape[:2]
+    any_spec = pl.BlockSpec(memory_space=pl.ANY)
+    back = pl.pallas_call(
+        functools.partial(collect_kernel, groups),
+        out_shape=jax.ShapeDtypeStruct(other.shape, jnp.bfloat16),
+        in_specs=[pl.BlockSpec(memory_space=pltpu.VMEM), any_spec],
+        out_specs=any_spec,
+        scratch_shapes=[
+            pltpu.VMEM(other.shape, jnp.bfloat16),
+            pltpu.VMEM(other.shape, jnp.bfloat16),
+            pltpu.SemaphoreType.DMA((streams, groups)),
+            pltpu.SemaphoreType.DMA((streams, groups)),
+            pltpu.SemaphoreType.DMA((streams, groups)),
+            pltpu.SemaphoreType.DMA((streams, groups)),
+        ],
+        compiler_params=pltpu.CompilerParams(collective_id=1, has_side_effects=True),
+    )(mine, other)
+    return [back[s] for s in range(streams)]
 
 
 def body(
@@ -259,15 +355,15 @@
         return grouped.reshape(device_count * capacity, local_hidden)
 
     forward_part = expert_forward(forward_rows.reshape(rows_shape), weights)
-    forward_back = collect_from_holders(
-        forward_part.reshape(2, 2, group_count, capacity, feature_count)
-    ).reshape(expert_count * capacity, feature_count)
     backward_part = expert_backward(
         backward_rows.reshape(rows_shape), reorder(saved_gate), reorder(saved_up), weights
     )
-    backward_back = collect_from_holders(
-        backward_part.reshape(2, 2, group_count, capacity, feature_count)
-    ).reshape(expert_count * capacity, feature_count)
+    forward_back, backward_back = collect_from_holders(
+        forward_part.reshape(2, 2, group_count, capacity, feature_count),
+        backward_part.reshape(2, 2, group_count, capacity, feature_count),
+    )
+    forward_back = forward_back.reshape(expert_count * capacity, feature_count)
+    backward_back = backward_back.reshape(expert_count * capacity, feature_count)
 
     contract = (((0,), (0,)), ((), ()))
     picked = lax.dot_general(forward_layout, forward_back, contract, preferred_element_type=jnp.float32)

time: 372 us -> 355 us (0.954)
  Pallas kernels: 120 us -> 217 us
  waiting for transfers between devices: 145 us -> 50.1 us
  starting transfers between devices: 26.6 us -> 11.3 us
  blocking collectives: 9.33 us -> 18.2 us
  other arithmetic: 20.5 us -> 14.7 us
  matrix products: 33.1 us -> 28.7 us
    pallas_call x0 -> x1, Pallas kernels: none -> 97.4 us  [collect_from_holders(): pl.pallas_call(functools.partial(collect_kernel, groups), out_shape=jax.S...]
    ppermute x2 -> x0, waiting for transfers between devices: 62.8 us -> none  [swap_pair(): return lax.ppermute(value, 'ep', [(0, 1), (1, 0)])]
    all_to_all x3 -> x0, waiting for transfers between devices: 32.2 us -> none  [the longest x2 32.2 us: collect_from_holders(): lax.all_to_all(summed, GROUP, split_axis=0, concat_axis=0, tiled=True)]
    all_to_all x3 -> x0, starting transfers between devices: 13.3 us -> none  [the longest x2 7.14 us: collect_from_holders(): lax.all_to_all(summed, GROUP, split_axis=0, concat_axis=0, tiled=True)]
    all_to_all x1 -> x2, blocking collectives: 9.33 us -> 18.2 us  [collect_from_holders(): lax.all_to_all(part, 'ec', split_axis=0, concat_axis=0, tiled=True)]
    add x2, other arithmetic: 6.97 us -> 1.61 us  [collect_from_holders(): pair = swapped[0].astype(jnp.float32) + swapped[1].astype(jnp.float32)]
    convert_element_type x2 -> x0, other arithmetic: 4.94 us -> none  [collect_from_holders(): summed = (pair[0] + arrived.astype(jnp.float32)).astype(jnp.bfloat16)]
    another operation x0 -> x2, other arithmetic: none -> 4.58 us  [the longest x1 2.81 us: collect_from_holders(): mine = jnp.stack(mine)]
  transfers between devices with their start and end apart: 7 -> 2, of which waited for: 4 -> 1; matrix products, arithmetic and copies ran while one was open for 7% -> 3% of each run, Pallas kernels for 0% -> 0%
where the time goes in v4:
time: 355 us; the launch traced here: 351 us
  Pallas kernels  217 us (61%)
  waiting for transfers between devices  50.1 us (14%)
  matrix products  28.7 us (8%)
  blocking collectives  18.2 us (5%)
  other arithmetic  14.7 us (4%)
  starting transfers between devices  11.3 us (3%)
  local copies, waits for them, and re-layouts  9.16 us (3%)
    pallas_call x1, Pallas kernels, spread_to_holders(): pl.pallas_call(functools.partial(spread_kernel, groups), out_shape=[rows]...  120 us
    pallas_call x1, Pallas kernels, collect_from_holders(): pl.pallas_call(functools.partial(collect_kernel, groups), out_shape=jax.S...  97.4 us
    ppermute x2, waiting for transfers between devices, shifted(): return lax.ppermute(value, axis, pairs)  50.1 us
    all_to_all x2, blocking collectives, collect_from_holders(): lax.all_to_all(part, 'ec', split_axis=0, concat_axis=0, tiled=True)  18.2 us
    dot_general x1, matrix products, expert_forward(): jnp.dot(hidden, down_rows, preferred_element_type=jnp.float32)  11.5 us
    ppermute x2, starting transfers between devices, shifted(): return lax.ppermute(value, axis, pairs)  11.3 us
  transfers between devices with their start and end apart: 2, of which 1 were waited for; matrix products, arithmetic and copies ran while one was open for 3% of the time, Pallas kernels for 0%

profile of v4, /device:TPU:24, one launch (start us, length us, event | category | flops | bytes accessed | tf_op | source)
XLA Modules:
  0.0 350.8 jit_solution(5995743898641255934)
XLA Ops:
  0.7 9.2 %collective-permute-start = (bf16[1,128,3584]{2,1,0:T(8,128)(2,1)}, bf16[1,128,3584]{2,1,0:T(8,128)(2,1)}, u32[]{:S(2)}, u32[]{:S(2)}) collective-permute-start(bf16[1,128,3584]{2,1,0:T(8,128)(2,1)} %param.15), channel_id=1, source_target_pairs={{0,32},{32,64},{64,96},{96,128},{128,160},{160,192},{192,224},{1,3... | collective-permute-start | bytes 2752520 | tf_op jit(solution)/shard_map/ppermute | solution.py:22
  9.9 2.1 collective-permute-start.1
  12.0 1.3 multiply_reduce_fusion.1
  14.1 0.7 fusion.50
  15.0 0.8 select_reduce_fusion.1
  15.8 0.7 fusion.49
  16.8 1.0 copy.21
  17.8 1.0 copy.22
  19.3 50.1 %collective-permute-done.1 = bf16[1,128,3584]{2,1,0:T(8,128)(2,1)} collective-permute-done((bf16[1,128,3584]{2,1,0:T(8,128)(2,1)}, bf16[1,128,3584]{2,1,0:T(8,128)(2,1)}, u32[]{:S(2)}, u32[]{:S(2)}) %collective-permute-start.1) | collective-permute-done | bytes 917536 | tf_op jit(solution)/shard_map/ppermute | solution.py:22
  69.4 1.6 fusion.2
  71.0 1.8 convolution_convert_fusion.1
  72.8 2.8 convolution_convert_fusion.2
  75.6 119.6 %shard_map.157 = (bf16[2,2,8,24,3584]{4,3,2,1,0:T(8,128)(2,1)}, bf16[2,2,8,24,3584]{4,3,2,1,0:T(8,128)(2,1)}) custom-call(bf16[8,24,3584]{2,1,0:T(8,128)(2,1)} %bitcast.78, bf16[8,24,3584]{2,1,0:T(8,128)(2,1)} %bitcast.76), custom_call_target="tpu_custom_call" | custom-call | tf_op jit(solution)/shard_map/pallas_call | solution.py:176
  195.2 5.6 %fusion.13 = f32[768,256]{1,0:T(8,128)} fusion(bf16[768,3584]{1,0:T(8,128)(2,1)} %bitcast.96, bf16[1,3584,256]{2,1,0:T(8,128)(2,1)} %param.24), kind=kOutput, calls=%fused_computation.29 | convolution fusion | flops 1409286144 | bytes 8126464 | tf_op jit(solution)/shard_map/dot_general | solution.py:39
  200.8 11.5 %convolution_convert_fusion = bf16[768,3584]{1,0:T(8,128)(2,1)} fusion(bf16[1,256,3584]{2,1,0:T(8,128)(2,1)} %param.26, bf16[768,3584]{1,0:T(8,128)(2,1)} %bitcast.97, bf16[1,3584,256]{2,1,0:T(8,128)(2,1)S(1)} %copy-done, f32[768,256]{1,0:T(8,128)} %fusion.13), kind=kOutput, calls=%fused_computation.1 | convolution fusion | flops 2822504448 | bytes 15466496 | tf_op jit(solution)/shard_map/dot_general | solution.py:42
  212.3 10.0 %all_to_all.10 = bf16[2,2,8,24,3584]{4,3,2,1,0:T(8,128)(2,1)S(1)} all-to-all(bf16[2,2,8,24,3584]{4,3,2,1,0:T(8,128)(2,1)} %bitcast.75), channel_id=1, replica_groups=mesh['section'=8,'ex'=4,'em'=2,'ep'=2,'ec'=2] {'ec'}, dimensions={0} | all-to-all | bytes 11010048 | tf_op jit(solution)/shard_map/all_to_all | solution.py:271
  222.3 0.8 convert_add_fusion.1
  223.3 1.7 slice_bitcast_fusion.1
  225.0 0.7 copy-done.16
  225.7 1.6 fusion.5
  227.4 1.8 fusion.11
  229.1 1.7 add_convert_fusion
  230.8 8.2 %all_to_all.11 = bf16[2,2,8,24,3584]{4,3,2,1,0:T(8,128)(2,1)S(1)} all-to-all(bf16[2,2,8,24,3584]{4,3,2,1,0:T(8,128)(2,1)S(1)} %bitcast.73), channel_id=1, replica_groups=mesh['section'=8,'ex'=4,'em'=2,'ep'=2,'ec'=2] {'ec'}, dimensions={0} | all-to-all | bytes 11010048 | tf_op jit(solution)/shard_map/all_to_all | solution.py:271
  239.0 0.8 convert_add_fusion
  240.2 1.6 copy-done.2
  241.7 2.8 pad_maximum_fusion.mine
  244.6 1.8 pad_maximum_fusion.1.other
  246.3 97.4 %shard_map.158 = bf16[2,8,24,3584]{3,2,1,0:T(8,128)(2,1)} custom-call(f32[2,8,24,3584]{3,2,1,0:T(8,128)} %pad_maximum_fusion.mine, bf16[2,8,24,3584]{3,2,1,0:T(8,128)(2,1)} %pad_maximum_fusion.1.other), custom_call_target="tpu_custom_call" | custom-call | tf_op jit(solution)/shard_map/pallas_call | solution.py:279
  343.7 1.9 fusion.58
  345.7 1.4 fusion.1
  347.6 0.6 copy-done.4
  348.2 2.6 fusion.25
  (48 shorter events, 1.8 us)
Async XLA Ops:
  0.6 200.2 %copy-start = (bf16[1,3584,256]{2,1,0:T(8,128)(2,1)S(1)}, bf16[1,3584,256]{2,1,0:T(8,128)(2,1)}, u32[]{:S(2)}) copy-start(bf16[1,3584,256]{2,1,0:T(8,128)(2,1)} %param.25) | copy-start | bytes 5505028
  0.6 18.4 %copy-start.6 = (f32[1,3584]{1,0:T(1,128)S(1)}, f32[1,3584]{1,0:T(1,128)}, u32[]{:S(2)}) copy-start(f32[1,3584]{1,0:T(1,128)} %param.27) | copy-start | bytes 43012
  0.7 18.3 %copy-start.7 = (s32[1,128,1]{1,2,0:T(1,128)S(1)}, s32[1,128,1]{1,2,0:T(1,128)}, u32[]{:S(2)}) copy-start(s32[1,128,1]{1,2,0:T(1,128)} %param.16) | copy-start | bytes 1540
  0.7 18.1 %copy-start.8 = (s32[1,128,1]{1,2,0:T(1,128)S(1)}, s32[1,128,1]{1,2,0:T(1,128)}, u32[]{:S(2)}) copy-start(s32[1,128,1]{1,2,0:T(1,128)} %param.20) | copy-start | bytes 1540
  0.7 72.1 %collective-permute-start = (bf16[1,128,3584]{2,1,0:T(8,128)(2,1)}, bf16[1,128,3584]{2,1,0:T(8,128)(2,1)}, u32[]{:S(2)}, u32[]{:S(2)}) collective-permute-start(bf16[1,128,3584]{2,1,0:T(8,128)(2,1)} %param.15), channel_id=1, source_target_pairs={{0,32},{32,64},{64,96},{96,128},{128,160},{160,192},{192,224},{1,3... | collective-permute-start | bytes 2752520 | tf_op jit(solution)/shard_map/ppermute | solution.py:22
  9.9 59.5 %collective-permute-start.1 = (bf16[1,128,3584]{2,1,0:T(8,128)(2,1)}, bf16[1,128,3584]{2,1,0:T(8,128)(2,1)}, u32[]{:S(2)}, u32[]{:S(2)}) collective-permute-start(bf16[1,128,3584]{2,1,0:T(8,128)(2,1)} %param.19), channel_id=1, source_target_pairs={{32,0},{64,32},{96,64},{128,96},{160,128},{192,160},{224,192},{33,... | collective-permute-start | bytes 2752520 | tf_op jit(solution)/shard_map/ppermute | solution.py:22
  19.0 53.8 %copy-start.9 = (s32[128]{0:T(128)}, s32[128]{0:T(128)S(1)}, u32[]{:S(2)}) copy-start(s32[128]{0:T(128)S(1)} %multiply_add_fusion.1) | copy-start | bytes 1540
  19.1 52.0 %copy-start.12 = (s32[128]{0:T(128)}, s32[128]{0:T(128)S(1)}, u32[]{:S(2)}) copy-start(s32[128]{0:T(128)S(1)} %multiply_add_fusion) | copy-start | bytes 1540
  19.1 51.9 %copy-start.14 = (f32[1,128]{1,0:T(1,128)S(1)}, f32[1,128]{1,0:T(1,128)}, u32[]{:S(2)}) copy-start(f32[1,128]{1,0:T(1,128)} %param.21) | copy-start | bytes 1540
  71.0 1.8 copy-start.3
  212.3 12.7 %slice-start = ((s8[5505024]{0:T(1024)(128)(4,1)}), s8[4194304]{0:T(1024)(128)(4,1)S(1)}, s32[]{:S(2)}) async-start(s8[5505024]{0:T(1024)(128)(4,1)} %bitcast.93), calls=%async_computation.2 | async-start | bytes 8388608
  222.3 2.7 slice-start.1
  223.3 2.4 copy-start.16
  225.7 1.6 copy-start.5
  240.0 1.8 copy-start.2
  343.7 2.0 copy-start.13
  345.6 1.4 copy-start.10
  345.7 1.4 copy-start.15
  347.1 1.2 copy-start.4
  347.6 3.2 copy-start.11
  347.6 3.2 copy-start.1

commit v5 on v4

--- a/solution.py
+++ b/solution.py
@@ -125,16 +125,18 @@
         copy = pltpu.make_async_copy(sends[s].at[me], rows[s].at[ec, 0, me], first_recv.at[s, me])
         copy.start()
         local.append(copy)
-        for d in range(1, groups):
+    for d in range(1, groups):
+        for s in range(streams):
             g = (me + d) % groups
             first_copy(s, g, peer(g)).start()
     outgoing = []
-    for s in range(streams):
-        local[s].wait()
-        for d in range(groups):
+    for d in range(groups):
+        for s in range(streams):
             g = (me + groups - d) % groups
             if d > 0:
                 arrived(s, g).wait_recv()
+            else:
+                local[s].wait()
             for target, recv, send, slot in (
                 (partner, pair_recv, pair_send, 1),
                 (sibling, near_recv, near_send, 0),
@@ -142,8 +144,8 @@
                 copy = relay(s, 0, g, target, recv, send, slot)
                 copy.start()
                 outgoing.append(copy)
-    for s in range(streams):
-        for d in range(groups):
+    for d in range(groups):
+        for s in range(streams):
             g = (me + groups - d) % groups
             relay(s, 0, g, partner, pair_recv, pair_send, 1).wait_recv()
             copy = relay(s, 1, g, sibling, near_recv, near_send, 1)
@@ -239,12 +241,12 @@
             device_id_type=MESH_IDS,
         )
 
-    for s in range(streams):
-        for d in range(1, groups + 1):
+    for d in range(1, groups + 1):
+        for s in range(streams):
             swap(s, (me + d) % groups).start()
     local = []
-    for s in range(streams):
-        for d in range(1, groups + 1):
+    for d in range(1, groups + 1):
+        for s in range(streams):
             g = (me + d) % groups
             swap(s, g).wait_recv()
             summed[s, g] = (mine[s, g] + landed[s, g].astype(jnp.float32)).astype(summed.dtype)

time: 355 us -> 357 us (level)
  no operation moved by 1% of the time
where the time goes in v5:
time: 357 us; the launch traced here: 352 us
  Pallas kernels  218 us (61%)
  waiting for transfers between devices  50.1 us (14%)
  matrix products  28.7 us (8%)
  blocking collectives  18.2 us (5%)
  other arithmetic  14.7 us (4%)
  starting transfers between devices  11.3 us (3%)
  local copies, waits for them, and re-layouts  9.16 us (3%)
    pallas_call x1, Pallas kernels, spread_to_holders(): pl.pallas_call(functools.partial(spread_kernel, groups), out_shape=[rows]...  121 us
    pallas_call x1, Pallas kernels, collect_from_holders(): pl.pallas_call(functools.partial(collect_kernel, groups), out_shape=jax.S...  97.4 us
    ppermute x2, waiting for transfers between devices, shifted(): return lax.ppermute(value, axis, pairs)  50.1 us
    all_to_all x2, blocking collectives, collect_from_holders(): lax.all_to_all(part, 'ec', split_axis=0, concat_axis=0, tiled=True)  18.2 us
    dot_general x1, matrix products, expert_forward(): jnp.dot(hidden, down_rows, preferred_element_type=jnp.float32)  11.5 us
    ppermute x2, starting transfers between devices, shifted(): return lax.ppermute(value, axis, pairs)  11.3 us
  transfers between devices with their start and end apart: 2, of which 1 were waited for; matrix products, arithmetic and copies ran while one was open for 3% of the time, Pallas kernels for 0%

profile of v5, /device:TPU:24, one launch (start us, length us, event | category | flops | bytes accessed | tf_op | source)
XLA Modules:
  0.0 352.3 jit_solution(9402977907085221047)
XLA Ops:
  0.7 9.2 %collective-permute-start = (bf16[1,128,3584]{2,1,0:T(8,128)(2,1)}, bf16[1,128,3584]{2,1,0:T(8,128)(2,1)}, u32[]{:S(2)}, u32[]{:S(2)}) collective-permute-start(bf16[1,128,3584]{2,1,0:T(8,128)(2,1)} %param.15), channel_id=1, source_target_pairs={{0,32},{32,64},{64,96},{96,128},{128,160},{160,192},{192,224},{1,3... | collective-permute-start | bytes 2752520 | tf_op jit(solution)/shard_map/ppermute | solution.py:22
  9.9 2.1 collective-permute-start.1
  12.0 1.3 multiply_reduce_fusion.1
  14.1 0.7 fusion.50
  15.0 0.8 select_reduce_fusion.1
  15.8 0.7 fusion.49
  16.8 1.0 copy.21
  17.8 1.0 copy.22
  19.3 50.1 %collective-permute-done.1 = bf16[1,128,3584]{2,1,0:T(8,128)(2,1)} collective-permute-done((bf16[1,128,3584]{2,1,0:T(8,128)(2,1)}, bf16[1,128,3584]{2,1,0:T(8,128)(2,1)}, u32[]{:S(2)}, u32[]{:S(2)}) %collective-permute-start.1) | collective-permute-done | bytes 917536 | tf_op jit(solution)/shard_map/ppermute | solution.py:22
  69.4 1.6 fusion.2
  71.0 1.8 convolution_convert_fusion.1
  72.8 2.8 convolution_convert_fusion.2
  75.6 121.1 %shard_map.157 = (bf16[2,2,8,24,3584]{4,3,2,1,0:T(8,128)(2,1)}, bf16[2,2,8,24,3584]{4,3,2,1,0:T(8,128)(2,1)}) custom-call(bf16[8,24,3584]{2,1,0:T(8,128)(2,1)} %bitcast.78, bf16[8,24,3584]{2,1,0:T(8,128)(2,1)} %bitcast.76), custom_call_target="tpu_custom_call" | custom-call | tf_op jit(solution)/shard_map/pallas_call | solution.py:178
  196.8 5.6 %fusion.13 = f32[768,256]{1,0:T(8,128)} fusion(bf16[768,3584]{1,0:T(8,128)(2,1)} %bitcast.96, bf16[1,3584,256]{2,1,0:T(8,128)(2,1)} %param.24), kind=kOutput, calls=%fused_computation.29 | convolution fusion | flops 1409286144 | bytes 8126464 | tf_op jit(solution)/shard_map/dot_general | solution.py:39
  202.4 11.5 %convolution_convert_fusion = bf16[768,3584]{1,0:T(8,128)(2,1)} fusion(bf16[1,256,3584]{2,1,0:T(8,128)(2,1)} %param.26, bf16[768,3584]{1,0:T(8,128)(2,1)} %bitcast.97, bf16[1,3584,256]{2,1,0:T(8,128)(2,1)S(1)} %copy-done, f32[768,256]{1,0:T(8,128)} %fusion.13), kind=kOutput, calls=%fused_computation.1 | convolution fusion | flops 2822504448 | bytes 15466496 | tf_op jit(solution)/shard_map/dot_general | solution.py:42
  213.8 10.0 %all_to_all.10 = bf16[2,2,8,24,3584]{4,3,2,1,0:T(8,128)(2,1)S(1)} all-to-all(bf16[2,2,8,24,3584]{4,3,2,1,0:T(8,128)(2,1)} %bitcast.75), channel_id=1, replica_groups=mesh['section'=8,'ex'=4,'em'=2,'ep'=2,'ec'=2] {'ec'}, dimensions={0} | all-to-all | bytes 11010048 | tf_op jit(solution)/shard_map/all_to_all | solution.py:273
  223.9 0.8 convert_add_fusion.1
  224.8 1.7 slice_bitcast_fusion.1
  226.6 0.7 copy-done.16
  227.3 1.6 fusion.5
  228.9 1.8 fusion.11
  230.7 1.7 add_convert_fusion
  232.4 8.2 %all_to_all.11 = bf16[2,2,8,24,3584]{4,3,2,1,0:T(8,128)(2,1)S(1)} all-to-all(bf16[2,2,8,24,3584]{4,3,2,1,0:T(8,128)(2,1)S(1)} %bitcast.73), channel_id=1, replica_groups=mesh['section'=8,'ex'=4,'em'=2,'ep'=2,'ec'=2] {'ec'}, dimensions={0} | all-to-all | bytes 11010048 | tf_op jit(solution)/shard_map/all_to_all | solution.py:273
  240.5 0.8 convert_add_fusion
  241.7 1.6 copy-done.2
  243.3 2.8 pad_maximum_fusion.mine
  246.1 1.8 pad_maximum_fusion.1.other
  247.9 97.4 %shard_map.158 = bf16[2,8,24,3584]{3,2,1,0:T(8,128)(2,1)} custom-call(f32[2,8,24,3584]{3,2,1,0:T(8,128)} %pad_maximum_fusion.mine, bf16[2,8,24,3584]{3,2,1,0:T(8,128)(2,1)} %pad_maximum_fusion.1.other), custom_call_target="tpu_custom_call" | custom-call | tf_op jit(solution)/shard_map/pallas_call | solution.py:281
  345.2 1.9 fusion.58
  347.2 1.4 fusion.1
  349.2 0.6 copy-done.4
  349.8 2.6 fusion.25
  (48 shorter events, 1.8 us)
Async XLA Ops:
  0.6 201.7 %copy-start = (bf16[1,3584,256]{2,1,0:T(8,128)(2,1)S(1)}, bf16[1,3584,256]{2,1,0:T(8,128)(2,1)}, u32[]{:S(2)}) copy-start(bf16[1,3584,256]{2,1,0:T(8,128)(2,1)} %param.25) | copy-start | bytes 5505028
  0.6 18.4 %copy-start.6 = (f32[1,3584]{1,0:T(1,128)S(1)}, f32[1,3584]{1,0:T(1,128)}, u32[]{:S(2)}) copy-start(f32[1,3584]{1,0:T(1,128)} %param.27) | copy-start | bytes 43012
  0.7 18.3 %copy-start.7 = (s32[1,128,1]{1,2,0:T(1,128)S(1)}, s32[1,128,1]{1,2,0:T(1,128)}, u32[]{:S(2)}) copy-start(s32[1,128,1]{1,2,0:T(1,128)} %param.16) | copy-start | bytes 1540
  0.7 18.1 %copy-start.8 = (s32[1,128,1]{1,2,0:T(1,128)S(1)}, s32[1,128,1]{1,2,0:T(1,128)}, u32[]{:S(2)}) copy-start(s32[1,128,1]{1,2,0:T(1,128)} %param.20) | copy-start | bytes 1540
  0.7 72.1 %collective-permute-start = (bf16[1,128,3584]{2,1,0:T(8,128)(2,1)}, bf16[1,128,3584]{2,1,0:T(8,128)(2,1)}, u32[]{:S(2)}, u32[]{:S(2)}) collective-permute-start(bf16[1,128,3584]{2,1,0:T(8,128)(2,1)} %param.15), channel_id=1, source_target_pairs={{0,32},{32,64},{64,96},{96,128},{128,160},{160,192},{192,224},{1,3... | collective-permute-start | bytes 2752520 | tf_op jit(solution)/shard_map/ppermute | solution.py:22
  9.9 59.5 %collective-permute-start.1 = (bf16[1,128,3584]{2,1,0:T(8,128)(2,1)}, bf16[1,128,3584]{2,1,0:T(8,128)(2,1)}, u32[]{:S(2)}, u32[]{:S(2)}) collective-permute-start(bf16[1,128,3584]{2,1,0:T(8,128)(2,1)} %param.19), channel_id=1, source_target_pairs={{32,0},{64,32},{96,64},{128,96},{160,128},{192,160},{224,192},{33,... | collective-permute-start | bytes 2752520 | tf_op jit(solution)/shard_map/ppermute | solution.py:22
  19.0 53.8 %copy-start.9 = (s32[128]{0:T(128)}, s32[128]{0:T(128)S(1)}, u32[]{:S(2)}) copy-start(s32[128]{0:T(128)S(1)} %multiply_add_fusion.1) | copy-start | bytes 1540
  19.1 52.0 %copy-start.12 = (s32[128]{0:T(128)}, s32[128]{0:T(128)S(1)}, u32[]{:S(2)}) copy-start(s32[128]{0:T(128)S(1)} %multiply_add_fusion) | copy-start | bytes 1540
  19.1 51.9 %copy-start.14 = (f32[1,128]{1,0:T(1,128)S(1)}, f32[1,128]{1,0:T(1,128)}, u32[]{:S(2)}) copy-start(f32[1,128]{1,0:T(1,128)} %param.21) | copy-start | bytes 1540
  71.0 1.8 copy-start.3
  213.8 12.7 %slice-start = ((s8[5505024]{0:T(1024)(128)(4,1)}), s8[4194304]{0:T(1024)(128)(4,1)S(1)}, s32[]{:S(2)}) async-start(s8[5505024]{0:T(1024)(128)(4,1)} %bitcast.93), calls=%async_computation.2 | async-start | bytes 8388608
  223.9 2.7 slice-start.1
  224.8 2.4 copy-start.16
  227.3 1.6 copy-start.5
  241.5 1.8 copy-start.2
  345.2 2.0 copy-start.13
  347.2 1.4 copy-start.10
  347.2 1.4 copy-start.15
  348.6 1.2 copy-start.4
  349.1 3.2 copy-start.11
  349.1 3.2 copy-start.1

commit v6 on v5

--- a/solution.py
+++ b/solution.py
@@ -192,8 +192,11 @@
     )(*sends)
 
 
-def collect_kernel(groups, mine, other, back, landed, summed, swap_recv, swap_send, back_recv, back_send):
-    streams = mine.shape[0]
+def collect_kernel(
+    groups, parts, back, near_land, other_buf, pair_land, summed,
+    near_recv, near_send, swap_recv, swap_send, back_recv, back_send,
+):
+    streams = parts.shape[0]
     section = lax.axis_index("section")
     ex = lax.axis_index("ex")
     em = lax.axis_index("em")
@@ -201,6 +204,7 @@
     ec = lax.axis_index("ec")
     me = ex * 2 + em
     partner = (section, ex, em, 1 - ep, ec)
+    sibling = (section, ex, em, ep, 1 - ec)
 
     def peer(g):
         return (section, g // 2, g % 2, ep, ec)
@@ -209,12 +213,23 @@
     for d in range(1, groups):
         pl.semaphore_signal(barrier, inc=1, device_id=peer((me + d) % groups), device_id_type=MESH_IDS)
     pl.semaphore_signal(barrier, inc=1, device_id=partner, device_id_type=MESH_IDS)
-    pl.semaphore_wait(barrier, groups)
+    pl.semaphore_signal(barrier, inc=1, device_id=sibling, device_id_type=MESH_IDS)
+    pl.semaphore_wait(barrier, groups + 1)
+
+    def near(s, q, g):
+        return pltpu.make_async_remote_copy(
+            src_ref=parts.at[s, 1 - ec, q, g],
+            dst_ref=near_land.at[s, q, g],
+            send_sem=near_send.at[s, q, g],
+            recv_sem=near_recv.at[s, q, g],
+            device_id=sibling,
+            device_id_type=MESH_IDS,
+        )
 
     def swap(s, g):
         return pltpu.make_async_remote_copy(
-            src_ref=other.at[s, g],
-            dst_ref=landed.at[s, g],
+            src_ref=other_buf.at[s, g],
+            dst_ref=pair_land.at[s, g],
             send_sem=swap_send.at[s, g],
             recv_sem=swap_recv.at[s, g],
             device_id=partner,
@@ -241,15 +256,26 @@
             device_id_type=MESH_IDS,
         )
 
+    for q in (1, 0):
+        for d in range(1, groups + 1):
+            for s in range(streams):
+                near(s, q, (me + d) % groups).start()
     for d in range(1, groups + 1):
         for s in range(streams):
-            swap(s, (me + d) % groups).start()
+            g = (me + d) % groups
+            near(s, 1, g).wait_recv()
+            other_buf[s, g] = (
+                parts[s, ec, 1, g].astype(jnp.float32) + near_land[s, 1, g].astype(jnp.float32)
+            ).astype(other_buf.dtype)
+            swap(s, g).start()
     local = []
     for d in range(1, groups + 1):
         for s in range(streams):
             g = (me + d) % groups
+            near(s, 0, g).wait_recv()
             swap(s, g).wait_recv()
-            summed[s, g] = (mine[s, g] + landed[s, g].astype(jnp.float32)).astype(summed.dtype)
+            pair = parts[s, ec, 0, g].astype(jnp.float32) + near_land[s, 0, g].astype(jnp.float32)
+            summed[s, g] = (pair + pair_land[s, g].astype(jnp.float32)).astype(summed.dtype)
             if d < groups:
                 reply(s, g).start()
             else:
@@ -262,37 +288,40 @@
             incoming(s, (me + d) % groups).wait_recv()
     for s in range(streams):
         for d in range(1, groups + 1):
-            swap(s, (me + d) % groups).wait_send()
+            g = (me + d) % groups
+            swap(s, g).wait_send()
+            near(s, 0, g).wait_send()
+            near(s, 1, g).wait_send()
         for d in range(1, groups):
             reply(s, (me + d) % groups).wait_send()
 
 
 def collect_from_holders(*parts):
-    mine, other = [], []
-    for part in parts:
-        swapped = lax.all_to_all(part, "ec", split_axis=0, concat_axis=0, tiled=True)
-        pair = swapped[0].astype(jnp.float32) + swapped[1].astype(jnp.float32)
-        mine.append(pair[0])
-        other.append(pair[1].astype(jnp.bfloat16))
-    mine = jnp.stack(mine)
-    other = jnp.stack(other)
-    streams, groups = mine.shape[:2]
+    parts = jnp.stack(parts)
+    streams, _, _, groups, capacity, features = parts.shape
+    block = (streams, groups, capacity, features)
     any_spec = pl.BlockSpec(memory_space=pl.ANY)
     back = pl.pallas_call(
         functools.partial(collect_kernel, groups),
-        out_shape=jax.ShapeDtypeStruct(other.shape, jnp.bfloat16),
-        in_specs=[pl.BlockSpec(memory_space=pltpu.VMEM), any_spec],
+        out_shape=jax.ShapeDtypeStruct(block, jnp.bfloat16),
+        in_specs=[pl.BlockSpec(memory_space=pltpu.VMEM)],
         out_specs=any_spec,
         scratch_shapes=[
-            pltpu.VMEM(other.shape, jnp.bfloat16),
-            pltpu.VMEM(other.shape, jnp.bfloat16),
+            pltpu.VMEM((streams, 2, groups, capacity, features), jnp.bfloat16),
+            pltpu.VMEM(block, jnp.bfloat16),
+            pltpu.VMEM(block, jnp.bfloat16),
+            pltpu.VMEM(block, jnp.bfloat16),
+            pltpu.SemaphoreType.DMA((streams, 2, groups)),
+            pltpu.SemaphoreType.DMA((streams, 2, groups)),
             pltpu.SemaphoreType.DMA((streams, groups)),
             pltpu.SemaphoreType.DMA((streams, groups)),
             pltpu.SemaphoreType.DMA((streams, groups)),
             pltpu.SemaphoreType.DMA((streams, groups)),
         ],
-        compiler_params=pltpu.CompilerParams(collective_id=1, has_side_effects=True),
-    )(mine, other)
+        compiler_params=pltpu.CompilerParams(
+            collective_id=1, has_side_effects=True, vmem_limit_bytes=60 * 1024 * 1024
+        ),
+    )(parts)
     return [back[s] for s in range(streams)]
 
 

time: 357 us -> 342 us (0.958)
  blocking collectives: 18.2 us -> 0 us
  local copies, waits for them, and re-layouts: 9.16 us -> 4.68 us
  Pallas kernels: 218 us -> 222 us
    all_to_all x2 -> x0, blocking collectives: 18.2 us -> none  [collect_from_holders(): lax.all_to_all(part, 'ec', split_axis=0, concat_axis=0, tiled=True)]
    dot_general x1, matrix products: 1.61 us -> 5.77 us  [expert_backward(): lax.dot_general(slot_rows, down_rows, contract, preferred_element_type=jn...]
    pallas_call x1, Pallas kernels: 97.4 us -> 101 us  [collect_from_holders(): pl.pallas_call(functools.partial(collect_kernel, groups), out_shape=jax.S...]
    another operation x2 -> x1, other arithmetic: 4.58 us -> 7.66 us  [collect_from_holders(): parts = jnp.stack(parts)]
where the time goes in v6:
time: 342 us; the launch traced here: 338 us
  Pallas kernels  222 us (65%)
  waiting for transfers between devices  50.1 us (15%)
  matrix products  31.7 us (9%)
  other arithmetic  16.2 us (5%)
  starting transfers between devices  11.3 us (3%)
  local copies, waits for them, and re-layouts  4.68 us (1%)
    pallas_call x1, Pallas kernels, spread_to_holders(): pl.pallas_call(functools.partial(spread_kernel, groups), out_shape=[rows]...  121 us
    pallas_call x1, Pallas kernels, collect_from_holders(): pl.pallas_call(functools.partial(collect_kernel, groups), out_shape=jax.S...  101 us
    ppermute x2, waiting for transfers between devices, shifted(): return lax.ppermute(value, axis, pairs)  50.1 us
    dot_general x1, matrix products, expert_forward(): jnp.dot(hidden, down_rows, preferred_element_type=jnp.float32)  11.5 us
    ppermute x2, starting transfers between devices, shifted(): return lax.ppermute(value, axis, pairs)  11.3 us
    another operation x1, other arithmetic, collect_from_holders(): parts = jnp.stack(parts)  7.66 us
  transfers between devices with their start and end apart: 2, of which 1 were waited for; matrix products, arithmetic and copies ran while one was open for 3% of the time, Pallas kernels for 0%

profile of v6, /device:TPU:24, one launch (start us, length us, event | category | flops | bytes accessed | tf_op | source)
XLA Modules:
  0.0 337.7 jit_solution(15306123287959575305)
XLA Ops:
  0.6 0.0 copy-start
  0.7 0.0 copy-start.7
  0.7 9.2 %collective-permute-start = (bf16[1,128,3584]{2,1,0:T(8,128)(2,1)}, bf16[1,128,3584]{2,1,0:T(8,128)(2,1)}, u32[]{:S(2)}, u32[]{:S(2)}) collective-permute-start(bf16[1,128,3584]{2,1,0:T(8,128)(2,1)} %param.15), channel_id=1, source_target_pairs={{0,32},{32,64},{64,96},{96,128},{128,160},{160,192},{192,224},{1,3... | collective-permute-start | bytes 2752520 | tf_op jit(solution)/shard_map/ppermute | solution.py:22
  9.9 2.1 collective-permute-start.1
  12.0 1.3 multiply_reduce_fusion.1
  14.1 0.7 fusion.48
  14.8 0.2 reduce_window_sum.17
  15.0 0.8 select_reduce_fusion.1
  15.8 0.7 fusion.47
  16.6 0.2 reduce_window_sum.18
  16.8 1.0 copy.21
  17.8 1.0 copy.22
  18.8 0.2 select_reduce_fusion
  19.1 0.1 reverse_select_fusion
  19.3 50.1 %collective-permute-done.1 = bf16[1,128,3584]{2,1,0:T(8,128)(2,1)} collective-permute-done((bf16[1,128,3584]{2,1,0:T(8,128)(2,1)}, bf16[1,128,3584]{2,1,0:T(8,128)(2,1)}, u32[]{:S(2)}, u32[]{:S(2)}) %collective-permute-start.1) | collective-permute-done | bytes 917536 | tf_op jit(solution)/shard_map/ppermute | solution.py:22
  69.4 1.6 fusion.2
  71.0 0.0 copy-start.2
  71.0 1.8 convolution_convert_fusion.1
  72.8 2.8 convolution_convert_fusion.2
  75.6 121.1 %shard_map.157 = (bf16[2,2,8,24,3584]{4,3,2,1,0:T(8,128)(2,1)}, bf16[2,2,8,24,3584]{4,3,2,1,0:T(8,128)(2,1)}) custom-call(bf16[8,24,3584]{2,1,0:T(8,128)(2,1)} %bitcast.70, bf16[8,24,3584]{2,1,0:T(8,128)(2,1)} %bitcast.68), custom_call_target="tpu_custom_call" | custom-call | tf_op jit(solution)/shard_map/pallas_call | solution.py:178
  196.7 5.8 %fusion.5 = f32[768,256]{1,0:T(8,128)} fusion(bf16[768,3584]{1,0:T(8,128)(2,1)} %bitcast.87, bf16[1,256,3584]{2,1,0:T(8,128)(2,1)} %param.26), kind=kOutput, calls=%fused_computation.14 | convolution fusion | flops 1409286144 | bytes 8126464 | tf_op jit(solution)/shard_map/dot_general | solution.py:48
  202.5 2.5 fusion.13
  205.0 11.5 %convolution_convert_fusion = bf16[768,3584]{1,0:T(8,128)(2,1)} fusion(bf16[1,256,3584]{2,1,0:T(8,128)(2,1)} %param.26, bf16[768,3584]{1,0:T(8,128)(2,1)} %bitcast.85, bf16[1,3584,256]{2,1,0:T(8,128)(2,1)S(1)} %copy-done, f32[768,256]{1,0:T(8,128)} %fusion.13), kind=kOutput, calls=%fused_computation.2 | convolution fusion | flops 2822504448 | bytes 15466496 | tf_op jit(solution)/shard_map/dot_general | solution.py:42
  216.5 3.6 %fusion.11 = f32[768,3584]{1,0:T(8,128)S(1)} fusion(bf16[1,3584,256]{2,1,0:T(8,128)(2,1)} %param.24, bf16[768,256]{1,0:T(8,128)(2,1)S(1)} %bitcast.71, f32[768,256]{1,0:T(8,128)} %fusion.5, bf16[768,256]{1,0:T(8,128)(2,1)S(1)} %bitcast.73), kind=kOutput, calls=%fused_computation.20 | convolution fusion | flops 1411645440 | bytes 14417920 | tf_op jit(solution)/shard_map/dot_general | solution.py:58
  220.0 1.9 add_convert_fusion
  222.0 7.7 %pad_maximum_fusion.parts = bf16[2,2,2,8,24,3584]{5,4,3,2,1,0:T(8,128)(2,1)} fusion(bf16[1,2,2,8,24,3584]{5,4,3,2,1,0:T(8,128)(2,1)S(1)} %bitcast.65, bf16[1,2,2,8,24,3584]{5,4,3,2,1,0:T(8,128)(2,1)} %bitcast.67), kind=kLoop, calls=%fused_computation | loop fusion | flops 5505024 | bytes 22020096 | tf_op jit(solution)/shard_map/stack | solution.py:300
  229.6 101.0 %shard_map.158 = bf16[2,8,24,3584]{3,2,1,0:T(8,128)(2,1)} custom-call(bf16[2,2,2,8,24,3584]{5,4,3,2,1,0:T(8,128)(2,1)} %pad_maximum_fusion.parts), custom_call_target="tpu_custom_call" | custom-call | tf_op jit(solution)/shard_map/pallas_call | solution.py:304
  330.6 1.9 fusion.56
  332.6 1.4 fusion.1
  334.0 0.5 multiply_reduce_fusion
  334.5 0.6 copy-done.3
  335.1 2.6 fusion.23
  (34 shorter events, 0.1 us)
Async XLA Ops:
  0.6 204.4 %copy-start = (bf16[1,3584,256]{2,1,0:T(8,128)(2,1)S(1)}, bf16[1,3584,256]{2,1,0:T(8,128)(2,1)}, u32[]{:S(2)}) copy-start(bf16[1,3584,256]{2,1,0:T(8,128)(2,1)} %param.25) | copy-start | bytes 5505028
  0.6 18.4 %copy-start.6 = (f32[1,3584]{1,0:T(1,128)S(1)}, f32[1,3584]{1,0:T(1,128)}, u32[]{:S(2)}) copy-start(f32[1,3584]{1,0:T(1,128)} %param.27) | copy-start | bytes 43012
  0.7 18.3 %copy-start.7 = (s32[1,128,1]{1,2,0:T(1,128)S(1)}, s32[1,128,1]{1,2,0:T(1,128)}, u32[]{:S(2)}) copy-start(s32[1,128,1]{1,2,0:T(1,128)} %param.16) | copy-start | bytes 1540
  0.7 18.1 %copy-start.8 = (s32[1,128,1]{1,2,0:T(1,128)S(1)}, s32[1,128,1]{1,2,0:T(1,128)}, u32[]{:S(2)}) copy-start(s32[1,128,1]{1,2,0:T(1,128)} %param.20) | copy-start | bytes 1540
  0.7 72.1 %collective-permute-start = (bf16[1,128,3584]{2,1,0:T(8,128)(2,1)}, bf16[1,128,3584]{2,1,0:T(8,128)(2,1)}, u32[]{:S(2)}, u32[]{:S(2)}) collective-permute-start(bf16[1,128,3584]{2,1,0:T(8,128)(2,1)} %param.15), channel_id=1, source_target_pairs={{0,32},{32,64},{64,96},{96,128},{128,160},{160,192},{192,224},{1,3... | collective-permute-start | bytes 2752520 | tf_op jit(solution)/shard_map/ppermute | solution.py:22
  9.9 59.5 %collective-permute-start.1 = (bf16[1,128,3584]{2,1,0:T(8,128)(2,1)}, bf16[1,128,3584]{2,1,0:T(8,128)(2,1)}, u32[]{:S(2)}, u32[]{:S(2)}) collective-permute-start(bf16[1,128,3584]{2,1,0:T(8,128)(2,1)} %param.19), channel_id=1, source_target_pairs={{32,0},{64,32},{96,64},{128,96},{160,128},{192,160},{224,192},{33,... | collective-permute-start | bytes 2752520 | tf_op jit(solution)/shard_map/ppermute | solution.py:22
  19.0 53.8 %copy-start.9 = (s32[128]{0:T(128)}, s32[128]{0:T(128)S(1)}, u32[]{:S(2)}) copy-start(s32[128]{0:T(128)S(1)} %multiply_add_fusion.1) | copy-start | bytes 1540
  19.1 52.0 %copy-start.12 = (s32[128]{0:T(128)}, s32[128]{0:T(128)S(1)}, u32[]{:S(2)}) copy-start(s32[128]{0:T(128)S(1)} %multiply_add_fusion) | copy-start | bytes 1540
  19.1 51.9 %copy-start.14 = (f32[1,128]{1,0:T(1,128)S(1)}, f32[1,128]{1,0:T(1,128)}, u32[]{:S(2)}) copy-start(f32[1,128]{1,0:T(1,128)} %param.21) | copy-start | bytes 1540
  71.0 1.8 copy-start.2
  196.7 5.8 %copy-start.5 = (bf16[1,3584,256]{2,1,0:T(8,128)(2,1)S(1)}, bf16[1,3584,256]{2,1,0:T(8,128)(2,1)}, u32[]{:S(2)}) copy-start(bf16[1,3584,256]{2,1,0:T(8,128)(2,1)} %param.24) | copy-start | bytes 5505028
  196.7 5.8 %copy-start.16 = (bf16[2,2,8,24,3584]{4,3,2,1,0:T(8,128)(2,1)S(1)}, bf16[2,2,8,24,3584]{4,3,2,1,0:T(8,128)(2,1)}, u32[]{:S(2)}) copy-start(bf16[2,2,8,24,3584]{4,3,2,1,0:T(8,128)(2,1)} %get-tuple-element.5) | copy-start | bytes 16515076
  216.4 3.6 %copy-start.4 = (f32[768,256]{1,0:T(8,128)S(1)}, f32[768,256]{1,0:T(8,128)}, u32[]{:S(2)}) copy-start(f32[768,256]{1,0:T(8,128)} %fusion.5) | copy-start | bytes 2359300
  330.6 2.0 copy-start.13
  332.5 1.4 copy-start.10
  332.6 1.4 copy-start.15
  334.0 1.2 copy-start.3
  334.5 3.2 copy-start.11
  334.5 3.2 copy-start.1

commit v7 on v6

--- a/solution.py
+++ b/solution.py
@@ -192,11 +192,11 @@
     )(*sends)
 
 
-def collect_kernel(
-    groups, parts, back, near_land, other_buf, pair_land, summed,
-    near_recv, near_send, swap_recv, swap_send, back_recv, back_send,
-):
-    streams = parts.shape[0]
+def collect_kernel(groups, *refs):
+    streams = len(refs) - 11
+    parts = refs[:streams]
+    back, near_land, other_buf, pair_land, summed = refs[streams : streams + 5]
+    near_recv, near_send, swap_recv, swap_send, back_recv, back_send = refs[streams + 5 :]
     section = lax.axis_index("section")
     ex = lax.axis_index("ex")
     em = lax.axis_index("em")
@@ -218,7 +218,7 @@
 
     def near(s, q, g):
         return pltpu.make_async_remote_copy(
-            src_ref=parts.at[s, 1 - ec, q, g],
+            src_ref=parts[s].at[1 - ec, q, g],
             dst_ref=near_land.at[s, q, g],
             send_sem=near_send.at[s, q, g],
             recv_sem=near_recv.at[s, q, g],
@@ -265,7 +265,7 @@
             g = (me + d) % groups
             near(s, 1, g).wait_recv()
             other_buf[s, g] = (
-                parts[s, ec, 1, g].astype(jnp.float32) + near_land[s, 1, g].astype(jnp.float32)
+                parts[s][ec, 1, g].astype(jnp.float32) + near_land[s, 1, g].astype(jnp.float32)
             ).astype(other_buf.dtype)
             swap(s, g).start()
     local = []
@@ -274,7 +274,7 @@
             g = (me + d) % groups
             near(s, 0, g).wait_recv()
             swap(s, g).wait_recv()
-            pair = parts[s, ec, 0, g].astype(jnp.float32) + near_land[s, 0, g].astype(jnp.float32)
+            pair = parts[s][ec, 0, g].astype(jnp.float32) + near_land[s, 0, g].astype(jnp.float32)
             summed[s, g] = (pair + pair_land[s, g].astype(jnp.float32)).astype(summed.dtype)
             if d < groups:
                 reply(s, g).start()
@@ -297,14 +297,14 @@
 
 
 def collect_from_holders(*parts):
-    parts = jnp.stack(parts)
-    streams, _, _, groups, capacity, features = parts.shape
+    streams = len(parts)
+    _, _, groups, capacity, features = parts[0].shape
     block = (streams, groups, capacity, features)
     any_spec = pl.BlockSpec(memory_space=pl.ANY)
     back = pl.pallas_call(
         functools.partial(collect_kernel, groups),
         out_shape=jax.ShapeDtypeStruct(block, jnp.bfloat16),
-        in_specs=[pl.BlockSpec(memory_space=pltpu.VMEM)],
+        in_specs=[pl.BlockSpec(memory_space=pltpu.VMEM)] * streams,
         out_specs=any_spec,
         scratch_shapes=[
             pltpu.VMEM((streams, 2, groups, capacity, features), jnp.bfloat16),
@@ -321,7 +321,7 @@
         compiler_params=pltpu.CompilerParams(
             collective_id=1, has_side_effects=True, vmem_limit_bytes=60 * 1024 * 1024
         ),
-    )(parts)
+    )(*parts)
     return [back[s] for s in range(streams)]
 
 

time: 342 us -> 337 us (0.985)
  other arithmetic: 16.2 us -> 8.54 us
    another operation x1 -> x0, other arithmetic: 7.66 us -> none  [collect_from_holders(): parts = jnp.stack(parts)]
where the time goes in v7:
time: 337 us; the launch traced here: 333 us
  Pallas kernels  222 us (66%)
  waiting for transfers between devices  50.1 us (15%)
  matrix products  34.2 us (10%)
  starting transfers between devices  11.3 us (3%)
  other arithmetic  8.54 us (3%)
  local copies, waits for them, and re-layouts  4.68 us (1%)
    pallas_call x1, Pallas kernels, spread_to_holders(): pl.pallas_call(functools.partial(spread_kernel, groups), out_shape=[rows]...  121 us
    pallas_call x1, Pallas kernels, collect_from_holders(): pl.pallas_call(functools.partial(collect_kernel, groups), out_shape=jax.S...  101 us
    ppermute x2, waiting for transfers between devices, shifted(): return lax.ppermute(value, axis, pairs)  50.1 us
    dot_general x1, matrix products, expert_forward(): jnp.dot(hidden, down_rows, preferred_element_type=jnp.float32)  11.6 us
    ppermute x2, starting transfers between devices, shifted(): return lax.ppermute(value, axis, pairs)  11.3 us
  transfers between devices with their start and end apart: 2, of which 1 were waited for; matrix products, arithmetic and copies ran while one was open for 3% of the time, Pallas kernels for 0%

profile of v7, /device:TPU:24, one launch (start us, length us, event | category | flops | bytes accessed | tf_op | source)
XLA Modules:
  0.0 332.6 jit_solution(1128308426982939554)
XLA Ops:
  0.6 0.0 copy-start
  0.7 9.2 %collective-permute-start = (bf16[1,128,3584]{2,1,0:T(8,128)(2,1)}, bf16[1,128,3584]{2,1,0:T(8,128)(2,1)}, u32[]{:S(2)}, u32[]{:S(2)}) collective-permute-start(bf16[1,128,3584]{2,1,0:T(8,128)(2,1)} %param.15), channel_id=1, source_target_pairs={{0,32},{32,64},{64,96},{96,128},{128,160},{160,192},{192,224},{1,3... | collective-permute-start | bytes 2752520 | tf_op jit(solution)/shard_map/ppermute | solution.py:22
  9.9 2.1 collective-permute-start.1
  12.0 1.3 multiply_reduce_fusion.1
  14.1 0.7 fusion.48
  14.8 0.2 reduce_window_sum.17
  15.0 0.8 select_reduce_fusion.1
  15.8 0.7 fusion.47
  16.6 0.2 reduce_window_sum.18
  16.8 1.0 copy.21
  17.8 1.0 copy.22
  18.8 0.2 select_reduce_fusion
  19.1 0.1 reverse_select_fusion
  19.3 50.1 %collective-permute-done.1 = bf16[1,128,3584]{2,1,0:T(8,128)(2,1)} collective-permute-done((bf16[1,128,3584]{2,1,0:T(8,128)(2,1)}, bf16[1,128,3584]{2,1,0:T(8,128)(2,1)}, u32[]{:S(2)}, u32[]{:S(2)}) %collective-permute-start.1) | collective-permute-done | bytes 917536 | tf_op jit(solution)/shard_map/ppermute | solution.py:22
  69.4 1.6 fusion.2
  71.0 0.0 copy-start.1
  71.0 1.8 convolution_convert_fusion.1
  72.8 2.8 convolution_convert_fusion.2
  75.6 121.1 %shard_map.157 = (bf16[2,2,8,24,3584]{4,3,2,1,0:T(8,128)(2,1)}, bf16[2,2,8,24,3584]{4,3,2,1,0:T(8,128)(2,1)}) custom-call(bf16[8,24,3584]{2,1,0:T(8,128)(2,1)} %bitcast.70, bf16[8,24,3584]{2,1,0:T(8,128)(2,1)} %bitcast.68), custom_call_target="tpu_custom_call" | custom-call | tf_op jit(solution)/shard_map/pallas_call | solution.py:178
  196.7 0.0 copy-start.4
  196.8 5.8 %fusion.5 = f32[768,256]{1,0:T(8,128)} fusion(bf16[768,3584]{1,0:T(8,128)(2,1)} %bitcast.87, bf16[1,256,3584]{2,1,0:T(8,128)(2,1)} %param.26), kind=kOutput, calls=%fused_computation.13 | convolution fusion | flops 1409286144 | bytes 8126464 | tf_op jit(solution)/shard_map/dot_general | solution.py:48
  202.5 2.5 fusion.13
  205.0 11.6 %convolution_convert_fusion = bf16[768,3584]{1,0:T(8,128)(2,1)} fusion(bf16[1,256,3584]{2,1,0:T(8,128)(2,1)} %param.26, bf16[768,3584]{1,0:T(8,128)(2,1)} %bitcast.85, bf16[1,3584,256]{2,1,0:T(8,128)(2,1)S(1)} %copy-done, f32[768,256]{1,0:T(8,128)} %fusion.13), kind=kOutput, calls=%fused_computation.1 | convolution fusion | flops 2822504448 | bytes 15466496 | tf_op jit(solution)/shard_map/dot_general | solution.py:42
  216.6 3.6 %fusion.11 = f32[768,3584]{1,0:T(8,128)S(1)} fusion(bf16[1,3584,256]{2,1,0:T(8,128)(2,1)} %param.24, bf16[768,256]{1,0:T(8,128)(2,1)S(1)} %bitcast.71, f32[768,256]{1,0:T(8,128)} %fusion.5, bf16[768,256]{1,0:T(8,128)(2,1)S(1)} %bitcast.73), kind=kOutput, calls=%fused_computation.19 | convolution fusion | flops 1411645440 | bytes 14417920 | tf_op jit(solution)/shard_map/dot_general | solution.py:58
  220.1 4.3 %add_convert_fusion = bf16[768,3584]{1,0:T(8,128)(2,1)} fusion(f32[768,3584]{1,0:T(8,128)S(1)} %fusion.11, bf16[1,3584,256]{2,1,0:T(8,128)(2,1)S(1)} %copy-done, f32[768,256]{1,0:T(8,128)S(1)} %copy-done.3, bf16[768,256]{1,0:T(8,128)(2,1)S(1)} %bitcast.72), kind=kOutput, calls=%fused_computation | convolution fusion | flops 1416167424 | bytes 19529728 | tf_op jit(solution)/shard_map/dot_general | solution.py:59
  224.4 101.0 %shard_map.158 = bf16[2,8,24,3584]{3,2,1,0:T(8,128)(2,1)} custom-call(bf16[2,2,8,24,3584]{4,3,2,1,0:T(8,128)(2,1)} %bitcast.67, bf16[2,2,8,24,3584]{4,3,2,1,0:T(8,128)(2,1)} %bitcast.65), custom_call_target="tpu_custom_call" | custom-call | tf_op jit(solution)/shard_map/pallas_call | solution.py:304
  325.5 1.9 fusion.56
  327.5 0.0 copy-start.14
  327.5 1.4 fusion.1
  328.9 0.5 multiply_reduce_fusion
  329.4 0.6 copy-done.2
  330.0 2.6 fusion.23
  (31 shorter events, 0.1 us)
Async XLA Ops:
  0.6 204.4 %copy-start = (bf16[1,3584,256]{2,1,0:T(8,128)(2,1)S(1)}, bf16[1,3584,256]{2,1,0:T(8,128)(2,1)}, u32[]{:S(2)}) copy-start(bf16[1,3584,256]{2,1,0:T(8,128)(2,1)} %param.25) | copy-start | bytes 5505028
  0.6 18.4 %copy-start.5 = (f32[1,3584]{1,0:T(1,128)S(1)}, f32[1,3584]{1,0:T(1,128)}, u32[]{:S(2)}) copy-start(f32[1,3584]{1,0:T(1,128)} %param.27) | copy-start | bytes 43012
  0.7 18.3 %copy-start.6 = (s32[1,128,1]{1,2,0:T(1,128)S(1)}, s32[1,128,1]{1,2,0:T(1,128)}, u32[]{:S(2)}) copy-start(s32[1,128,1]{1,2,0:T(1,128)} %param.16) | copy-start | bytes 1540
  0.7 18.1 %copy-start.7 = (s32[1,128,1]{1,2,0:T(1,128)S(1)}, s32[1,128,1]{1,2,0:T(1,128)}, u32[]{:S(2)}) copy-start(s32[1,128,1]{1,2,0:T(1,128)} %param.20) | copy-start | bytes 1540
  0.7 72.1 %collective-permute-start = (bf16[1,128,3584]{2,1,0:T(8,128)(2,1)}, bf16[1,128,3584]{2,1,0:T(8,128)(2,1)}, u32[]{:S(2)}, u32[]{:S(2)}) collective-permute-start(bf16[1,128,3584]{2,1,0:T(8,128)(2,1)} %param.15), channel_id=1, source_target_pairs={{0,32},{32,64},{64,96},{96,128},{128,160},{160,192},{192,224},{1,3... | collective-permute-start | bytes 2752520 | tf_op jit(solution)/shard_map/ppermute | solution.py:22
  9.9 59.5 %collective-permute-start.1 = (bf16[1,128,3584]{2,1,0:T(8,128)(2,1)}, bf16[1,128,3584]{2,1,0:T(8,128)(2,1)}, u32[]{:S(2)}, u32[]{:S(2)}) collective-permute-start(bf16[1,128,3584]{2,1,0:T(8,128)(2,1)} %param.19), channel_id=1, source_target_pairs={{32,0},{64,32},{96,64},{128,96},{160,128},{192,160},{224,192},{33,... | collective-permute-start | bytes 2752520 | tf_op jit(solution)/shard_map/ppermute | solution.py:22
  19.0 53.8 %copy-start.8 = (s32[128]{0:T(128)}, s32[128]{0:T(128)S(1)}, u32[]{:S(2)}) copy-start(s32[128]{0:T(128)S(1)} %multiply_add_fusion.1) | copy-start | bytes 1540
  19.0 52.0 %copy-start.11 = (s32[128]{0:T(128)}, s32[128]{0:T(128)S(1)}, u32[]{:S(2)}) copy-start(s32[128]{0:T(128)S(1)} %multiply_add_fusion) | copy-start | bytes 1540
  19.1 51.9 %copy-start.13 = (f32[1,128]{1,0:T(1,128)S(1)}, f32[1,128]{1,0:T(1,128)}, u32[]{:S(2)}) copy-start(f32[1,128]{1,0:T(1,128)} %param.21) | copy-start | bytes 1540
  71.0 1.8 copy-start.1
  196.7 5.8 %copy-start.4 = (bf16[1,3584,256]{2,1,0:T(8,128)(2,1)S(1)}, bf16[1,3584,256]{2,1,0:T(8,128)(2,1)}, u32[]{:S(2)}) copy-start(bf16[1,3584,256]{2,1,0:T(8,128)(2,1)} %param.24) | copy-start | bytes 5505028
  196.7 5.8 %copy-start.15 = (bf16[2,2,8,24,3584]{4,3,2,1,0:T(8,128)(2,1)S(1)}, bf16[2,2,8,24,3584]{4,3,2,1,0:T(8,128)(2,1)}, u32[]{:S(2)}) copy-start(bf16[2,2,8,24,3584]{4,3,2,1,0:T(8,128)(2,1)} %get-tuple-element.5) | copy-start | bytes 16515076
  216.6 3.6 %copy-start.3 = (f32[768,256]{1,0:T(8,128)S(1)}, f32[768,256]{1,0:T(8,128)}, u32[]{:S(2)}) copy-start(f32[768,256]{1,0:T(8,128)} %fusion.5) | copy-start | bytes 2359300
  325.5 2.0 copy-start.12
  327.4 1.4 copy-start.9
  327.5 1.4 copy-start.14
  328.9 1.2 copy-start.2
  329.4 3.2 copy-start.10

commit v8 on v5

--- a/solution.py
+++ b/solution.py
@@ -67,10 +67,10 @@
 
 
 def spread_kernel(groups, *refs):
-    streams = (len(refs) - 6) // 2
+    streams = (len(refs) - 4) // 2
     sends = refs[:streams]
     rows = refs[streams : 2 * streams]
-    first_recv, first_send, pair_recv, pair_send, near_recv, near_send = refs[2 * streams : 2 * streams + 6]
+    first_recv, first_send, pair_recv, pair_send = refs[2 * streams :]
     section = lax.axis_index("section")
     ex = lax.axis_index("ex")
     em = lax.axis_index("em")
@@ -78,7 +78,6 @@
     ec = lax.axis_index("ec")
     me = ex * 2 + em
     partner = (section, ex, em, 1 - ep, ec)
-    sibling = (section, ex, em, ep, 1 - ec)
 
     def peer(g):
         return (section, g // 2, g % 2, ep, ec)
@@ -87,49 +86,46 @@
     for d in range(1, groups):
         pl.semaphore_signal(barrier, inc=1, device_id=peer((me + d) % groups), device_id_type=MESH_IDS)
     pl.semaphore_signal(barrier, inc=1, device_id=partner, device_id_type=MESH_IDS)
-    pl.semaphore_signal(barrier, inc=1, device_id=sibling, device_id_type=MESH_IDS)
-    pl.semaphore_wait(barrier, groups + 1)
-
-    def first_copy(s, g, target):
+    pl.semaphore_wait(barrier, groups)
+
+    def first_copy(s, g):
         return pltpu.make_async_remote_copy(
             src_ref=sends[s].at[g],
-            dst_ref=rows[s].at[ec, 0, me],
+            dst_ref=rows[s].at[0, me],
             send_sem=first_send.at[s, g],
             recv_sem=first_recv.at[s, me],
-            device_id=target,
+            device_id=peer(g),
             device_id_type=MESH_IDS,
         )
 
     def arrived(s, g):
         return pltpu.make_async_remote_copy(
             src_ref=sends[s].at[g],
-            dst_ref=rows[s].at[ec, 0, g],
+            dst_ref=rows[s].at[0, g],
             send_sem=first_send.at[s, g],
             recv_sem=first_recv.at[s, g],
             device_id=peer(g),
             device_id_type=MESH_IDS,
         )
 
-    def relay(s, q, g, target, recv, send, slot):
-        return pltpu.make_async_remote_copy(
-            src_ref=rows[s].at[ec, q, g],
-            dst_ref=rows[s].at[ec, slot, g],
-            send_sem=send.at[s, q, g],
-            recv_sem=recv.at[s, q, g],
-            device_id=target,
+    def relay(s, g):
+        return pltpu.make_async_remote_copy(
+            src_ref=rows[s].at[0, g],
+            dst_ref=rows[s].at[1, g],
+            send_sem=pair_send.at[s, g],
+            recv_sem=pair_recv.at[s, g],
+            device_id=partner,
             device_id_type=MESH_IDS,
         )
 
     local = []
     for s in range(streams):
-        copy = pltpu.make_async_copy(sends[s].at[me], rows[s].at[ec, 0, me], first_recv.at[s, me])
+        copy = pltpu.make_async_copy(sends[s].at[me], rows[s].at[0, me], first_recv.at[s, me])
         copy.start()
         local.append(copy)
     for d in range(1, groups):
         for s in range(streams):
-            g = (me + d) % groups
-            first_copy(s, g, peer(g)).start()
-    outgoing = []
+            first_copy(s, (me + d) % groups).start()
     for d in range(groups):
         for s in range(streams):
             g = (me + groups - d) % groups
@@ -137,43 +133,21 @@
                 arrived(s, g).wait_recv()
             else:
                 local[s].wait()
-            for target, recv, send, slot in (
-                (partner, pair_recv, pair_send, 1),
-                (sibling, near_recv, near_send, 0),
-            ):
-                copy = relay(s, 0, g, target, recv, send, slot)
-                copy.start()
-                outgoing.append(copy)
+            relay(s, g).start()
     for d in range(groups):
         for s in range(streams):
-            g = (me + groups - d) % groups
-            relay(s, 0, g, partner, pair_recv, pair_send, 1).wait_recv()
-            copy = relay(s, 1, g, sibling, near_recv, near_send, 1)
-            copy.start()
-            outgoing.append(copy)
-    for s in range(streams):
-        for q in range(2):
-            for g in range(groups):
-                pltpu.make_async_remote_copy(
-                    src_ref=rows[s].at[1 - ec, q, g],
-                    dst_ref=rows[s].at[1 - ec, q, g],
-                    send_sem=near_send.at[s, q, g],
-                    recv_sem=near_recv.at[s, q, g],
-                    device_id=sibling,
-                    device_id_type=MESH_IDS,
-                ).wait_recv()
+            relay(s, (me + groups - d) % groups).wait_recv()
     for s in range(streams):
         for d in range(1, groups):
-            g = (me + d) % groups
-            first_copy(s, g, peer(g)).wait_send()
-    for copy in outgoing:
-        copy.wait_send()
+            first_copy(s, (me + d) % groups).wait_send()
+        for g in range(groups):
+            relay(s, g).wait_send()
 
 
 def spread_to_holders(*sends):
     groups, capacity, features = sends[0].shape
     streams = len(sends)
-    rows = jax.ShapeDtypeStruct((2, 2, groups, capacity, features), sends[0].dtype)
+    rows = jax.ShapeDtypeStruct((2, groups, capacity, features), sends[0].dtype)
     any_spec = pl.BlockSpec(memory_space=pl.ANY)
     return pl.pallas_call(
         functools.partial(spread_kernel, groups),
@@ -183,10 +157,8 @@
         scratch_shapes=[
             pltpu.SemaphoreType.DMA((streams, groups)),
             pltpu.SemaphoreType.DMA((streams, groups)),
-            pltpu.SemaphoreType.DMA((streams, 2, groups)),
-            pltpu.SemaphoreType.DMA((streams, 2, groups)),
-            pltpu.SemaphoreType.DMA((streams, 2, groups)),
-            pltpu.SemaphoreType.DMA((streams, 2, groups)),
+            pltpu.SemaphoreType.DMA((streams, groups)),
+            pltpu.SemaphoreType.DMA((streams, groups)),
         ],
         compiler_params=pltpu.CompilerParams(collective_id=0, has_side_effects=True),
     )(*sends)
@@ -241,12 +213,12 @@
             device_id_type=MESH_IDS,
         )
 
-    for d in range(1, groups + 1):
-        for s in range(streams):
+    for s in range(streams):
+        for d in range(1, groups + 1):
             swap(s, (me + d) % groups).start()
     local = []
-    for d in range(1, groups + 1):
-        for s in range(streams):
+    for s in range(streams):
+        for d in range(1, groups + 1):
             g = (me + d) % groups
             swap(s, g).wait_recv()
             summed[s, g] = (mine[s, g] + landed[s, g].astype(jnp.float32)).astype(summed.dtype)
@@ -267,18 +239,10 @@
             reply(s, (me + d) % groups).wait_send()
 
 
-def collect_from_holders(*parts):
-    mine, other = [], []
-    for part in parts:
-        swapped = lax.all_to_all(part, "ec", split_axis=0, concat_axis=0, tiled=True)
-        pair = swapped[0].astype(jnp.float32) + swapped[1].astype(jnp.float32)
-        mine.append(pair[0])
-        other.append(pair[1].astype(jnp.bfloat16))
-    mine = jnp.stack(mine)
-    other = jnp.stack(other)
+def collect_from_holders(mine, other):
     streams, groups = mine.shape[:2]
     any_spec = pl.BlockSpec(memory_space=pl.ANY)
-    back = pl.pallas_call(
+    return pl.pallas_call(
         functools.partial(collect_kernel, groups),
         out_shape=jax.ShapeDtypeStruct(other.shape, jnp.bfloat16),
         in_specs=[pl.BlockSpec(memory_space=pltpu.VMEM), any_spec],
@@ -293,7 +257,6 @@
         ],
         compiler_params=pltpu.CompilerParams(collective_id=1, has_side_effects=True),
     )(mine, other)
-    return [back[s] for s in range(streams)]
 
 
 def body(
@@ -328,7 +291,8 @@
     backward_in = jnp.where(section_index == section_count - 1, loss_cotangent, returning)
     direction = steering[0]
     unit_dir = direction / jnp.sqrt(jnp.sum(direction * direction) + 1e-06)
-    weights = (gate_weight[0], up_weight[0], down_weight[0])
+    both = [lax.all_gather(w[0], "ec", axis=0, tiled=False) for w in (gate_weight, up_weight, down_weight)]
+    slices = [tuple(w[k] for w in both) for k in range(2)]
 
     forward_layout = dispatch_layout(forward_route[0, :, 0], expert_count, capacity)
     forward_send = jnp.dot(forward_layout, forward_in, preferred_element_type=jnp.float32).astype(
@@ -353,17 +317,26 @@
 
     def reorder(saved):
         grouped = saved[0].reshape(group_count, 2, 2, capacity, local_hidden).transpose(2, 1, 0, 3, 4)
-        grouped = jnp.where(flip, grouped[:, ::-1], grouped)
-        return grouped.reshape(device_count * capacity, local_hidden)
-
-    forward_part = expert_forward(forward_rows.reshape(rows_shape), weights)
-    backward_part = expert_backward(
-        backward_rows.reshape(rows_shape), reorder(saved_gate), reorder(saved_up), weights
-    )
-    forward_back, backward_back = collect_from_holders(
-        forward_part.reshape(2, 2, group_count, capacity, feature_count),
-        backward_part.reshape(2, 2, group_count, capacity, feature_count),
-    )
+        mine = lax.all_to_all(grouped, "ec", split_axis=0, concat_axis=0, tiled=True)
+        mine = jnp.where(flip, mine[:, ::-1], mine)
+        return mine.reshape(2, device_count * capacity // 2, local_hidden)
+
+    gate_rows = reorder(saved_gate)
+    up_rows = reorder(saved_up)
+    half_rows = (device_count * capacity // 2, feature_count)
+    forward_rows = forward_rows.reshape(half_rows)
+    backward_rows = backward_rows.reshape(half_rows)
+    forward_pair = sum(
+        expert_forward(forward_rows, slices[k]).astype(jnp.float32) for k in range(2)
+    )
+    backward_pair = sum(
+        expert_backward(backward_rows, gate_rows[k], up_rows[k], slices[k]).astype(jnp.float32)
+        for k in range(2)
+    )
+    pairs = jnp.stack([forward_pair, backward_pair]).reshape(
+        2, 2, group_count, capacity, feature_count
+    )
+    forward_back, backward_back = collect_from_holders(pairs[:, 0], pairs[:, 1].astype(jnp.bfloat16))
     forward_back = forward_back.reshape(expert_count * capacity, feature_count)
     backward_back = backward_back.reshape(expert_count * capacity, feature_count)
 

time: 357 us -> 366 us (1.025)
  matrix products: 28.7 us -> 45.9 us
  blocking collectives: 18.2 us -> 4.29 us
  between operations: 1.69 us -> 14.9 us
  other arithmetic: 14.7 us -> 9.44 us
  local copies, waits for them, and re-layouts: 9.16 us -> 4.21 us
    all_to_all x2 -> x1, blocking collectives: 18.2 us -> 4.29 us  [reorder(): lax.all_to_all(grouped, 'ec', split_axis=0, concat_axis=0, tiled=True)]
    dot_general x1 -> x2, matrix products: 11.5 us -> 17 us  [expert_forward(): jnp.dot(hidden, down_rows, preferred_element_type=jnp.float32)]
    dot_general x1 -> x2, matrix products: 1.61 us -> 6.97 us  [expert_backward(): lax.dot_general(slot_rows, down_rows, contract, preferred_element_type=jn...]
    another operation x2 -> x0, other arithmetic: 4.58 us -> none  [the longest x1 2.81 us: collect_from_holders(): mine = jnp.stack(mine)]
    dot_general x1 -> x2, matrix products: 1.72 us -> 6.29 us  [expert_backward(): lax.dot_general(grad_up, up_cols, contract, preferred_element_type=jnp.fl...]
  transfers between devices with their start and end apart: 2 -> 6, of which waited for: 1 -> 1; matrix products, arithmetic and copies ran while one was open for 3% -> 6% of each run, Pallas kernels for 0% -> 33%
where the time goes in v8:
time: 366 us; the launch traced here: 360 us
  Pallas kernels  215 us (59%)
  waiting for transfers between devices  51.7 us (14%)
  matrix products  45.9 us (13%)
  between operations  14.9 us (4%)
  starting transfers between devices  14.8 us (4%)
  other arithmetic  9.44 us (3%)
  blocking collectives  4.29 us (1%)
  local copies, waits for them, and re-layouts  4.21 us (1%)
    pallas_call x1, Pallas kernels, spread_to_holders(): pl.pallas_call(functools.partial(spread_kernel, groups), out_shape=[rows]...  119 us
    pallas_call x1, Pallas kernels, collect_from_holders(): pl.pallas_call(functools.partial(collect_kernel, groups), out_shape=jax.S...  95.1 us
    ppermute x2, waiting for transfers between devices, shifted(): return lax.ppermute(value, axis, pairs)  50.3 us
    dot_general x2, matrix products, expert_forward(): jnp.dot(hidden, down_rows, preferred_element_type=jnp.float32)  17 us
    ppermute x2, starting transfers between devices, shifted(): return lax.ppermute(value, axis, pairs)  11.2 us
  transfers between devices with their start and end apart: 6, of which 1 were waited for; matrix products, arithmetic and copies ran while one was open for 6% of the time, Pallas kernels for 33%

profile of v8, /device:TPU:24, one launch (start us, length us, event | category | flops | bytes accessed | tf_op | source)
XLA Modules:
  0.0 359.8 jit_solution(18051815025052346590)
XLA Ops:
  7.2 0.7 all-gather.8.cloned.1.call-update
  8.0 0.7 all-gather.4.cloned.1.call-update
  8.7 0.8 copy.23
  9.5 3.5 all-to-all-start.1
  13.0 9.1 %collective-permute-start = (bf16[1,128,3584]{2,1,0:T(8,128)(2,1)}, bf16[1,128,3584]{2,1,0:T(8,128)(2,1)S(1)}, u32[]{:S(2)}, u32[]{:S(2)}) collective-permute-start(bf16[1,128,3584]{2,1,0:T(8,128)(2,1)} %param.15), channel_id=1, source_target_pairs={{0,32},{32,64},{64,96},{96,128},{128,160},{160,192},{192,224},{1,3... | collective-permute-start | bytes 2752520 | tf_op jit(solution)/shard_map/ppermute | solution.py:22
  22.1 2.1 collective-permute-start.1
  25.2 0.6 multiply_reduce_fusion.1
  26.6 4.3 %all_to_all.10 = bf16[2,2,8,24,256]{4,3,2,1,0:T(8,128)(2,1)S(1)} all-to-all(bf16[2,2,8,24,256]{4,3,2,1,0:T(8,128)(2,1)S(1)} %bitcast.109), channel_id=1, replica_groups=mesh['section'=8,'ex'=4,'em'=2,'ep'=2,'ec'=2] {'ec'}, dimensions={0} | all-to-all | bytes 786432 | tf_op jit(solution)/shard_map/all_to_all | solution.py:320
  31.1 0.8 fusion.85
  31.9 50.3 %collective-permute-done.1 = bf16[1,128,3584]{2,1,0:T(8,128)(2,1)} collective-permute-done((bf16[1,128,3584]{2,1,0:T(8,128)(2,1)}, bf16[1,128,3584]{2,1,0:T(8,128)(2,1)}, u32[]{:S(2)}, u32[]{:S(2)}) %collective-permute-start.1) | collective-permute-done | bytes 917536 | tf_op jit(solution)/shard_map/ppermute | solution.py:22
  82.2 1.6 fusion.14
  83.8 1.8 convolution_convert_fusion.2
  85.6 1.7 convolution_convert_fusion.3
  87.3 119.5 %shard_map.157 = (bf16[2,8,24,3584]{3,2,1,0:T(8,128)(2,1)}, bf16[2,8,24,3584]{3,2,1,0:T(8,128)(2,1)}) custom-call(bf16[8,24,3584]{2,1,0:T(8,128)(2,1)} %bitcast.104, bf16[8,24,3584]{2,1,0:T(8,128)(2,1)} %bitcast.102), custom_call_target="tpu_custom_call" | custom-call | tf_op jit(solution)/shard_map/pallas_call | solution.py:152
  206.8 4.1 %fusion.24 = f32[384,256]{1,0:T(8,128)} fusion(bf16[384,3584]{1,0:T(8,128)(2,1)} %bitcast.121, bf16[2,256,3584]{2,1,0:T(8,128)(2,1)} %all-gather.8.cloned.1.call-done), kind=kOutput, calls=%fused_computation.45 | convolution fusion | flops 704643072 | bytes 4980736 | tf_op jit(solution)/shard_map/dot_general | solution.py:48
  211.0 2.8 fusion.20
  213.9 3.3 fusion.22
  217.1 1.6 fusion.18
  218.7 7.7 %fusion.4 = f32[384,3584]{1,0:T(8,128)} fusion(bf16[2,256,3584]{2,1,0:T(8,128)(2,1)} %all-gather.8.cloned.1.call-done, bf16[384,3584]{1,0:T(8,128)(2,1)S(1)} %bitcast.99, bf16[2,3584,256]{2,1,0:T(8,128)(2,1)} %all-gather.6.cloned.1.call-done, f32[384,256]{1,0:T(8,128)} %fusion.22), kind=kOutput, calls=%fused_computation.10 | convolution fusion | flops 1412628480 | bytes 12320768 | tf_op jit(solution)/shard_map/dot_general | solution.py:42
  226.4 2.7 fusion.17
  229.2 3.3 fusion.7
  232.5 9.3 %fusion.3 = f32[384,3584]{1,0:T(8,128)} fusion(f32[384,3584]{1,0:T(8,128)} %fusion.4, bf16[2,256,3584]{2,1,0:T(8,128)(2,1)} %all-gather.8.cloned.1.call-done, bf16[384,3584]{1,0:T(8,128)(2,1)S(1)} %bitcast.100, bf16[2,3584,256]{2,1,0:T(8,128)(2,1)} %all-gather.6.cloned.1.call-done, f32[384,256]{1,0:T(8,128)} %fusion.18), kind=kOutput, calls=%fused_computation.9 | convolution fusion | flops 1414004736 | bytes 17825792 | tf_op jit(solution)/shard_map/dot_general | solution.py:42
  241.8 2.6 fusion.21
  244.5 0.5 copy-done
  244.9 3.0 fusion.6
  247.9 2.1 fusion.13.other
  250.0 2.7 fusion.9.mine
  252.8 95.1 %shard_map.158 = bf16[2,8,24,3584]{3,2,1,0:T(8,128)(2,1)} custom-call(f32[2,8,24,3584]{3,2,1,0:T(8,128)} %fusion.9.mine, bf16[2,8,24,3584]{3,2,1,0:T(8,128)(2,1)} %fusion.13.other), custom_call_target="tpu_custom_call" | custom-call | tf_op jit(solution)/shard_map/pallas_call | solution.py:245
  347.9 2.0 fusion.84
  349.9 1.4 fusion.12
  351.3 0.6 multiply_reduce_fusion
  351.9 1.4 fusion.29
  (75 shorter events, 1.4 us)
Async XLA Ops:
  7.2 1.5 copy-start.13
  7.2 199.6 %all-gather.8.cloned.1.call-start = ((), (), s32[]{:S(2)}) async-start(), calls=%async_computation.4 | async-start | bytes 5505024 | tf_op jit(solution)/shard_map/all_gather | solution.py:294
  7.9 16.3 %copy-start.16 = (s32[1,128,1]{1,2,0:T(1,128)S(1)}, s32[1,128,1]{1,2,0:T(1,128)}, u32[]{:S(2)}) copy-start(s32[1,128,1]{1,2,0:T(1,128)} %param.16) | copy-start | bytes 1540
  7.9 16.8 %copy-start.17 = (s32[1,128,1]{1,2,0:T(1,128)S(1)}, s32[1,128,1]{1,2,0:T(1,128)}, u32[]{:S(2)}) copy-start(s32[1,128,1]{1,2,0:T(1,128)} %param.20) | copy-start | bytes 1540
  7.9 17.3 %copy-start.15 = (f32[1,3584]{1,0:T(1,128)S(1)}, f32[1,3584]{1,0:T(1,128)}, u32[]{:S(2)}) copy-start(f32[1,3584]{1,0:T(1,128)} %param.27) | copy-start | bytes 43012
  7.9 18.6 %copy-start.14 = (bf16[1,768,256]{2,1,0:T(8,128)(2,1)S(1)}, bf16[1,768,256]{2,1,0:T(8,128)(2,1)}, u32[]{:S(2)}) copy-start(bf16[1,768,256]{2,1,0:T(8,128)(2,1)} %param.23) | copy-start | bytes 1179652
  8.0 205.9 %all-gather.4.cloned.1.call-start = ((), (), s32[]{:S(2)}) async-start(), calls=%async_computation.2 | async-start | bytes 5505024 | tf_op jit(solution)/shard_map/all_gather | solution.py:294
  9.5 17.1 %all-to-all-start.1 = ((bf16[2,2,8,24,256]{4,3,2,1,0:T(8,128)(2,1)}), bf16[2,2,8,24,256]{4,3,2,1,0:T(8,128)(2,1)S(1)}, u32[]{:S(2)}, u32[]{:S(2)}) async-start(bf16[2,2,8,24,256]{4,3,2,1,0:T(8,128)(2,1)} %bitcast.89), calls=%async_computation.1 | async-start | bytes 786432 | tf_op jit(solution)/shard_map/all_to_all | solution.py:320
  13.0 205.8 %all-gather.6.cloned.1.call-start = ((), (), s32[]{:S(2)}) async-start(), calls=%async_computation.3 | async-start | bytes 5505024 | tf_op jit(solution)/shard_map/all_gather | solution.py:294
  13.0 72.6 %collective-permute-start = (bf16[1,128,3584]{2,1,0:T(8,128)(2,1)}, bf16[1,128,3584]{2,1,0:T(8,128)(2,1)S(1)}, u32[]{:S(2)}, u32[]{:S(2)}) collective-permute-start(bf16[1,128,3584]{2,1,0:T(8,128)(2,1)} %param.15), channel_id=1, source_target_pairs={{0,32},{32,64},{64,96},{96,128},{128,160},{160,192},{192,224},{1,3... | collective-permute-start | bytes 2752520 | tf_op jit(solution)/shard_map/ppermute | solution.py:22
  22.1 60.1 %collective-permute-start.1 = (bf16[1,128,3584]{2,1,0:T(8,128)(2,1)}, bf16[1,128,3584]{2,1,0:T(8,128)(2,1)}, u32[]{:S(2)}, u32[]{:S(2)}) collective-permute-start(bf16[1,128,3584]{2,1,0:T(8,128)(2,1)} %param.19), channel_id=1, source_target_pairs={{32,0},{64,32},{96,64},{128,96},{160,128},{192,160},{224,192},{33,... | collective-permute-start | bytes 2752520 | tf_op jit(solution)/shard_map/ppermute | solution.py:22
  24.7 60.9 %copy-start.18 = (s32[128]{0:T(128)}, s32[128]{0:T(128)S(1)}, u32[]{:S(2)}) copy-start(s32[128]{0:T(128)S(1)} %multiply_add_fusion.1) | copy-start | bytes 1540
  25.2 58.6 %copy-start.21 = (s32[128]{0:T(128)}, s32[128]{0:T(128)S(1)}, u32[]{:S(2)}) copy-start(s32[128]{0:T(128)S(1)} %multiply_add_fusion) | copy-start | bytes 1540
  30.9 52.9 %copy-start.23 = (f32[1,128]{1,0:T(1,128)S(1)}, f32[1,128]{1,0:T(1,128)}, u32[]{:S(2)}) copy-start(f32[1,128]{1,0:T(1,128)} %param.21) | copy-start | bytes 1540
  31.1 54.5 %copy-start.7 = (bf16[128,3584]{1,0:T(8,128)(2,1)S(1)}, bf16[128,3584]{1,0:T(8,128)(2,1)}, u32[]{:S(2)}) copy-start(bf16[128,3584]{1,0:T(8,128)(2,1)} %param.14) | copy-start | bytes 2752516
  83.8 3.5 copy-start.3
  85.6 121.2 %copy-start.9 = (bf16[1,128,3584]{2,1,0:T(8,128)(2,1)}, bf16[1,128,3584]{2,1,0:T(8,128)(2,1)S(1)}, u32[]{:S(2)}) copy-start(bf16[1,128,3584]{2,1,0:T(8,128)(2,1)S(1)} %collective-permute-done) | copy-start | bytes 2752516
  206.8 4.2 %copy-start.5 = (bf16[2,256,3584]{2,1,0:T(8,128)(2,1)S(1)}, bf16[2,256,3584]{2,1,0:T(8,128)(2,1)}, u32[]{:S(2)}) copy-start(bf16[2,256,3584]{2,1,0:T(8,128)(2,1)} %all-gather.8.cloned.1.call-done) | copy-start | bytes 11010052
  211.0 2.9 copy-start.2
  213.8 3.3 copy-start.6
  226.4 2.7 copy-start.1
  232.5 9.4 %copy-start.11 = (f32[384,256]{1,0:T(8,128)S(1)}, f32[384,256]{1,0:T(8,128)}, u32[]{:S(2)}) copy-start(f32[384,256]{1,0:T(8,128)} %fusion.24) | copy-start | bytes 1179652
  232.5 9.4 %copy-start.12 = (bf16[1,2,8,24,256]{4,3,2,1,0:T(8,128)(2,1)S(1)}, bf16[1,2,8,24,256]{4,3,2,1,0:T(8,128)(2,1)}, u32[]{:S(2)}) copy-start(bf16[1,2,8,24,256]{4,3,2,1,0:T(8,128)(2,1)} %get-tuple-element.11) | copy-start | bytes 589828
  241.8 3.1 copy-start
  241.8 6.1 %slice-start = ((s8[5505024]{0:T(1024)(128)(4,1)}), s8[4194304]{0:T(1024)(128)(4,1)S(1)}, s32[]{:S(2)}) async-start(s8[5505024]{0:T(1024)(128)(4,1)} %bitcast.91), calls=%async_computation.5 | async-start | bytes 8388608
  244.9 3.0 slice-start.1
  347.8 2.1 copy-start.4
  347.9 2.1 copy-start.22
  349.9 1.4 copy-start.19
  349.9 1.4 copy-start.24
  349.9 2.0 copy-start.8
  349.9 2.0 copy-start.10
  (1 other events, 1.4 us)
Sparse Core Ops, SparseCore 0:
  9.8 21.1 all-gather.7
  32.9 19.5 all-gather.3
  54.2 19.5 all-gather.5

commit v9 on v7

--- a/solution.py
+++ b/solution.py
@@ -38,7 +38,7 @@
     gate_cols, up_cols, down_rows = weights
     gate_pre = jnp.dot(slot_rows, gate_cols, preferred_element_type=jnp.float32)
     up_pre = jnp.dot(slot_rows, up_cols, preferred_element_type=jnp.float32)
-    hidden = (jax.nn.silu(gate_pre) * up_pre).astype(jnp.bfloat16)
+    hidden = lax.optimization_barrier((jax.nn.silu(gate_pre) * up_pre).astype(jnp.bfloat16))
     return jnp.dot(hidden, down_rows, preferred_element_type=jnp.float32).astype(jnp.bfloat16)
 
 
@@ -55,6 +55,7 @@
         grad_hidden * up_pre * sigmoid_gate * (1.0 + gate_pre * (1.0 - sigmoid_gate))
     ).astype(jnp.bfloat16)
     grad_up = (grad_hidden * gate_pre * sigmoid_gate).astype(jnp.bfloat16)
+    grad_gate, grad_up = lax.optimization_barrier((grad_gate, grad_up))
     grad_part = lax.dot_general(grad_gate, gate_cols, contract, preferred_element_type=jnp.float32)
     grad_part = grad_part + lax.dot_general(
         grad_up, up_cols, contract, preferred_element_type=jnp.float32

time: 337 us -> 327 us (0.970)
  matrix products: 34.2 us -> 23.8 us
    dot_general x1, matrix products: 11.6 us -> 3.98 us  [expert_forward(): jnp.dot(hidden, down_rows, preferred_element_type=jnp.float32)]
where the time goes in v9:
time: 327 us; the launch traced here: 323 us
  Pallas kernels  222 us (68%)
  waiting for transfers between devices  50.1 us (15%)
  matrix products  23.8 us (7%)
  starting transfers between devices  11.3 us (3%)
  other arithmetic  8.54 us (3%)
  local copies, waits for them, and re-layouts  4.91 us (2%)
    pallas_call x1, Pallas kernels, spread_to_holders(): pl.pallas_call(functools.partial(spread_kernel, groups), out_shape=[rows]...  121 us
    pallas_call x1, Pallas kernels, collect_from_holders(): pl.pallas_call(functools.partial(collect_kernel, groups), out_shape=jax.S...  101 us
    ppermute x2, waiting for transfers between devices, shifted(): return lax.ppermute(value, axis, pairs)  50.1 us
    ppermute x2, starting transfers between devices, shifted(): return lax.ppermute(value, axis, pairs)  11.3 us
  transfers between devices with their start and end apart: 2, of which 1 were waited for; matrix products, arithmetic and copies ran while one was open for 3% of the time, Pallas kernels for 0%

profile of v9, /device:TPU:24, one launch (start us, length us, event | category | flops | bytes accessed | tf_op | source)
XLA Modules:
  0.0 322.5 jit_solution(11232708726533300274)
XLA Ops:
  0.6 0.0 copy-start
  0.7 9.2 %collective-permute-start = (bf16[1,128,3584]{2,1,0:T(8,128)(2,1)}, bf16[1,128,3584]{2,1,0:T(8,128)(2,1)}, u32[]{:S(2)}, u32[]{:S(2)}) collective-permute-start(bf16[1,128,3584]{2,1,0:T(8,128)(2,1)} %param.15), channel_id=1, source_target_pairs={{0,32},{32,64},{64,96},{96,128},{128,160},{160,192},{192,224},{1,3... | collective-permute-start | bytes 2752520 | tf_op jit(solution)/shard_map/ppermute | solution.py:22
  9.9 2.1 collective-permute-start.1
  12.0 1.3 multiply_reduce_fusion.1
  14.1 0.7 fusion.36
  14.8 0.2 reduce_window_sum.17
  15.0 0.8 select_reduce_fusion.1
  15.8 0.7 fusion.35
  16.6 0.2 reduce_window_sum.18
  16.8 1.0 copy.21
  17.8 1.0 copy.22
  18.8 0.2 select_reduce_fusion
  19.0 0.0 copy-start.11
  19.1 0.1 reverse_select_fusion
  19.3 50.1 %collective-permute-done.1 = bf16[1,128,3584]{2,1,0:T(8,128)(2,1)} collective-permute-done((bf16[1,128,3584]{2,1,0:T(8,128)(2,1)}, bf16[1,128,3584]{2,1,0:T(8,128)(2,1)}, u32[]{:S(2)}, u32[]{:S(2)}) %collective-permute-start.1) | collective-permute-done | bytes 917536 | tf_op jit(solution)/shard_map/ppermute | solution.py:22
  69.4 1.6 fusion.2
  71.0 1.8 convolution_convert_fusion.1
  72.8 2.8 convolution_convert_fusion.2
  75.6 121.1 %shard_map.157 = (bf16[2,2,8,24,3584]{4,3,2,1,0:T(8,128)(2,1)}, bf16[2,2,8,24,3584]{4,3,2,1,0:T(8,128)(2,1)}) custom-call(bf16[8,24,3584]{2,1,0:T(8,128)(2,1)} %bitcast.76, bf16[8,24,3584]{2,1,0:T(8,128)(2,1)} %bitcast.74), custom_call_target="tpu_custom_call" | custom-call | tf_op jit(solution)/shard_map/pallas_call | solution.py:179
  196.7 4.5 %fusion.33 = (bf16[768,256]{1,0:T(8,128)(2,1)S(1)}, bf16[768,256]{1,0:T(8,128)(2,1)S(1)}) fusion(bf16[2,2,8,24,256]{4,3,2,1,0:T(8,128)(2,1)S(1)} %get-tuple-element.19, bf16[2,2,8,24,256]{4,3,2,1,0:T(8,128)(2,1)S(1)} %get-tuple-element.20, bf16[768,3584]{1,0:T(8,128)(2,1)} %bitcast.90, bf16[1,256,3584]{2,1,0:T(8,128)(2,1)S(1)} %copy-done), kind=kOutput, calls=%fused_computation.43 | convolution fusion | flops 1412235264 | bytes 8912896 | tf_op jit(solution)/shard_map/dot_general | solution.py:48
  201.2 0.2 copy-done.15
  201.5 1.6 fusion.13
  203.1 1.6 fusion.18
  204.7 4.0 %convolution_convert_fusion = bf16[768,3584]{1,0:T(8,128)(2,1)} fusion(bf16[768,256]{1,0:T(8,128)(2,1)S(1)} %fusion.18, bf16[1,256,3584]{2,1,0:T(8,128)(2,1)S(1)} %copy-done), kind=kOutput, calls=%fused_computation.1 | convolution fusion | flops 1412038656 | bytes 7733248 | tf_op jit(solution)/shard_map/dot_general | solution.py:42
  208.7 1.6 fusion.11
  210.3 4.1 %add_convert_fusion = bf16[768,3584]{1,0:T(8,128)(2,1)} fusion(f32[768,3584]{1,0:T(8,128)S(1)} %fusion.11, bf16[768,256]{1,0:T(8,128)(2,1)S(1)} %get-tuple-element.10, bf16[1,3584,256]{2,1,0:T(8,128)(2,1)S(1)} %copy-done.3), kind=kOutput, calls=%fused_computation | convolution fusion | flops 1414791168 | bytes 18743296 | tf_op jit(solution)/shard_map/dot_general | solution.py:60
  214.4 101.0 %shard_map.158 = bf16[2,8,24,3584]{3,2,1,0:T(8,128)(2,1)} custom-call(bf16[2,2,8,24,3584]{4,3,2,1,0:T(8,128)(2,1)} %bitcast.71, bf16[2,2,8,24,3584]{4,3,2,1,0:T(8,128)(2,1)} %bitcast.72), custom_call_target="tpu_custom_call" | custom-call | tf_op jit(solution)/shard_map/pallas_call | solution.py:305
  315.4 1.9 fusion.41
  317.4 1.4 fusion.1
  318.8 0.5 multiply_reduce_fusion
  319.3 0.6 copy-done.2
  319.9 2.6 fusion.21
  (32 shorter events, 0.1 us)
Async XLA Ops:
  0.6 196.1 %copy-start = (bf16[1,256,3584]{2,1,0:T(8,128)(2,1)S(1)}, bf16[1,256,3584]{2,1,0:T(8,128)(2,1)}, u32[]{:S(2)}) copy-start(bf16[1,256,3584]{2,1,0:T(8,128)(2,1)} %param.26) | copy-start | bytes 5505028
  0.6 18.4 %copy-start.5 = (f32[1,3584]{1,0:T(1,128)S(1)}, f32[1,3584]{1,0:T(1,128)}, u32[]{:S(2)}) copy-start(f32[1,3584]{1,0:T(1,128)} %param.27) | copy-start | bytes 43012
  0.7 18.3 %copy-start.6 = (s32[1,128,1]{1,2,0:T(1,128)S(1)}, s32[1,128,1]{1,2,0:T(1,128)}, u32[]{:S(2)}) copy-start(s32[1,128,1]{1,2,0:T(1,128)} %param.16) | copy-start | bytes 1540
  0.7 18.1 %copy-start.7 = (s32[1,128,1]{1,2,0:T(1,128)S(1)}, s32[1,128,1]{1,2,0:T(1,128)}, u32[]{:S(2)}) copy-start(s32[1,128,1]{1,2,0:T(1,128)} %param.20) | copy-start | bytes 1540
  0.7 72.1 %collective-permute-start = (bf16[1,128,3584]{2,1,0:T(8,128)(2,1)}, bf16[1,128,3584]{2,1,0:T(8,128)(2,1)}, u32[]{:S(2)}, u32[]{:S(2)}) collective-permute-start(bf16[1,128,3584]{2,1,0:T(8,128)(2,1)} %param.15), channel_id=1, source_target_pairs={{0,32},{32,64},{64,96},{96,128},{128,160},{160,192},{192,224},{1,3... | collective-permute-start | bytes 2752520 | tf_op jit(solution)/shard_map/ppermute | solution.py:22
  9.9 59.5 %collective-permute-start.1 = (bf16[1,128,3584]{2,1,0:T(8,128)(2,1)}, bf16[1,128,3584]{2,1,0:T(8,128)(2,1)}, u32[]{:S(2)}, u32[]{:S(2)}) collective-permute-start(bf16[1,128,3584]{2,1,0:T(8,128)(2,1)} %param.19), channel_id=1, source_target_pairs={{32,0},{64,32},{96,64},{128,96},{160,128},{192,160},{224,192},{33,... | collective-permute-start | bytes 2752520 | tf_op jit(solution)/shard_map/ppermute | solution.py:22
  19.0 53.8 %copy-start.8 = (s32[128]{0:T(128)}, s32[128]{0:T(128)S(1)}, u32[]{:S(2)}) copy-start(s32[128]{0:T(128)S(1)} %multiply_add_fusion.1) | copy-start | bytes 1540
  19.0 52.0 %copy-start.11 = (s32[128]{0:T(128)}, s32[128]{0:T(128)S(1)}, u32[]{:S(2)}) copy-start(s32[128]{0:T(128)S(1)} %multiply_add_fusion) | copy-start | bytes 1540
  19.1 51.9 %copy-start.13 = (f32[1,128]{1,0:T(1,128)S(1)}, f32[1,128]{1,0:T(1,128)}, u32[]{:S(2)}) copy-start(f32[1,128]{1,0:T(1,128)} %param.21) | copy-start | bytes 1540
  71.0 1.8 copy-start.1
  196.7 4.5 %copy-start.4 = (bf16[1,3584,256]{2,1,0:T(8,128)(2,1)S(1)}, bf16[1,3584,256]{2,1,0:T(8,128)(2,1)}, u32[]{:S(2)}) copy-start(bf16[1,3584,256]{2,1,0:T(8,128)(2,1)} %param.24) | copy-start | bytes 5505028
  196.7 4.7 %copy-start.15 = (bf16[2,2,8,24,3584]{4,3,2,1,0:T(8,128)(2,1)S(1)}, bf16[2,2,8,24,3584]{4,3,2,1,0:T(8,128)(2,1)}, u32[]{:S(2)}) copy-start(bf16[2,2,8,24,3584]{4,3,2,1,0:T(8,128)(2,1)} %get-tuple-element.7) | copy-start | bytes 16515076
  201.5 1.6 copy-start.3
  315.4 2.0 copy-start.12
  317.3 1.4 copy-start.9
  317.4 1.4 copy-start.14
  318.8 1.2 copy-start.2
  319.3 3.2 copy-start.10

commit v10 on v9

--- a/solution.py
+++ b/solution.py
@@ -20,6 +20,35 @@
     devices = lax.axis_size(axis)
     pairs = [(i, i + by) for i in range(devices) if 0 <= i + by < devices]
     return lax.ppermute(value, axis, pairs)
+
+
+def section_shift(value, by):
+    axes = ("section",) + EXPERT_AXES
+    sections = lax.axis_size("section")
+    experts = lax.axis_size(EXPERT_AXES)
+    ring = 8
+    first = {2: [], -2: []}
+    second = {2: [], -2: []}
+    for s in range(sections):
+        t = s + by
+        if not 0 <= t < sections:
+            continue
+        y, high = divmod(s, 2)
+        for e in range(experts):
+            x, rest = divmod(e, 8)
+            low, core = divmod(rest, 2)
+            z = high * 4 + low
+            for dz in (2, -2):
+                hop = (z + dz) % ring
+                middle = (y * 2 + hop // 4) * experts + (x * 4 + hop % 4) * 2 + core
+                first[dz].append((s * experts + e, middle))
+                second[dz].append((middle, t * experts + e))
+    half = value.shape[1] // 2
+    up = lax.ppermute(value[:, :half], axes, first[2])
+    down = lax.ppermute(value[:, half:], axes, first[-2])
+    up = lax.ppermute(up, axes, second[2])
+    down = lax.ppermute(down, axes, second[-2])
+    return jnp.concatenate([up, down], axis=1)
 
 
 def dispatch_layout(expert_ids, expert_count, capacity):
@@ -352,9 +381,9 @@
     capacity = saved_gate.shape[1] // device_count
     feature_count = embedded.shape[1]
     rows_shape = (device_count * capacity, feature_count)
-    arriving = shifted(forward_held, "section", 1)[0]
+    arriving = section_shift(forward_held, 1)[0]
     forward_in = jnp.where(section_index == 0, embedded, arriving)
-    returning = shifted(backward_held, "section", -1)[0]
+    returning = section_shift(backward_held, -1)[0]
     backward_in = jnp.where(section_index == section_count - 1, loss_cotangent, returning)
     direction = steering[0]
     unit_dir = direction / jnp.sqrt(jnp.sum(direction * direction) + 1e-06)

time: 327 us -> 328 us (level); the launches traced: 323 us -> 327 us
  starting transfers between devices: 11.3 us -> 42.3 us
  Pallas kernels: 222 us -> 204 us
  waiting for transfers between devices: 50.1 us -> 41.8 us
    ppermute x2 -> x8, starting transfers between devices: 11.3 us -> 42.3 us  [the longest x2 15.9 us: section_shift(): up = lax.ppermute(up, axes, second[2])]
    pallas_call x1, Pallas kernels: 121 us -> 104 us  [spread_to_holders(): pl.pallas_call(functools.partial(spread_kernel, groups), out_shape=[rows]...]
    ppermute x2 -> x8, waiting for transfers between devices: 50.1 us -> 41.8 us  [the longest x2 16.8 us: section_shift(): up = lax.ppermute(up, axes, second[2])]
  transfers between devices with their start and end apart: 2 -> 8, of which waited for: 1 -> 5; matrix products, arithmetic and copies ran while one was open for 3% -> 3% of each run, Pallas kernels for 0% -> 0%
where the time goes in v10:
time: 328 us; the launch traced here: 327 us
  Pallas kernels  204 us (62%)
  starting transfers between devices  42.3 us (13%)
  waiting for transfers between devices  41.8 us (13%)
  matrix products  22.8 us (7%)
  other arithmetic  8.4 us (3%)
  local copies, waits for them, and re-layouts  6.45 us (2%)
    pallas_call x1, Pallas kernels, spread_to_holders(): pl.pallas_call(functools.partial(spread_kernel, groups), out_shape=[rows]...  104 us
    pallas_call x1, Pallas kernels, collect_from_holders(): pl.pallas_call(functools.partial(collect_kernel, groups), out_shape=jax.S...  99.9 us
    ppermute x2, waiting for transfers between devices, section_shift(): up = lax.ppermute(up, axes, second[2])  16.8 us
    ppermute x2, starting transfers between devices, section_shift(): up = lax.ppermute(up, axes, second[2])  15.9 us
    ppermute x2, waiting for transfers between devices, section_shift(): down = lax.ppermute(down, axes, second[-2])  13.9 us
    ppermute x2, waiting for transfers between devices, section_shift(): up = lax.ppermute(value[:, :half], axes, first[2])  11 us
    ppermute x2, starting transfers between devices, section_shift(): up = lax.ppermute(value[:, :half], axes, first[2])  9.95 us
    ppermute x2, starting transfers between devices, section_shift(): down = lax.ppermute(down, axes, second[-2])  8.81 us
  transfers between devices with their start and end apart: 8, of which 5 were waited for; matrix products, arithmetic and copies ran while one was open for 3% of the time, Pallas kernels for 0%

profile of v10, /device:TPU:24, one launch (start us, length us, event | category | flops | bytes accessed | tf_op | source)
XLA Modules:
  0.0 327.1 jit_solution(6726491030916018494)
XLA Ops:
  0.7 1.4 fusion.48
  2.1 6.0 %collective-permute-start = (bf16[1,64,3584]{2,1,0:T(8,128)(2,1)S(1)}, bf16[1,64,3584]{2,1,0:T(8,128)(2,1)}, u32[]{:S(2)}, u32[]{:S(2)}) collective-permute-start(bf16[1,64,3584]{2,1,0:T(8,128)(2,1)S(1)} %get-tuple-element.19), channel_id=1, source_target_pairs={{0,4},{1,5},{2,6},{3,7},{4,32},{5,33},{6,34},{7,35},{8,12},{9,13},... | collective-permute-start | bytes 1376264 | tf_op jit(solution)/shard_map/ppermute | solution.py:47
  8.0 3.7 %collective-permute-start.2 = (bf16[1,64,3584]{2,1,0:T(8,128)(2,1)S(1)}, bf16[1,64,3584]{2,1,0:T(8,128)(2,1)}, u32[]{:S(2)}, u32[]{:S(2)}) collective-permute-start(bf16[1,64,3584]{2,1,0:T(8,128)(2,1)S(1)} %get-tuple-element.20), channel_id=1, source_target_pairs={{0,36},{1,37},{2,38},{3,39},{4,0},{5,1},{6,2},{7,3},{8,44},{9,45},... | collective-permute-start | bytes 1376264 | tf_op jit(solution)/shard_map/ppermute | solution.py:48
  11.7 1.0 fusion.47
  12.7 4.0 %collective-permute-start.4 = (bf16[1,64,3584]{2,1,0:T(8,128)(2,1)}, bf16[1,64,3584]{2,1,0:T(8,128)(2,1)}, u32[]{:S(2)}, u32[]{:S(2)}) collective-permute-start(bf16[1,64,3584]{2,1,0:T(8,128)(2,1)} %get-tuple-element.17), channel_id=1, source_target_pairs={{32,36},{33,37},{34,38},{35,39},{36,0},{37,1},{38,2},{39,3},{40,44... | collective-permute-start | bytes 1376264 | tf_op jit(solution)/shard_map/ppermute | solution.py:47
  16.7 4.0 %collective-permute-start.6 = (bf16[1,64,3584]{2,1,0:T(8,128)(2,1)}, bf16[1,64,3584]{2,1,0:T(8,128)(2,1)}, u32[]{:S(2)}, u32[]{:S(2)}) collective-permute-start(bf16[1,64,3584]{2,1,0:T(8,128)(2,1)} %get-tuple-element.18), channel_id=1, source_target_pairs={{32,4},{33,5},{34,6},{35,7},{36,32},{37,33},{38,34},{39,35},{40,12... | collective-permute-start | bytes 1376264 | tf_op jit(solution)/shard_map/ppermute | solution.py:48
  23.9 1.0 copy.22
  24.9 1.0 select_reduce_fusion
  25.9 0.8 divide_reduce_fusion
  27.4 11.0 %collective-permute-done.4 = bf16[1,64,3584]{2,1,0:T(8,128)(2,1)} collective-permute-done((bf16[1,64,3584]{2,1,0:T(8,128)(2,1)}, bf16[1,64,3584]{2,1,0:T(8,128)(2,1)}, u32[]{:S(2)}, u32[]{:S(2)}) %collective-permute-start.4) | collective-permute-done | bytes 458784 | tf_op jit(solution)/shard_map/ppermute | solution.py:47
  38.4 14.6 %collective-permute-start.5 = (bf16[1,64,3584]{2,1,0:T(8,128)(2,1)}, bf16[1,64,3584]{2,1,0:T(8,128)(2,1)S(1)}, u32[]{:S(2)}, u32[]{:S(2)}) collective-permute-start(bf16[1,64,3584]{2,1,0:T(8,128)(2,1)} %collective-permute-done.4), channel_id=1, source_target_pairs={{36,0},{37,1},{38,2},{39,3},{0,4},{1,5},{2,6},{3,7},{44,8},{45,9},... | collective-permute-start | bytes 1376264 | tf_op jit(solution)/shard_map/ppermute | solution.py:49
  53.0 5.2 %collective-permute-start.7 = (bf16[1,64,3584]{2,1,0:T(8,128)(2,1)}, bf16[1,64,3584]{2,1,0:T(8,128)(2,1)S(1)}, u32[]{:S(2)}, u32[]{:S(2)}) collective-permute-start(bf16[1,64,3584]{2,1,0:T(8,128)(2,1)} %collective-permute-done.6), channel_id=1, source_target_pairs={{4,0},{5,1},{6,2},{7,3},{32,4},{33,5},{34,6},{35,7},{12,8},{13,9},... | collective-permute-start | bytes 1376264 | tf_op jit(solution)/shard_map/ppermute | solution.py:50
  58.9 1.0 reverse_select_fusion
  60.0 1.3 collective-permute-start.1
  61.3 3.6 %collective-permute-start.3 = (bf16[1,64,3584]{2,1,0:T(8,128)(2,1)}, bf16[1,64,3584]{2,1,0:T(8,128)(2,1)S(1)}, u32[]{:S(2)}, u32[]{:S(2)}) collective-permute-start(bf16[1,64,3584]{2,1,0:T(8,128)(2,1)} %collective-permute-done.2), channel_id=1, source_target_pairs={{36,32},{37,33},{38,34},{39,35},{0,36},{1,37},{2,38},{3,39},{44,40... | collective-permute-start | bytes 1376264 | tf_op jit(solution)/shard_map/ppermute | solution.py:50
  64.8 7.2 %collective-permute-done.5 = bf16[1,64,3584]{2,1,0:T(8,128)(2,1)S(1)} collective-permute-done((bf16[1,64,3584]{2,1,0:T(8,128)(2,1)}, bf16[1,64,3584]{2,1,0:T(8,128)(2,1)S(1)}, u32[]{:S(2)}, u32[]{:S(2)}) %collective-permute-start.5) | collective-permute-done | bytes 458784 | tf_op jit(solution)/shard_map/ppermute | solution.py:49
  72.1 5.9 %collective-permute-done.7 = bf16[1,64,3584]{2,1,0:T(8,128)(2,1)S(1)} collective-permute-done((bf16[1,64,3584]{2,1,0:T(8,128)(2,1)}, bf16[1,64,3584]{2,1,0:T(8,128)(2,1)S(1)}, u32[]{:S(2)}, u32[]{:S(2)}) %collective-permute-start.7) | collective-permute-done | bytes 458784 | tf_op jit(solution)/shard_map/ppermute | solution.py:50
  78.5 1.7 convolution_convert_fusion.1
  80.2 9.6 %collective-permute-done.1 = bf16[1,64,3584]{2,1,0:T(8,128)(2,1)S(1)} collective-permute-done((bf16[1,64,3584]{2,1,0:T(8,128)(2,1)}, bf16[1,64,3584]{2,1,0:T(8,128)(2,1)S(1)}, u32[]{:S(2)}, u32[]{:S(2)}) %collective-permute-start.1) | collective-permute-done | bytes 458784 | tf_op jit(solution)/shard_map/ppermute | solution.py:49
  89.8 8.0 %collective-permute-done.3 = bf16[1,64,3584]{2,1,0:T(8,128)(2,1)S(1)} collective-permute-done((bf16[1,64,3584]{2,1,0:T(8,128)(2,1)}, bf16[1,64,3584]{2,1,0:T(8,128)(2,1)S(1)}, u32[]{:S(2)}, u32[]{:S(2)}) %collective-permute-start.3) | collective-permute-done | bytes 458784 | tf_op jit(solution)/shard_map/ppermute | solution.py:50
  97.8 1.7 convolution_convert_fusion.2
  99.5 103.7 %shard_map.157 = (bf16[2,2,8,24,3584]{4,3,2,1,0:T(8,128)(2,1)}, bf16[2,2,8,24,3584]{4,3,2,1,0:T(8,128)(2,1)}) custom-call(bf16[8,24,3584]{2,1,0:T(8,128)(2,1)} %bitcast.80, bf16[8,24,3584]{2,1,0:T(8,128)(2,1)} %bitcast.78), custom_call_target="tpu_custom_call" | custom-call | tf_op jit(solution)/shard_map/pallas_call | solution.py:208
  203.2 4.6 %fusion.35 = (bf16[768,256]{1,0:T(8,128)(2,1)S(1)}, bf16[768,256]{1,0:T(8,128)(2,1)S(1)}) fusion(bf16[2,2,8,24,256]{4,3,2,1,0:T(8,128)(2,1)} %get-tuple-element.23, bf16[2,2,8,24,256]{4,3,2,1,0:T(8,128)(2,1)} %get-tuple-element.24, bf16[768,3584]{1,0:T(8,128)(2,1)} %bitcast.94, bf16[1,256,3584]{2,1,0:T(8,128)(2,1)S(1)} %copy-done), kind=kOutput, calls=%fused_computation.45 | convolution fusion | flops 1412235264 | bytes 8912896 | tf_op jit(solution)/shard_map/dot_general | solution.py:77
  208.1 1.6 fusion.13
  209.7 1.6 fusion.18
  211.3 4.0 %convolution_convert_fusion = bf16[768,3584]{1,0:T(8,128)(2,1)} fusion(bf16[768,256]{1,0:T(8,128)(2,1)S(1)} %fusion.18, bf16[1,256,3584]{2,1,0:T(8,128)(2,1)S(1)} %copy-done), kind=kOutput, calls=%fused_computation.1 | convolution fusion | flops 1412038656 | bytes 7733248 | tf_op jit(solution)/shard_map/dot_general | solution.py:71
  215.3 1.6 fusion.11
  217.0 4.1 %add_convert_fusion = bf16[768,3584]{1,0:T(8,128)(2,1)} fusion(f32[768,3584]{1,0:T(8,128)S(1)} %fusion.11, bf16[768,256]{1,0:T(8,128)(2,1)S(1)} %get-tuple-element.10, bf16[1,3584,256]{2,1,0:T(8,128)(2,1)S(1)} %copy-done.3), kind=kOutput, calls=%fused_computation | convolution fusion | flops 1414791168 | bytes 18743296 | tf_op jit(solution)/shard_map/dot_general | solution.py:89
  221.1 99.9 %shard_map.158 = bf16[2,8,24,3584]{3,2,1,0:T(8,128)(2,1)} custom-call(bf16[2,2,8,24,3584]{4,3,2,1,0:T(8,128)(2,1)} %bitcast.75, bf16[2,2,8,24,3584]{4,3,2,1,0:T(8,128)(2,1)} %bitcast.76), custom_call_target="tpu_custom_call" | custom-call | tf_op jit(solution)/shard_map/pallas_call | solution.py:334
  321.0 1.9 fusion.46
  323.0 1.4 fusion.1
  325.7 1.4 fusion.21
  (54 shorter events, 5.9 us)
Async XLA Ops:
  0.6 202.5 %copy-start = (bf16[1,256,3584]{2,1,0:T(8,128)(2,1)S(1)}, bf16[1,256,3584]{2,1,0:T(8,128)(2,1)}, u32[]{:S(2)}) copy-start(bf16[1,256,3584]{2,1,0:T(8,128)(2,1)} %param.26) | copy-start | bytes 5505028
  0.6 11.1 %copy-start.7 = (bf16[1,128,3584]{2,1,0:T(8,128)(2,1)S(1)}, bf16[1,128,3584]{2,1,0:T(8,128)(2,1)}, u32[]{:S(2)}) copy-start(bf16[1,128,3584]{2,1,0:T(8,128)(2,1)} %param.19) | copy-start | bytes 2752516
  0.7 20.0 %copy-start.9 = (f32[1,3584]{1,0:T(1,128)S(1)}, f32[1,3584]{1,0:T(1,128)}, u32[]{:S(2)}) copy-start(f32[1,3584]{1,0:T(1,128)} %param.27) | copy-start | bytes 43012
  0.7 21.4 %copy-start.10 = (s32[1,128,1]{1,2,0:T(1,128)S(1)}, s32[1,128,1]{1,2,0:T(1,128)}, u32[]{:S(2)}) copy-start(s32[1,128,1]{1,2,0:T(1,128)} %param.16) | copy-start | bytes 1540
  0.7 22.3 %copy-start.11 = (s32[1,128,1]{1,2,0:T(1,128)S(1)}, s32[1,128,1]{1,2,0:T(1,128)}, u32[]{:S(2)}) copy-start(s32[1,128,1]{1,2,0:T(1,128)} %param.20) | copy-start | bytes 1540
  0.7 23.2 %copy-start.8 = (bf16[1,768,256]{2,1,0:T(8,128)(2,1)S(1)}, bf16[1,768,256]{2,1,0:T(8,128)(2,1)}, u32[]{:S(2)}) copy-start(bf16[1,768,256]{2,1,0:T(8,128)(2,1)} %param.22) | copy-start | bytes 1179652
  2.1 57.9 %collective-permute-start = (bf16[1,64,3584]{2,1,0:T(8,128)(2,1)S(1)}, bf16[1,64,3584]{2,1,0:T(8,128)(2,1)}, u32[]{:S(2)}, u32[]{:S(2)}) collective-permute-start(bf16[1,64,3584]{2,1,0:T(8,128)(2,1)S(1)} %get-tuple-element.19), channel_id=1, source_target_pairs={{0,4},{1,5},{2,6},{3,7},{4,32},{5,33},{6,34},{7,35},{8,12},{9,13},... | collective-permute-start | bytes 1376264 | tf_op jit(solution)/shard_map/ppermute | solution.py:47
  8.0 53.2 %collective-permute-start.2 = (bf16[1,64,3584]{2,1,0:T(8,128)(2,1)S(1)}, bf16[1,64,3584]{2,1,0:T(8,128)(2,1)}, u32[]{:S(2)}, u32[]{:S(2)}) collective-permute-start(bf16[1,64,3584]{2,1,0:T(8,128)(2,1)S(1)} %get-tuple-element.20), channel_id=1, source_target_pairs={{0,36},{1,37},{2,38},{3,39},{4,0},{5,1},{6,2},{7,3},{8,44},{9,45},... | collective-permute-start | bytes 1376264 | tf_op jit(solution)/shard_map/ppermute | solution.py:48
  12.7 25.7 %collective-permute-start.4 = (bf16[1,64,3584]{2,1,0:T(8,128)(2,1)}, bf16[1,64,3584]{2,1,0:T(8,128)(2,1)}, u32[]{:S(2)}, u32[]{:S(2)}) collective-permute-start(bf16[1,64,3584]{2,1,0:T(8,128)(2,1)} %get-tuple-element.17), channel_id=1, source_target_pairs={{32,36},{33,37},{34,38},{35,39},{36,0},{37,1},{38,2},{39,3},{40,44... | collective-permute-start | bytes 1376264 | tf_op jit(solution)/shard_map/ppermute | solution.py:47
  16.7 36.3 %collective-permute-start.6 = (bf16[1,64,3584]{2,1,0:T(8,128)(2,1)}, bf16[1,64,3584]{2,1,0:T(8,128)(2,1)}, u32[]{:S(2)}, u32[]{:S(2)}) collective-permute-start(bf16[1,64,3584]{2,1,0:T(8,128)(2,1)} %get-tuple-element.18), channel_id=1, source_target_pairs={{32,4},{33,5},{34,6},{35,7},{36,32},{37,33},{38,34},{39,35},{40,12... | collective-permute-start | bytes 1376264 | tf_op jit(solution)/shard_map/ppermute | solution.py:48
  27.4 70.4 %copy-start.12 = (s32[128]{0:T(128)}, s32[128]{0:T(128)S(1)}, u32[]{:S(2)}) copy-start(s32[128]{0:T(128)S(1)} %multiply_add_fusion.1) | copy-start | bytes 1540
  38.4 33.7 %collective-permute-start.5 = (bf16[1,64,3584]{2,1,0:T(8,128)(2,1)}, bf16[1,64,3584]{2,1,0:T(8,128)(2,1)S(1)}, u32[]{:S(2)}, u32[]{:S(2)}) collective-permute-start(bf16[1,64,3584]{2,1,0:T(8,128)(2,1)} %collective-permute-done.4), channel_id=1, source_target_pairs={{36,0},{37,1},{38,2},{39,3},{0,4},{1,5},{2,6},{3,7},{44,8},{45,9},... | collective-permute-start | bytes 1376264 | tf_op jit(solution)/shard_map/ppermute | solution.py:49
  53.0 25.0 %collective-permute-start.7 = (bf16[1,64,3584]{2,1,0:T(8,128)(2,1)}, bf16[1,64,3584]{2,1,0:T(8,128)(2,1)S(1)}, u32[]{:S(2)}, u32[]{:S(2)}) collective-permute-start(bf16[1,64,3584]{2,1,0:T(8,128)(2,1)} %collective-permute-done.6), channel_id=1, source_target_pairs={{4,0},{5,1},{6,2},{7,3},{32,4},{33,5},{34,6},{35,7},{12,8},{13,9},... | collective-permute-start | bytes 1376264 | tf_op jit(solution)/shard_map/ppermute | solution.py:50
  58.9 19.5 %copy-start.15 = (s32[128]{0:T(128)}, s32[128]{0:T(128)S(1)}, u32[]{:S(2)}) copy-start(s32[128]{0:T(128)S(1)} %multiply_add_fusion) | copy-start | bytes 1540
  58.9 19.5 %copy-start.17 = (f32[1,128]{1,0:T(1,128)S(1)}, f32[1,128]{1,0:T(1,128)}, u32[]{:S(2)}) copy-start(f32[1,128]{1,0:T(1,128)} %param.21) | copy-start | bytes 1540
  60.0 29.8 %collective-permute-start.1 = (bf16[1,64,3584]{2,1,0:T(8,128)(2,1)}, bf16[1,64,3584]{2,1,0:T(8,128)(2,1)S(1)}, u32[]{:S(2)}, u32[]{:S(2)}) collective-permute-start(bf16[1,64,3584]{2,1,0:T(8,128)(2,1)} %collective-permute-done), channel_id=1, source_target_pairs={{4,32},{5,33},{6,34},{7,35},{32,36},{33,37},{34,38},{35,39},{12,40... | collective-permute-start | bytes 1376264 | tf_op jit(solution)/shard_map/ppermute | solution.py:49
  61.3 36.5 %collective-permute-start.3 = (bf16[1,64,3584]{2,1,0:T(8,128)(2,1)}, bf16[1,64,3584]{2,1,0:T(8,128)(2,1)S(1)}, u32[]{:S(2)}, u32[]{:S(2)}) collective-permute-start(bf16[1,64,3584]{2,1,0:T(8,128)(2,1)} %collective-permute-done.2), channel_id=1, source_target_pairs={{36,32},{37,33},{38,34},{39,35},{0,36},{1,37},{2,38},{3,39},{44,40... | collective-permute-start | bytes 1376264 | tf_op jit(solution)/shard_map/ppermute | solution.py:50
  78.4 19.3 %copy-start.1 = (bf16[128,3584]{1,0:T(8,128)(2,1)S(1)}, bf16[128,3584]{1,0:T(8,128)(2,1)}, u32[]{:S(2)}) copy-start(bf16[128,3584]{1,0:T(8,128)(2,1)} %param.14) | copy-start | bytes 2752516
  97.8 1.7 copy-start.5
  203.2 4.7 %copy-start.4 = (bf16[1,3584,256]{2,1,0:T(8,128)(2,1)S(1)}, bf16[1,3584,256]{2,1,0:T(8,128)(2,1)}, u32[]{:S(2)}) copy-start(bf16[1,3584,256]{2,1,0:T(8,128)(2,1)} %param.24) | copy-start | bytes 5505028
  203.2 5.0 %copy-start.19 = (bf16[2,2,8,24,3584]{4,3,2,1,0:T(8,128)(2,1)S(1)}, bf16[2,2,8,24,3584]{4,3,2,1,0:T(8,128)(2,1)}, u32[]{:S(2)}) copy-start(bf16[2,2,8,24,3584]{4,3,2,1,0:T(8,128)(2,1)} %get-tuple-element.7) | copy-start | bytes 16515076
  208.1 1.6 copy-start.3
  321.0 2.0 copy-start.16
  322.9 1.4 copy-start.13
  322.9 1.4 copy-start.18
  324.4 1.2 copy-start.2
  324.4 1.3 copy-start.6
  324.9 2.1 copy-start.14

commit v11 on v9

--- a/solution.py
+++ b/solution.py
@@ -171,7 +171,7 @@
         copy.wait_send()
 
 
-def spread_to_holders(*sends):
+def spread_to_holders(*sends, collective_id=0):
     groups, capacity, features = sends[0].shape
     streams = len(sends)
     rows = jax.ShapeDtypeStruct((2, 2, groups, capacity, features), sends[0].dtype)
@@ -189,7 +189,7 @@
             pltpu.SemaphoreType.DMA((streams, 2, groups)),
             pltpu.SemaphoreType.DMA((streams, 2, groups)),
         ],
-        compiler_params=pltpu.CompilerParams(collective_id=0, has_side_effects=True),
+        compiler_params=pltpu.CompilerParams(collective_id=collective_id, has_side_effects=True),
     )(*sends)
 
 
@@ -365,6 +365,10 @@
         jnp.bfloat16
     )
 
+    (forward_rows,) = spread_to_holders(
+        forward_send.reshape(expert_count, capacity, feature_count), collective_id=0
+    )
+
     backward_dy = backward_in.astype(jnp.float32)
     along_dir = jnp.sum(backward_dy * unit_dir[None, :], axis=1)
     sent_rows = (
@@ -374,9 +378,8 @@
     backward_send = jnp.dot(backward_layout, sent_rows, preferred_element_type=jnp.float32).astype(
         jnp.bfloat16
     )
-    forward_rows, backward_rows = spread_to_holders(
-        forward_send.reshape(expert_count, capacity, feature_count),
-        backward_send.reshape(expert_count, capacity, feature_count),
+    (backward_rows,) = spread_to_holders(
+        backward_send.reshape(expert_count, capacity, feature_count), collective_id=2
     )
 
     flip = lax.axis_index("ep") == 1

time: 327 us -> 329 us (level)
  waiting for transfers between devices: 50.1 us -> 30.9 us
  Pallas kernels: 222 us -> 241 us
    pallas_call x1 -> x2, Pallas kernels: 121 us -> 141 us  [spread_to_holders(): pl.pallas_call(functools.partial(spread_kernel, groups), out_shape=[rows]...]
    ppermute x2, waiting for transfers between devices: 50.1 us -> 30.9 us  [shifted(): return lax.ppermute(value, axis, pairs)]
  transfers between devices with their start and end apart: 2 -> 2, of which waited for: 1 -> 1; matrix products, arithmetic and copies ran while one was open for 3% -> 5% of each run, Pallas kernels for 0% -> 25%
where the time goes in v11:
time: 329 us; the launch traced here: 326 us
  Pallas kernels  241 us (73%)
  waiting for transfers between devices  30.9 us (9%)
  matrix products  26.2 us (8%)
  starting transfers between devices  11.4 us (3%)
  other arithmetic  9.14 us (3%)
  local copies, waits for them, and re-layouts  5.06 us (2%)
    pallas_call x2, Pallas kernels, spread_to_holders(): pl.pallas_call(functools.partial(spread_kernel, groups), out_shape=[rows]...  141 us
    pallas_call x1, Pallas kernels, collect_from_holders(): pl.pallas_call(functools.partial(collect_kernel, groups), out_shape=jax.S...  100 us
    ppermute x2, waiting for transfers between devices, shifted(): return lax.ppermute(value, axis, pairs)  30.9 us
    ppermute x2, starting transfers between devices, shifted(): return lax.ppermute(value, axis, pairs)  11.4 us
  transfers between devices with their start and end apart: 2, of which 1 were waited for; matrix products, arithmetic and copies ran while one was open for 5% of the time, Pallas kernels for 25%

profile of v11, /device:TPU:24, one launch (start us, length us, event | category | flops | bytes accessed | tf_op | source)
XLA Modules:
  0.0 325.8 jit_solution(7560354910911462169)
XLA Ops:
  0.7 9.4 %collective-permute-start.1 = (bf16[1,128,3584]{2,1,0:T(8,128)(2,1)}, bf16[1,128,3584]{2,1,0:T(8,128)(2,1)}, u32[]{:S(2)}, u32[]{:S(2)}) collective-permute-start(bf16[1,128,3584]{2,1,0:T(8,128)(2,1)} %param.19), channel_id=1, source_target_pairs={{32,0},{64,32},{96,64},{128,96},{160,128},{192,160},{224,192},{33,... | collective-permute-start | bytes 2752520 | tf_op jit(solution)/shard_map/ppermute | solution.py:22
  10.1 2.0 collective-permute-start
  12.1 1.3 multiply_reduce_fusion.1
  14.2 0.7 fusion.35
  14.9 0.2 reduce_window_sum.18
  15.1 0.8 select_reduce_fusion
  15.9 1.0 copy.21
  17.0 1.0 copy.22
  18.0 0.1 fusion.36
  18.1 0.2 reduce_window_sum.17
  18.3 0.2 select_reduce_fusion.1
  18.6 0.5 multiply_add_fusion.1
  19.1 0.9 reverse_select_fusion
  20.0 30.9 %collective-permute-done.1 = bf16[1,128,3584]{2,1,0:T(8,128)(2,1)} collective-permute-done((bf16[1,128,3584]{2,1,0:T(8,128)(2,1)}, bf16[1,128,3584]{2,1,0:T(8,128)(2,1)}, u32[]{:S(2)}, u32[]{:S(2)}) %collective-permute-start.1) | collective-permute-done | bytes 917536 | tf_op jit(solution)/shard_map/ppermute | solution.py:22
  50.9 1.6 fusion.2
  52.5 1.8 convolution_convert_fusion.1
  54.3 82.5 %shard_map.158 = bf16[2,2,8,24,3584]{4,3,2,1,0:T(8,128)(2,1)} custom-call(bf16[8,24,3584]{2,1,0:T(8,128)(2,1)} %bitcast.75), custom_call_target="tpu_custom_call" | custom-call | tf_op jit(solution)/shard_map/pallas_call | solution.py:179
  136.8 5.2 %fusion.33 = (bf16[768,256]{1,0:T(8,128)(2,1)}, bf16[768,256]{1,0:T(8,128)(2,1)S(1)}) fusion(bf16[2,2,8,24,256]{4,3,2,1,0:T(8,128)(2,1)S(1)} %get-tuple-element.15, bf16[2,2,8,24,256]{4,3,2,1,0:T(8,128)(2,1)} %get-tuple-element.16, bf16[768,3584]{1,0:T(8,128)(2,1)} %bitcast.77, bf16[1,256,3584]{2,1,0:T(8,128)(2,1)S(1)} %copy-done), kind=kOutput, calls=%fused_computation.43 | convolution fusion | flops 1412235264 | bytes 8912896 | tf_op jit(solution)/shard_map/dot_general | solution.py:48
  142.1 2.9 convolution_convert_fusion.2
  144.9 58.8 %shard_map.157 = bf16[2,2,8,24,3584]{4,3,2,1,0:T(8,128)(2,1)} custom-call(bf16[8,24,3584]{2,1,0:T(8,128)(2,1)} %bitcast.76), custom_call_target="tpu_custom_call" | custom-call | tf_op jit(solution)/shard_map/pallas_call | solution.py:179
  203.7 3.3 %fusion.11 = f32[768,3584]{1,0:T(8,128)S(1)} fusion(bf16[768,256]{1,0:T(8,128)(2,1)S(1)} %get-tuple-element.5, bf16[1,3584,256]{2,1,0:T(8,128)(2,1)} %param.24), kind=kOutput, calls=%fused_computation.19 | convolution fusion | flops 1409286144 | bytes 13238272 | tf_op jit(solution)/shard_map/dot_general | solution.py:59
  207.0 0.4 copy-done.5
  207.4 1.6 fusion.13
  209.0 1.6 fusion.18
  210.6 4.0 %convolution_convert_fusion = bf16[768,3584]{1,0:T(8,128)(2,1)} fusion(bf16[768,256]{1,0:T(8,128)(2,1)S(1)} %fusion.18, bf16[1,256,3584]{2,1,0:T(8,128)(2,1)S(1)} %copy-done), kind=kOutput, calls=%fused_computation.1 | convolution fusion | flops 1412038656 | bytes 7733248 | tf_op jit(solution)/shard_map/dot_general | solution.py:42
  214.6 4.1 %add_convert_fusion = bf16[768,3584]{1,0:T(8,128)(2,1)} fusion(f32[768,3584]{1,0:T(8,128)S(1)} %fusion.11, bf16[768,256]{1,0:T(8,128)(2,1)S(1)} %copy-done.6, bf16[1,3584,256]{2,1,0:T(8,128)(2,1)S(1)} %copy-done.4), kind=kOutput, calls=%fused_computation | convolution fusion | flops 1414791168 | bytes 18743296 | tf_op jit(solution)/shard_map/dot_general | solution.py:60
  218.7 100.0 %shard_map.159 = bf16[2,8,24,3584]{3,2,1,0:T(8,128)(2,1)} custom-call(bf16[2,2,8,24,3584]{4,3,2,1,0:T(8,128)(2,1)} %bitcast.71, bf16[2,2,8,24,3584]{4,3,2,1,0:T(8,128)(2,1)} %bitcast.72), custom_call_target="tpu_custom_call" | custom-call | tf_op jit(solution)/shard_map/pallas_call | solution.py:305
  318.7 1.9 fusion.41
  320.7 1.4 fusion.1
  322.1 0.5 multiply_reduce_fusion
  322.6 0.6 copy-done.3
  323.3 2.6 fusion.21
  (35 shorter events, 0.1 us)
Async XLA Ops:
  0.6 136.2 %copy-start = (bf16[1,256,3584]{2,1,0:T(8,128)(2,1)S(1)}, bf16[1,256,3584]{2,1,0:T(8,128)(2,1)}, u32[]{:S(2)}) copy-start(bf16[1,256,3584]{2,1,0:T(8,128)(2,1)} %param.26) | copy-start | bytes 5505028
  0.6 17.8 %copy-start.7 = (f32[1,3584]{1,0:T(1,128)S(1)}, f32[1,3584]{1,0:T(1,128)}, u32[]{:S(2)}) copy-start(f32[1,3584]{1,0:T(1,128)} %param.27) | copy-start | bytes 43012
  0.7 17.9 %copy-start.8 = (s32[1,128,1]{1,2,0:T(1,128)S(1)}, s32[1,128,1]{1,2,0:T(1,128)}, u32[]{:S(2)}) copy-start(s32[1,128,1]{1,2,0:T(1,128)} %param.20) | copy-start | bytes 1540
  0.7 17.3 %copy-start.9 = (s32[1,128,1]{1,2,0:T(1,128)S(1)}, s32[1,128,1]{1,2,0:T(1,128)}, u32[]{:S(2)}) copy-start(s32[1,128,1]{1,2,0:T(1,128)} %param.16) | copy-start | bytes 1540
  0.7 50.2 %collective-permute-start.1 = (bf16[1,128,3584]{2,1,0:T(8,128)(2,1)}, bf16[1,128,3584]{2,1,0:T(8,128)(2,1)}, u32[]{:S(2)}, u32[]{:S(2)}) collective-permute-start(bf16[1,128,3584]{2,1,0:T(8,128)(2,1)} %param.19), channel_id=1, source_target_pairs={{32,0},{64,32},{96,64},{128,96},{160,128},{192,160},{224,192},{33,... | collective-permute-start | bytes 2752520 | tf_op jit(solution)/shard_map/ppermute | solution.py:22
  10.1 132.0 %collective-permute-start = (bf16[1,128,3584]{2,1,0:T(8,128)(2,1)}, bf16[1,128,3584]{2,1,0:T(8,128)(2,1)}, u32[]{:S(2)}, u32[]{:S(2)}) collective-permute-start(bf16[1,128,3584]{2,1,0:T(8,128)(2,1)} %param.15), channel_id=1, source_target_pairs={{0,32},{32,64},{64,96},{96,128},{128,160},{160,192},{192,224},{1,3... | collective-permute-start | bytes 2752520 | tf_op jit(solution)/shard_map/ppermute | solution.py:22
  18.5 34.0 %copy-start.13 = (s32[128]{0:T(128)}, s32[128]{0:T(128)S(1)}, u32[]{:S(2)}) copy-start(s32[128]{0:T(128)S(1)} %multiply_add_fusion) | copy-start | bytes 1540
  19.1 33.4 %copy-start.15 = (f32[1,128]{1,0:T(1,128)S(1)}, f32[1,128]{1,0:T(1,128)}, u32[]{:S(2)}) copy-start(f32[1,128]{1,0:T(1,128)} %param.21) | copy-start | bytes 1540
  136.8 5.2 %copy-start.2 = (bf16[128,3584]{1,0:T(8,128)(2,1)S(1)}, bf16[128,3584]{1,0:T(8,128)(2,1)}, u32[]{:S(2)}) copy-start(bf16[128,3584]{1,0:T(8,128)(2,1)} %param.14) | copy-start | bytes 2752516
  136.8 5.2 %copy-start.10 = (s32[128]{0:T(128)S(1)}, s32[128]{0:T(128)}, u32[]{:S(2)}) copy-start(s32[128]{0:T(128)} %multiply_add_fusion.1) | copy-start | bytes 1540
  203.7 3.3 %copy-start.1 = (bf16[2,2,8,24,3584]{4,3,2,1,0:T(8,128)(2,1)S(1)}, bf16[2,2,8,24,3584]{4,3,2,1,0:T(8,128)(2,1)}, u32[]{:S(2)}) copy-start(bf16[2,2,8,24,3584]{4,3,2,1,0:T(8,128)(2,1)} %shard_map.157) | copy-start | bytes 16515076
  203.7 3.7 %copy-start.5 = (bf16[1,3584,256]{2,1,0:T(8,128)(2,1)S(1)}, bf16[1,3584,256]{2,1,0:T(8,128)(2,1)}, u32[]{:S(2)}) copy-start(bf16[1,3584,256]{2,1,0:T(8,128)(2,1)} %param.24) | copy-start | bytes 5505028
  207.4 1.6 copy-start.4
  210.6 4.0 %copy-start.6 = (bf16[768,256]{1,0:T(8,128)(2,1)S(1)}, bf16[768,256]{1,0:T(8,128)(2,1)}, u32[]{:S(2)}) copy-start(bf16[768,256]{1,0:T(8,128)(2,1)} %get-tuple-element.6) | copy-start | bytes 1179652
  318.7 2.0 copy-start.14
  320.7 1.4 copy-start.11
  320.7 1.4 copy-start.16
  322.1 1.2 copy-start.3
  322.6 3.2 copy-start.12

commit v12 on v9

--- a/solution.py
+++ b/solution.py
@@ -56,10 +56,9 @@
     ).astype(jnp.bfloat16)
     grad_up = (grad_hidden * gate_pre * sigmoid_gate).astype(jnp.bfloat16)
     grad_gate, grad_up = lax.optimization_barrier((grad_gate, grad_up))
-    grad_part = lax.dot_general(grad_gate, gate_cols, contract, preferred_element_type=jnp.float32)
-    grad_part = grad_part + lax.dot_general(
-        grad_up, up_cols, contract, preferred_element_type=jnp.float32
-    )
+    grads = jnp.concatenate([grad_gate, grad_up], axis=1)
+    both_cols = jnp.concatenate([gate_cols, up_cols], axis=1)
+    grad_part = lax.dot_general(grads, both_cols, contract, preferred_element_type=jnp.float32)
     return grad_part.astype(jnp.bfloat16)
 
 

time: 327 us -> 320 us (0.979); the launches traced: 323 us -> 319 us
  waiting for transfers between devices: 50.1 us -> 46.6 us
    ppermute x2, waiting for transfers between devices: 50.1 us -> 46.6 us  [shifted(): return lax.ppermute(value, axis, pairs)]
  transfers between devices with their start and end apart: 2 -> 2, of which waited for: 1 -> 2; matrix products, arithmetic and copies ran while one was open for 3% -> 3% of each run, Pallas kernels for 0% -> 0%
where the time goes in v12:
time: 320 us; the launch traced here: 319 us
  Pallas kernels  223 us (70%)
  waiting for transfers between devices  46.6 us (15%)
  matrix products  22.9 us (7%)
  starting transfers between devices  11.4 us (4%)
  other arithmetic  8.54 us (3%)
  local copies, waits for them, and re-layouts  4.92 us (2%)
    pallas_call x1, Pallas kernels, spread_to_holders(): pl.pallas_call(functools.partial(spread_kernel, groups), out_shape=[rows]...  123 us
    pallas_call x1, Pallas kernels, collect_from_holders(): pl.pallas_call(functools.partial(collect_kernel, groups), out_shape=jax.S...  101 us
    ppermute x2, waiting for transfers between devices, shifted(): return lax.ppermute(value, axis, pairs)  46.6 us
    ppermute x2, starting transfers between devices, shifted(): return lax.ppermute(value, axis, pairs)  11.4 us
  transfers between devices with their start and end apart: 2, of which 2 were waited for; matrix products, arithmetic and copies ran while one was open for 3% of the time, Pallas kernels for 0%

profile of v12, /device:TPU:24, one launch (start us, length us, event | category | flops | bytes accessed | tf_op | source)
XLA Modules:
  0.0 319.5 jit_solution(4152930780281421543)
XLA Ops:
  0.6 0.0 copy-start
  0.7 0.0 copy-start.4
  0.7 9.4 %collective-permute-start.1 = (bf16[1,128,3584]{2,1,0:T(8,128)(2,1)}, bf16[1,128,3584]{2,1,0:T(8,128)(2,1)}, u32[]{:S(2)}, u32[]{:S(2)}) collective-permute-start(bf16[1,128,3584]{2,1,0:T(8,128)(2,1)} %param.19), channel_id=1, source_target_pairs={{32,0},{64,32},{96,64},{128,96},{160,128},{192,160},{224,192},{33,... | collective-permute-start | bytes 2752520 | tf_op jit(solution)/shard_map/ppermute | solution.py:22
  10.1 2.0 collective-permute-start
  12.1 1.3 multiply_reduce_fusion.1
  14.2 0.7 fusion.29
  14.9 0.2 reduce_window_sum.18
  15.1 0.8 select_reduce_fusion
  15.9 0.7 fusion.30
  16.7 0.2 reduce_window_sum.17
  16.9 1.0 copy.21
  17.9 1.0 copy.22
  18.9 0.2 select_reduce_fusion.1
  19.2 0.1 reverse_select_fusion
  19.4 31.5 %collective-permute-done.1 = bf16[1,128,3584]{2,1,0:T(8,128)(2,1)} collective-permute-done((bf16[1,128,3584]{2,1,0:T(8,128)(2,1)}, bf16[1,128,3584]{2,1,0:T(8,128)(2,1)}, u32[]{:S(2)}, u32[]{:S(2)}) %collective-permute-start.1) | collective-permute-done | bytes 917536 | tf_op jit(solution)/shard_map/ppermute | solution.py:22
  50.9 1.6 fusion.5
  52.5 1.8 convolution_convert_fusion.2
  54.3 15.1 %collective-permute-done = bf16[1,128,3584]{2,1,0:T(8,128)(2,1)} collective-permute-done((bf16[1,128,3584]{2,1,0:T(8,128)(2,1)}, bf16[1,128,3584]{2,1,0:T(8,128)(2,1)}, u32[]{:S(2)}, u32[]{:S(2)}) %collective-permute-start) | collective-permute-done | bytes 917536 | tf_op jit(solution)/shard_map/ppermute | solution.py:22
  69.4 2.8 convolution_convert_fusion.3
  72.2 122.5 %shard_map.157 = (bf16[2,2,8,24,3584]{4,3,2,1,0:T(8,128)(2,1)}, bf16[2,2,8,24,3584]{4,3,2,1,0:T(8,128)(2,1)}) custom-call(bf16[8,24,3584]{2,1,0:T(8,128)(2,1)} %bitcast.66, bf16[8,24,3584]{2,1,0:T(8,128)(2,1)} %bitcast.64), custom_call_target="tpu_custom_call" | custom-call | tf_op jit(solution)/shard_map/pallas_call | solution.py:178
  194.8 4.5 %fusion.24 = (bf16[768,256]{1,0:T(8,128)(2,1)S(1)}, bf16[768,256]{1,0:T(8,128)(2,1)S(1)}) fusion(bf16[2,2,8,24,256]{4,3,2,1,0:T(8,128)(2,1)S(1)} %get-tuple-element.19, bf16[2,2,8,24,256]{4,3,2,1,0:T(8,128)(2,1)S(1)} %get-tuple-element.20, bf16[768,3584]{1,0:T(8,128)(2,1)} %bitcast.80, bf16[1,256,3584]{2,1,0:T(8,128)(2,1)S(1)} %copy-done), kind=kOutput, calls=%fused_computation.39 | convolution fusion | flops 1412235264 | bytes 8912896 | tf_op jit(solution)/shard_map/dot_general | solution.py:48
  199.3 0.2 copy-done.14
  199.5 1.6 fusion.37
  201.1 1.6 fusion.11
  202.7 4.0 %convolution_convert_fusion.1 = bf16[768,3584]{1,0:T(8,128)(2,1)} fusion(bf16[768,256]{1,0:T(8,128)(2,1)S(1)} %fusion.11, bf16[1,256,3584]{2,1,0:T(8,128)(2,1)S(1)} %copy-done), kind=kOutput, calls=%fused_computation.1 | convolution fusion | flops 1412038656 | bytes 7733248 | tf_op jit(solution)/shard_map/dot_general | solution.py:42
  206.7 4.8 %convolution_convert_fusion = bf16[768,3584]{1,0:T(8,128)(2,1)} fusion(bf16[3584,256]{1,0:T(8,128)(2,1)S(1)} %bitcast.82, bf16[3584,256]{1,0:T(8,128)(2,1)S(1)} %bitcast.81, bf16[768,256]{1,0:T(8,128)(2,1)S(1)} %get-tuple-element.10, bf16[768,256]{1,0:T(8,128)(2,1)S(1)} %get-tuple-element.9), kind=kOutput, calls=%fused_computation | convolution fusion | flops 2830237696 | bytes 9961472 | tf_op jit(solution)/shard_map/dot_general | solution.py:61
  211.5 100.8 %shard_map.158 = bf16[2,8,24,3584]{3,2,1,0:T(8,128)(2,1)} custom-call(bf16[2,2,8,24,3584]{4,3,2,1,0:T(8,128)(2,1)} %bitcast.61, bf16[2,2,8,24,3584]{4,3,2,1,0:T(8,128)(2,1)} %bitcast.63), custom_call_target="tpu_custom_call" | custom-call | tf_op jit(solution)/shard_map/pallas_call | solution.py:304
  312.4 1.9 fusion.39
  314.3 1.4 fusion.1
  315.7 0.6 multiply_reduce_fusion
  316.3 0.6 copy-done.2
  316.9 2.6 fusion.12
  (31 shorter events, 0.1 us)
Async XLA Ops:
  0.6 194.1 %copy-start = (bf16[1,256,3584]{2,1,0:T(8,128)(2,1)S(1)}, bf16[1,256,3584]{2,1,0:T(8,128)(2,1)}, u32[]{:S(2)}) copy-start(bf16[1,256,3584]{2,1,0:T(8,128)(2,1)} %param.26) | copy-start | bytes 5505028
  0.6 18.5 %copy-start.3 = (f32[1,3584]{1,0:T(1,128)S(1)}, f32[1,3584]{1,0:T(1,128)}, u32[]{:S(2)}) copy-start(f32[1,3584]{1,0:T(1,128)} %param.27) | copy-start | bytes 43012
  0.7 18.5 %copy-start.4 = (s32[1,128,1]{1,2,0:T(1,128)S(1)}, s32[1,128,1]{1,2,0:T(1,128)}, u32[]{:S(2)}) copy-start(s32[1,128,1]{1,2,0:T(1,128)} %param.20) | copy-start | bytes 1540
  0.7 18.3 %copy-start.5 = (s32[1,128,1]{1,2,0:T(1,128)S(1)}, s32[1,128,1]{1,2,0:T(1,128)}, u32[]{:S(2)}) copy-start(s32[1,128,1]{1,2,0:T(1,128)} %param.16) | copy-start | bytes 1540
  0.7 50.2 %collective-permute-start.1 = (bf16[1,128,3584]{2,1,0:T(8,128)(2,1)}, bf16[1,128,3584]{2,1,0:T(8,128)(2,1)}, u32[]{:S(2)}, u32[]{:S(2)}) collective-permute-start(bf16[1,128,3584]{2,1,0:T(8,128)(2,1)} %param.19), channel_id=1, source_target_pairs={{32,0},{64,32},{96,64},{128,96},{160,128},{192,160},{224,192},{33,... | collective-permute-start | bytes 2752520 | tf_op jit(solution)/shard_map/ppermute | solution.py:22
  10.1 59.3 %collective-permute-start = (bf16[1,128,3584]{2,1,0:T(8,128)(2,1)}, bf16[1,128,3584]{2,1,0:T(8,128)(2,1)}, u32[]{:S(2)}, u32[]{:S(2)}) collective-permute-start(bf16[1,128,3584]{2,1,0:T(8,128)(2,1)} %param.15), channel_id=1, source_target_pairs={{0,32},{32,64},{64,96},{96,128},{128,160},{160,192},{192,224},{1,3... | collective-permute-start | bytes 2752520 | tf_op jit(solution)/shard_map/ppermute | solution.py:22
  19.1 33.4 %copy-start.9 = (s32[128]{0:T(128)}, s32[128]{0:T(128)S(1)}, u32[]{:S(2)}) copy-start(s32[128]{0:T(128)S(1)} %multiply_add_fusion) | copy-start | bytes 1540
  19.2 50.3 %copy-start.6 = (s32[128]{0:T(128)}, s32[128]{0:T(128)S(1)}, u32[]{:S(2)}) copy-start(s32[128]{0:T(128)S(1)} %multiply_add_fusion.1) | copy-start | bytes 1540
  19.2 33.3 %copy-start.11 = (f32[1,128]{1,0:T(1,128)S(1)}, f32[1,128]{1,0:T(1,128)}, u32[]{:S(2)}) copy-start(f32[1,128]{1,0:T(1,128)} %param.21) | copy-start | bytes 1540
  52.5 16.9 %copy-start.1 = (bf16[128,3584]{1,0:T(8,128)(2,1)S(1)}, bf16[128,3584]{1,0:T(8,128)(2,1)}, u32[]{:S(2)}) copy-start(bf16[128,3584]{1,0:T(8,128)(2,1)} %param.14) | copy-start | bytes 2752516
  194.8 4.5 %copy-start.13 = (bf16[2,2,8,24,3584]{4,3,2,1,0:T(8,128)(2,1)S(1)}, bf16[2,2,8,24,3584]{4,3,2,1,0:T(8,128)(2,1)}, u32[]{:S(2)}) copy-start(bf16[2,2,8,24,3584]{4,3,2,1,0:T(8,128)(2,1)} %get-tuple-element.7) | copy-start | bytes 16515076
  194.8 4.7 %copy-start.14 = (bf16[1,3584,256]{2,1,0:T(8,128)(2,1)S(1)}, bf16[1,3584,256]{2,1,0:T(8,128)(2,1)}, u32[]{:S(2)}) copy-start(bf16[1,3584,256]{2,1,0:T(8,128)(2,1)} %param.24) | copy-start | bytes 5505028
  199.5 1.6 copy-start.15
  312.3 2.0 copy-start.10
  314.3 1.4 copy-start.7
  314.3 1.4 copy-start.12
  315.7 1.2 copy-start.2
  316.3 3.2 %copy-start.8 = (f32[128]{0:T(128)}, f32[128]{0:T(128)S(1)}, u32[]{:S(2)}) copy-start(f32[128]{0:T(128)S(1)} %get-tuple-element.17) | copy-start | bytes 1540

commit v13 on v12

--- a/solution.py
+++ b/solution.py
@@ -36,8 +36,10 @@
 
 def expert_forward(slot_rows, weights):
     gate_cols, up_cols, down_rows = weights
-    gate_pre = jnp.dot(slot_rows, gate_cols, preferred_element_type=jnp.float32)
-    up_pre = jnp.dot(slot_rows, up_cols, preferred_element_type=jnp.float32)
+    both_pre = jnp.dot(
+        slot_rows, jnp.concatenate([gate_cols, up_cols], axis=1), preferred_element_type=jnp.float32
+    )
+    gate_pre, up_pre = jnp.split(both_pre, 2, axis=1)
     hidden = lax.optimization_barrier((jax.nn.silu(gate_pre) * up_pre).astype(jnp.bfloat16))
     return jnp.dot(hidden, down_rows, preferred_element_type=jnp.float32).astype(jnp.bfloat16)
 

time: 320 us -> 321 us (level)
  no operation moved by 1% of the time
where the time goes in v13:
time: 321 us; the launch traced here: 320 us
  Pallas kernels  223 us (69%)
  waiting for transfers between devices  46.6 us (15%)
  matrix products  22.7 us (7%)
  starting transfers between devices  11.4 us (4%)
  other arithmetic  8.77 us (3%)
  local copies, waits for them, and re-layouts  5.43 us (2%)
    pallas_call x1, Pallas kernels, spread_to_holders(): pl.pallas_call(functools.partial(spread_kernel, groups), out_shape=[rows]...  123 us
    pallas_call x1, Pallas kernels, collect_from_holders(): pl.pallas_call(functools.partial(collect_kernel, groups), out_shape=jax.S...  101 us
    ppermute x2, waiting for transfers between devices, shifted(): return lax.ppermute(value, axis, pairs)  46.6 us
    ppermute x2, starting transfers between devices, shifted(): return lax.ppermute(value, axis, pairs)  11.4 us
  transfers between devices with their start and end apart: 2, of which 2 were waited for; matrix products, arithmetic and copies ran while one was open for 3% of the time, Pallas kernels for 0%

profile of v13, /device:TPU:24, one launch (start us, length us, event | category | flops | bytes accessed | tf_op | source)
XLA Modules:
  0.0 320.0 jit_solution(14976813675353944485)
XLA Ops:
  0.6 0.0 copy-start
  0.7 9.4 %collective-permute-start.1 = (bf16[1,128,3584]{2,1,0:T(8,128)(2,1)}, bf16[1,128,3584]{2,1,0:T(8,128)(2,1)}, u32[]{:S(2)}, u32[]{:S(2)}) collective-permute-start(bf16[1,128,3584]{2,1,0:T(8,128)(2,1)} %param.19), channel_id=1, source_target_pairs={{32,0},{64,32},{96,64},{128,96},{160,128},{192,160},{224,192},{33,... | collective-permute-start | bytes 2752520 | tf_op jit(solution)/shard_map/ppermute | solution.py:22
  10.1 2.0 collective-permute-start
  12.1 1.3 multiply_reduce_fusion.1
  14.2 0.7 fusion.27
  14.9 0.2 reduce_window_sum.18
  15.1 0.8 select_reduce_fusion
  15.9 0.7 fusion.28
  16.7 0.2 reduce_window_sum.17
  16.9 1.0 copy.21
  17.9 1.0 copy.22
  18.9 0.2 select_reduce_fusion.1
  19.2 0.1 reverse_select_fusion
  19.4 31.5 %collective-permute-done.1 = bf16[1,128,3584]{2,1,0:T(8,128)(2,1)} collective-permute-done((bf16[1,128,3584]{2,1,0:T(8,128)(2,1)}, bf16[1,128,3584]{2,1,0:T(8,128)(2,1)}, u32[]{:S(2)}, u32[]{:S(2)}) %collective-permute-start.1) | collective-permute-done | bytes 917536 | tf_op jit(solution)/shard_map/ppermute | solution.py:22
  50.9 1.6 fusion.3
  52.5 1.8 convolution_convert_fusion.2
  54.3 15.1 %collective-permute-done = bf16[1,128,3584]{2,1,0:T(8,128)(2,1)} collective-permute-done((bf16[1,128,3584]{2,1,0:T(8,128)(2,1)}, bf16[1,128,3584]{2,1,0:T(8,128)(2,1)}, u32[]{:S(2)}, u32[]{:S(2)}) %collective-permute-start) | collective-permute-done | bytes 917536 | tf_op jit(solution)/shard_map/ppermute | solution.py:22
  69.4 2.8 convolution_convert_fusion.3
  72.2 122.5 %shard_map.157 = (bf16[2,2,8,24,3584]{4,3,2,1,0:T(8,128)(2,1)}, bf16[2,2,8,24,3584]{4,3,2,1,0:T(8,128)(2,1)}) custom-call(bf16[8,24,3584]{2,1,0:T(8,128)(2,1)} %bitcast.61, bf16[8,24,3584]{2,1,0:T(8,128)(2,1)} %bitcast.59), custom_call_target="tpu_custom_call" | custom-call | tf_op jit(solution)/shard_map/pallas_call | solution.py:180
  194.8 4.5 %fusion.21 = (bf16[768,256]{1,0:T(8,128)(2,1)S(1)}, bf16[768,256]{1,0:T(8,128)(2,1)S(1)}) fusion(bf16[2,2,8,24,256]{4,3,2,1,0:T(8,128)(2,1)S(1)} %get-tuple-element.19, bf16[2,2,8,24,256]{4,3,2,1,0:T(8,128)(2,1)S(1)} %get-tuple-element.20, bf16[768,3584]{1,0:T(8,128)(2,1)} %bitcast.74, bf16[1,256,3584]{2,1,0:T(8,128)(2,1)S(1)} %copy-done), kind=kOutput, calls=%fused_computation.36 | convolution fusion | flops 1412235264 | bytes 8912896 | tf_op jit(solution)/shard_map/dot_general | solution.py:50
  199.3 0.2 copy-done.14
  199.5 0.5 copy-done.15
  200.0 3.0 fusion.2
  203.0 0.2 fusion.22
  203.3 4.0 %convolution_convert_fusion.1 = bf16[768,3584]{1,0:T(8,128)(2,1)} fusion(bf16[768,256]{1,0:T(8,128)(2,1)S(1)} %fusion.22, bf16[1,256,3584]{2,1,0:T(8,128)(2,1)S(1)} %copy-done), kind=kOutput, calls=%fused_computation.1 | convolution fusion | flops 1412038656 | bytes 7733248 | tf_op jit(solution)/shard_map/dot_general | solution.py:44
  207.2 4.8 %convolution_convert_fusion = bf16[768,3584]{1,0:T(8,128)(2,1)} fusion(bf16[3584,256]{1,0:T(8,128)(2,1)S(1)} %bitcast.76, bf16[3584,256]{1,0:T(8,128)(2,1)S(1)} %bitcast.78, bf16[768,256]{1,0:T(8,128)(2,1)S(1)} %get-tuple-element.10, bf16[768,256]{1,0:T(8,128)(2,1)S(1)} %get-tuple-element.9), kind=kOutput, calls=%fused_computation | convolution fusion | flops 2830237696 | bytes 9961472 | tf_op jit(solution)/shard_map/dot_general | solution.py:63
  212.1 100.8 %shard_map.158 = bf16[2,8,24,3584]{3,2,1,0:T(8,128)(2,1)} custom-call(bf16[2,2,8,24,3584]{4,3,2,1,0:T(8,128)(2,1)} %bitcast.56, bf16[2,2,8,24,3584]{4,3,2,1,0:T(8,128)(2,1)} %bitcast.58), custom_call_target="tpu_custom_call" | custom-call | tf_op jit(solution)/shard_map/pallas_call | solution.py:306
  312.9 1.9 fusion.35
  314.9 1.4 fusion.1
  316.3 0.6 multiply_reduce_fusion
  316.8 0.6 copy-done.2
  317.5 2.6 fusion.9
  (31 shorter events, 0.1 us)
Async XLA Ops:
  0.6 194.1 %copy-start = (bf16[1,256,3584]{2,1,0:T(8,128)(2,1)S(1)}, bf16[1,256,3584]{2,1,0:T(8,128)(2,1)}, u32[]{:S(2)}) copy-start(bf16[1,256,3584]{2,1,0:T(8,128)(2,1)} %param.26) | copy-start | bytes 5505028
  0.6 18.5 %copy-start.3 = (f32[1,3584]{1,0:T(1,128)S(1)}, f32[1,3584]{1,0:T(1,128)}, u32[]{:S(2)}) copy-start(f32[1,3584]{1,0:T(1,128)} %param.27) | copy-start | bytes 43012
  0.7 18.5 %copy-start.4 = (s32[1,128,1]{1,2,0:T(1,128)S(1)}, s32[1,128,1]{1,2,0:T(1,128)}, u32[]{:S(2)}) copy-start(s32[1,128,1]{1,2,0:T(1,128)} %param.20) | copy-start | bytes 1540
  0.7 18.3 %copy-start.5 = (s32[1,128,1]{1,2,0:T(1,128)S(1)}, s32[1,128,1]{1,2,0:T(1,128)}, u32[]{:S(2)}) copy-start(s32[1,128,1]{1,2,0:T(1,128)} %param.16) | copy-start | bytes 1540
  0.7 50.2 %collective-permute-start.1 = (bf16[1,128,3584]{2,1,0:T(8,128)(2,1)}, bf16[1,128,3584]{2,1,0:T(8,128)(2,1)}, u32[]{:S(2)}, u32[]{:S(2)}) collective-permute-start(bf16[1,128,3584]{2,1,0:T(8,128)(2,1)} %param.19), channel_id=1, source_target_pairs={{32,0},{64,32},{96,64},{128,96},{160,128},{192,160},{224,192},{33,... | collective-permute-start | bytes 2752520 | tf_op jit(solution)/shard_map/ppermute | solution.py:22
  10.1 59.3 %collective-permute-start = (bf16[1,128,3584]{2,1,0:T(8,128)(2,1)}, bf16[1,128,3584]{2,1,0:T(8,128)(2,1)}, u32[]{:S(2)}, u32[]{:S(2)}) collective-permute-start(bf16[1,128,3584]{2,1,0:T(8,128)(2,1)} %param.15), channel_id=1, source_target_pairs={{0,32},{32,64},{64,96},{96,128},{128,160},{160,192},{192,224},{1,3... | collective-permute-start | bytes 2752520 | tf_op jit(solution)/shard_map/ppermute | solution.py:22
  19.1 33.4 %copy-start.9 = (s32[128]{0:T(128)}, s32[128]{0:T(128)S(1)}, u32[]{:S(2)}) copy-start(s32[128]{0:T(128)S(1)} %multiply_add_fusion) | copy-start | bytes 1540
  19.2 50.3 %copy-start.6 = (s32[128]{0:T(128)}, s32[128]{0:T(128)S(1)}, u32[]{:S(2)}) copy-start(s32[128]{0:T(128)S(1)} %multiply_add_fusion.1) | copy-start | bytes 1540
  19.2 33.3 %copy-start.11 = (f32[1,128]{1,0:T(1,128)S(1)}, f32[1,128]{1,0:T(1,128)}, u32[]{:S(2)}) copy-start(f32[1,128]{1,0:T(1,128)} %param.21) | copy-start | bytes 1540
  52.5 16.9 %copy-start.1 = (bf16[128,3584]{1,0:T(8,128)(2,1)S(1)}, bf16[128,3584]{1,0:T(8,128)(2,1)}, u32[]{:S(2)}) copy-start(bf16[128,3584]{1,0:T(8,128)(2,1)} %param.14) | copy-start | bytes 2752516
  194.8 4.5 %copy-start.13 = (bf16[2,2,8,24,3584]{4,3,2,1,0:T(8,128)(2,1)S(1)}, bf16[2,2,8,24,3584]{4,3,2,1,0:T(8,128)(2,1)}, u32[]{:S(2)}) copy-start(bf16[2,2,8,24,3584]{4,3,2,1,0:T(8,128)(2,1)} %get-tuple-element.7) | copy-start | bytes 16515076
  194.8 4.7 %copy-start.14 = (bf16[1,3584,256]{2,1,0:T(8,128)(2,1)S(1)}, bf16[1,3584,256]{2,1,0:T(8,128)(2,1)}, u32[]{:S(2)}) copy-start(bf16[1,3584,256]{2,1,0:T(8,128)(2,1)} %param.25) | copy-start | bytes 5505028
  194.8 5.3 %copy-start.15 = (bf16[1,3584,256]{2,1,0:T(8,128)(2,1)S(1)}, bf16[1,3584,256]{2,1,0:T(8,128)(2,1)}, u32[]{:S(2)}) copy-start(bf16[1,3584,256]{2,1,0:T(8,128)(2,1)} %param.24) | copy-start | bytes 5505028
  312.9 2.0 copy-start.10
  314.9 1.4 copy-start.7
  314.9 1.4 copy-start.12
  316.3 1.2 copy-start.2
  316.8 3.2 %copy-start.8 = (f32[128]{0:T(128)}, f32[128]{0:T(128)S(1)}, u32[]{:S(2)}) copy-start(f32[128]{0:T(128)S(1)} %get-tuple-element.17) | copy-start | bytes 1540

commit v14 on v12

--- a/solution.py
+++ b/solution.py
@@ -32,6 +32,21 @@
     return (
         jnp.arange(expert_count * capacity, dtype=jnp.int32)[:, None] == target[None, :]
     ).astype(jnp.bfloat16)
+
+
+def gather_slots(expert_ids, expert_count, capacity, tokens):
+    onehot = (expert_ids[:, None] == jnp.arange(expert_count, dtype=jnp.int32)[None, :]).astype(
+        jnp.int32
+    )
+    earlier = jnp.cumsum(onehot, axis=0) - onehot
+    position = jnp.sum(earlier * onehot, axis=1)
+    target = expert_ids * capacity + position
+    count = tokens.shape[0]
+    slot_token = jnp.full((expert_count * capacity,), count, jnp.int32).at[target].set(
+        jnp.arange(count, dtype=jnp.int32)
+    )
+    padded = jnp.concatenate([tokens, jnp.zeros((1, tokens.shape[1]), tokens.dtype)], axis=0)
+    return padded[slot_token]
 
 
 def expert_forward(slot_rows, weights):
@@ -360,9 +375,7 @@
     weights = (gate_weight[0], up_weight[0], down_weight[0])
 
     forward_layout = dispatch_layout(forward_route[0, :, 0], expert_count, capacity)
-    forward_send = jnp.dot(forward_layout, forward_in, preferred_element_type=jnp.float32).astype(
-        jnp.bfloat16
-    )
+    forward_send = gather_slots(forward_route[0, :, 0], expert_count, capacity, forward_in)
 
     backward_dy = backward_in.astype(jnp.float32)
     along_dir = jnp.sum(backward_dy * unit_dir[None, :], axis=1)
@@ -370,9 +383,7 @@
         backward_weight[0][:, None] * (backward_dy - along_dir[:, None] * unit_dir[None, :])
     ).astype(jnp.bfloat16)
     backward_layout = dispatch_layout(backward_route[0, :, 0], expert_count, capacity)
-    backward_send = jnp.dot(backward_layout, sent_rows, preferred_element_type=jnp.float32).astype(
-        jnp.bfloat16
-    )
+    backward_send = gather_slots(backward_route[0, :, 0], expert_count, capacity, sent_rows)
     forward_rows, backward_rows = spread_to_holders(
         forward_send.reshape(expert_count, capacity, feature_count),
         backward_send.reshape(expert_count, capacity, feature_count),

time: 320 us -> 328 us (1.025)
  local copies, waits for them, and re-layouts: 4.92 us -> 17.4 us
  waiting for transfers between devices: 46.6 us -> 38.2 us
  other arithmetic: 8.54 us -> 16.1 us
  matrix products: 22.9 us -> 18.4 us
    ppermute x2, waiting for transfers between devices: 46.6 us -> 38.2 us  [shifted(): return lax.ppermute(value, axis, pairs)]
    gather x0 -> x2, local copies, waits for them, and re-layouts: none -> 8.02 us  [gather_slots(): return padded[slot_token]]
    dot_general x2 -> x0, matrix products: 4.54 us -> none  [the longest x1 2.78 us: body(): jnp.dot(forward_layout, forward_in, preferred_element_type=jnp.float32)]
  transfers between devices with their start and end apart: 2 -> 2, of which waited for: 2 -> 2; matrix products, arithmetic and copies ran while one was open for 3% -> 5% of each run, Pallas kernels for 0% -> 0%
where the time goes in v14:
time: 328 us; the launch traced here: 327 us
  Pallas kernels  223 us (68%)
  waiting for transfers between devices  38.2 us (12%)
  matrix products  18.4 us (6%)
  local copies, waits for them, and re-layouts  17.4 us (5%)
  other arithmetic  16.1 us (5%)
  starting transfers between devices  11.5 us (4%)
    pallas_call x1, Pallas kernels, spread_to_holders(): pl.pallas_call(functools.partial(spread_kernel, groups), out_shape=[rows]...  123 us
    pallas_call x1, Pallas kernels, collect_from_holders(): pl.pallas_call(functools.partial(collect_kernel, groups), out_shape=jax.S...  101 us
    ppermute x2, waiting for transfers between devices, shifted(): return lax.ppermute(value, axis, pairs)  38.2 us
    ppermute x2, starting transfers between devices, shifted(): return lax.ppermute(value, axis, pairs)  11.5 us
    gather x2, local copies, waits for them, and re-layouts, gather_slots(): return padded[slot_token]  8.02 us
  transfers between devices with their start and end apart: 2, of which 2 were waited for; matrix products, arithmetic and copies ran while one was open for 5% of the time, Pallas kernels for 0%

profile of v14, /device:TPU:24, one launch (start us, length us, event | category | flops | bytes accessed | tf_op | source)
XLA Modules:
  0.0 326.8 jit_solution(18174213954776301147)
XLA Ops:
  0.6 9.4 %collective-permute-start.1 = (bf16[1,128,3584]{2,1,0:T(8,128)(2,1)}, bf16[1,128,3584]{2,1,0:T(8,128)(2,1)}, u32[]{:S(2)}, u32[]{:S(2)}) collective-permute-start(bf16[1,128,3584]{2,1,0:T(8,128)(2,1)} %param.19), channel_id=1, source_target_pairs={{32,0},{64,32},{96,64},{128,96},{160,128},{192,160},{224,192},{33,... | collective-permute-start | bytes 2752520 | tf_op jit(solution)/shard_map/ppermute | solution.py:22
  10.1 2.1 collective-permute-start
  12.1 1.3 multiply_reduce_fusion.1
  14.2 0.7 fusion.25
  15.1 0.9 select_reduce_fusion
  16.7 1.0 scatter_custom_fusion.1
  19.2 0.8 select_reduce_fusion.1
  20.7 1.0 scatter_custom_fusion
  21.7 1.0 copy.21
  22.8 1.0 copy.22
  24.4 0.8 divide_reduce_fusion
  25.2 1.2 multiply_add_fusion
  26.4 1.2 multiply_add_fusion.1
  27.6 1.0 reverse_select_fusion
  28.6 22.3 %collective-permute-done.1 = bf16[1,128,3584]{2,1,0:T(8,128)(2,1)} collective-permute-done((bf16[1,128,3584]{2,1,0:T(8,128)(2,1)}, bf16[1,128,3584]{2,1,0:T(8,128)(2,1)}, u32[]{:S(2)}, u32[]{:S(2)}) %collective-permute-start.1) | collective-permute-done | bytes 917536 | tf_op jit(solution)/shard_map/ppermute | solution.py:22
  50.9 1.6 fusion.5
  53.4 16.0 %collective-permute-done = bf16[1,128,3584]{2,1,0:T(8,128)(2,1)} collective-permute-done((bf16[1,128,3584]{2,1,0:T(8,128)(2,1)}, bf16[1,128,3584]{2,1,0:T(8,128)(2,1)}, u32[]{:S(2)}, u32[]{:S(2)}) %collective-permute-start) | collective-permute-done | bytes 917536 | tf_op jit(solution)/shard_map/ppermute | solution.py:22
  69.4 1.3 bitcast_select_fusion.1
  70.7 0.9 copy-done.3
  71.6 1.0 concatenate.12
  72.6 2.6 gather_fusion.1
  75.2 5.4 %gather_fusion = bf16[192,3584]{1,0:T(8,128)(2,1)} fusion(bf16[129,3584]{1,0:T(8,128)(2,1)} %concatenate.12, s32[1024]{0:T(1024)} %pad_clamp_fusion.1), kind=kCustom, calls=%fused_computation | custom fusion | bytes 2753280 | tf_op jit(solution)/shard_map/gather | solution.py:49
  80.6 122.5 %shard_map.157 = (bf16[2,2,8,24,3584]{4,3,2,1,0:T(8,128)(2,1)}, bf16[2,2,8,24,3584]{4,3,2,1,0:T(8,128)(2,1)}) custom-call(bf16[8,24,3584]{2,1,0:T(8,128)(2,1)} %bitcast.76, bf16[8,24,3584]{2,1,0:T(8,128)(2,1)} %bitcast.75), custom_call_target="tpu_custom_call" | custom-call | tf_op jit(solution)/shard_map/pallas_call | solution.py:193
  203.2 4.5 %fusion.20 = (bf16[768,256]{1,0:T(8,128)(2,1)S(1)}, bf16[768,256]{1,0:T(8,128)(2,1)S(1)}) fusion(bf16[2,2,8,24,256]{4,3,2,1,0:T(8,128)(2,1)S(1)} %copy-done.7, bf16[2,2,8,24,256]{4,3,2,1,0:T(8,128)(2,1)S(1)} %copy-done.8, bf16[768,3584]{1,0:T(8,128)(2,1)} %bitcast.93, bf16[1,256,3584]{2,1,0:T(8,128)(2,1)S(1)} %copy-done), kind=kOutput, calls=%fused_computation.38 | convolution fusion | flops 1412235264 | bytes 8912896 | tf_op jit(solution)/shard_map/dot_general | solution.py:63
  208.0 1.6 fusion.37
  209.6 1.6 fusion.11
  211.1 4.0 %convolution_convert_fusion.1 = bf16[768,3584]{1,0:T(8,128)(2,1)} fusion(bf16[768,256]{1,0:T(8,128)(2,1)S(1)} %fusion.11, bf16[1,256,3584]{2,1,0:T(8,128)(2,1)S(1)} %copy-done), kind=kOutput, calls=%fused_computation.5 | convolution fusion | flops 1412038656 | bytes 7733248 | tf_op jit(solution)/shard_map/dot_general | solution.py:57
  215.1 4.9 %convolution_convert_fusion = bf16[768,3584]{1,0:T(8,128)(2,1)} fusion(bf16[3584,256]{1,0:T(8,128)(2,1)S(1)} %bitcast.95, bf16[3584,256]{1,0:T(8,128)(2,1)S(1)} %bitcast.94, bf16[768,256]{1,0:T(8,128)(2,1)S(1)} %get-tuple-element.10, bf16[768,256]{1,0:T(8,128)(2,1)S(1)} %get-tuple-element.9), kind=kOutput, calls=%fused_computation.4 | convolution fusion | flops 2830237696 | bytes 9961472 | tf_op jit(solution)/shard_map/dot_general | solution.py:76
  220.0 100.9 %shard_map.158 = bf16[2,8,24,3584]{3,2,1,0:T(8,128)(2,1)} custom-call(bf16[2,2,8,24,3584]{4,3,2,1,0:T(8,128)(2,1)} %bitcast.74, bf16[2,2,8,24,3584]{4,3,2,1,0:T(8,128)(2,1)} %bitcast.78), custom_call_target="tpu_custom_call" | custom-call | tf_op jit(solution)/shard_map/pallas_call | solution.py:319
  320.9 2.0 fusion.39
  323.0 1.4 fusion.1
  325.5 1.2 fusion.12
  (51 shorter events, 6.0 us)
Async XLA Ops:
  0.6 202.5 %copy-start = (bf16[1,256,3584]{2,1,0:T(8,128)(2,1)S(1)}, bf16[1,256,3584]{2,1,0:T(8,128)(2,1)}, u32[]{:S(2)}) copy-start(bf16[1,256,3584]{2,1,0:T(8,128)(2,1)} %param.26) | copy-start | bytes 5505028
  0.6 50.2 %collective-permute-start.1 = (bf16[1,128,3584]{2,1,0:T(8,128)(2,1)}, bf16[1,128,3584]{2,1,0:T(8,128)(2,1)}, u32[]{:S(2)}, u32[]{:S(2)}) collective-permute-start(bf16[1,128,3584]{2,1,0:T(8,128)(2,1)} %param.19), channel_id=1, source_target_pairs={{32,0},{64,32},{96,64},{128,96},{160,128},{192,160},{224,192},{33,... | collective-permute-start | bytes 2752520 | tf_op jit(solution)/shard_map/ppermute | solution.py:22
  10.1 59.3 %collective-permute-start = (bf16[1,128,3584]{2,1,0:T(8,128)(2,1)}, bf16[1,128,3584]{2,1,0:T(8,128)(2,1)}, u32[]{:S(2)}, u32[]{:S(2)}) collective-permute-start(bf16[1,128,3584]{2,1,0:T(8,128)(2,1)} %param.15), channel_id=1, source_target_pairs={{0,32},{32,64},{64,96},{96,128},{128,160},{160,192},{192,224},{1,3... | collective-permute-start | bytes 2752520 | tf_op jit(solution)/shard_map/ppermute | solution.py:22
  14.9 35.9 %copy-start.5 = (bf16[128,3584]{1,0:T(8,128)(2,1)S(1)}, bf16[128,3584]{1,0:T(8,128)(2,1)}, u32[]{:S(2)}) copy-start(bf16[128,3584]{1,0:T(8,128)(2,1)} %param.18) | copy-start | bytes 2752516
  16.1 2.3 copy-start.13
  20.1 0.7 copy-start.14
  27.6 24.9 %copy-start.10 = (f32[1,128]{1,0:T(1,128)S(1)}, f32[1,128]{1,0:T(1,128)}, u32[]{:S(2)}) copy-start(f32[1,128]{1,0:T(1,128)} %param.21) | copy-start | bytes 1540
  52.5 0.9 copy-start.1
  52.5 16.9 %copy-start.6 = (bf16[128,3584]{1,0:T(8,128)(2,1)S(1)}, bf16[128,3584]{1,0:T(8,128)(2,1)}, u32[]{:S(2)}) copy-start(bf16[128,3584]{1,0:T(8,128)(2,1)} %param.14) | copy-start | bytes 2752516
  70.7 0.9 copy-start.3
  80.6 122.6 %copy-start.7 = (bf16[2,2,8,24,256]{4,3,2,1,0:T(8,128)(2,1)S(1)}, bf16[2,2,8,24,256]{4,3,2,1,0:T(8,128)(2,1)}, u32[]{:S(2)}) copy-start(bf16[2,2,8,24,256]{4,3,2,1,0:T(8,128)(2,1)} %get-tuple-element.19) | copy-start | bytes 1179652
  80.6 122.6 %copy-start.8 = (bf16[2,2,8,24,256]{4,3,2,1,0:T(8,128)(2,1)S(1)}, bf16[2,2,8,24,256]{4,3,2,1,0:T(8,128)(2,1)}, u32[]{:S(2)}) copy-start(bf16[2,2,8,24,256]{4,3,2,1,0:T(8,128)(2,1)} %get-tuple-element.20) | copy-start | bytes 1179652
  203.2 4.5 %copy-start.16 = (bf16[2,2,8,24,3584]{4,3,2,1,0:T(8,128)(2,1)S(1)}, bf16[2,2,8,24,3584]{4,3,2,1,0:T(8,128)(2,1)}, u32[]{:S(2)}) copy-start(bf16[2,2,8,24,3584]{4,3,2,1,0:T(8,128)(2,1)} %get-tuple-element.7) | copy-start | bytes 16515076
  203.2 4.7 %copy-start.17 = (bf16[1,3584,256]{2,1,0:T(8,128)(2,1)S(1)}, bf16[1,3584,256]{2,1,0:T(8,128)(2,1)}, u32[]{:S(2)}) copy-start(bf16[1,3584,256]{2,1,0:T(8,128)(2,1)} %param.24) | copy-start | bytes 5505028
  208.0 1.6 copy-start.18
  320.9 2.1 copy-start.2
  320.9 2.1 copy-start.15
  322.9 1.4 copy-start.11
  323.0 1.4 copy-start.12
  324.4 1.2 copy-start.4
  324.9 1.9 copy-start.9

commit v15 on v12

--- a/solution.py
+++ b/solution.py
@@ -45,8 +45,8 @@
 def expert_backward(slot_rows, gate_saved, up_saved, weights):
     gate_cols, up_cols, down_rows = weights
     contract = (((1,), (1,)), ((), ()))
-    grad_hidden = lax.dot_general(
-        slot_rows, down_rows, contract, preferred_element_type=jnp.float32
+    grad_hidden = lax.optimization_barrier(
+        lax.dot_general(slot_rows, down_rows, contract, preferred_element_type=jnp.float32)
     )
     gate_pre = gate_saved.astype(jnp.float32)
     up_pre = up_saved.astype(jnp.float32)

time: 320 us -> 321 us (level)
  no operation moved by 1% of the time
where the time goes in v15:
time: 321 us
  Pallas kernels  223 us (69%)
  waiting for transfers between devices  46.6 us (15%)
  matrix products  22.8 us (7%)
  starting transfers between devices  11.4 us (4%)
  other arithmetic  8.99 us (3%)
  local copies, waits for them, and re-layouts  5.71 us (2%)
    pallas_call x1, Pallas kernels, spread_to_holders(): pl.pallas_call(functools.partial(spread_kernel, groups), out_shape=[rows]...  123 us
    pallas_call x1, Pallas kernels, collect_from_holders(): pl.pallas_call(functools.partial(collect_kernel, groups), out_shape=jax.S...  101 us
    ppermute x2, waiting for transfers between devices, shifted(): return lax.ppermute(value, axis, pairs)  46.6 us
    ppermute x2, starting transfers between devices, shifted(): return lax.ppermute(value, axis, pairs)  11.4 us
  transfers between devices with their start and end apart: 2, of which 2 were waited for; matrix products, arithmetic and copies ran while one was open for 3% of the time, Pallas kernels for 0%

profile of v15, /device:TPU:24, one launch (start us, length us, event | category | flops | bytes accessed | tf_op | source)
XLA Modules:
  0.0 320.5 jit_solution(8506745148174986528)
XLA Ops:
  0.6 0.0 copy-start
  0.7 9.4 %collective-permute-start.1 = (bf16[1,128,3584]{2,1,0:T(8,128)(2,1)}, bf16[1,128,3584]{2,1,0:T(8,128)(2,1)}, u32[]{:S(2)}, u32[]{:S(2)}) collective-permute-start(bf16[1,128,3584]{2,1,0:T(8,128)(2,1)} %param.19), channel_id=1, source_target_pairs={{32,0},{64,32},{96,64},{128,96},{160,128},{192,160},{224,192},{33,... | collective-permute-start | bytes 2752520 | tf_op jit(solution)/shard_map/ppermute | solution.py:22
  10.1 2.0 collective-permute-start
  12.1 1.3 multiply_reduce_fusion.1
  14.2 0.7 fusion.29
  14.9 0.2 reduce_window_sum.18
  15.1 0.8 select_reduce_fusion
  15.9 0.7 fusion.30
  16.7 0.2 reduce_window_sum.17
  16.9 1.0 copy.21
  17.9 1.0 copy.22
  18.9 0.2 select_reduce_fusion.1
  19.2 0.1 reverse_select_fusion
  19.4 31.5 %collective-permute-done.1 = bf16[1,128,3584]{2,1,0:T(8,128)(2,1)} collective-permute-done((bf16[1,128,3584]{2,1,0:T(8,128)(2,1)}, bf16[1,128,3584]{2,1,0:T(8,128)(2,1)}, u32[]{:S(2)}, u32[]{:S(2)}) %collective-permute-start.1) | collective-permute-done | bytes 917536 | tf_op jit(solution)/shard_map/ppermute | solution.py:22
  50.9 1.6 fusion.5
  52.5 1.8 convolution_convert_fusion.2
  54.3 15.1 %collective-permute-done = bf16[1,128,3584]{2,1,0:T(8,128)(2,1)} collective-permute-done((bf16[1,128,3584]{2,1,0:T(8,128)(2,1)}, bf16[1,128,3584]{2,1,0:T(8,128)(2,1)}, u32[]{:S(2)}, u32[]{:S(2)}) %collective-permute-start) | collective-permute-done | bytes 917536 | tf_op jit(solution)/shard_map/ppermute | solution.py:22
  69.4 2.8 convolution_convert_fusion.3
  72.2 122.5 %shard_map.157 = (bf16[2,2,8,24,3584]{4,3,2,1,0:T(8,128)(2,1)}, bf16[2,2,8,24,3584]{4,3,2,1,0:T(8,128)(2,1)}) custom-call(bf16[8,24,3584]{2,1,0:T(8,128)(2,1)} %bitcast.64, bf16[8,24,3584]{2,1,0:T(8,128)(2,1)} %bitcast.62), custom_call_target="tpu_custom_call" | custom-call | tf_op jit(solution)/shard_map/pallas_call | solution.py:178
  194.8 4.3 %fusion.8 = f32[768,256]{1,0:T(8,128)S(1)} fusion(bf16[768,3584]{1,0:T(8,128)(2,1)} %bitcast.80, bf16[1,256,3584]{2,1,0:T(8,128)(2,1)S(1)} %copy-done), kind=kOutput, calls=%fused_computation.16 | convolution fusion | flops 1409286144 | bytes 8126464 | tf_op jit(solution)/shard_map/dot_general | solution.py:49
  199.1 0.5 fusion.24
  199.6 1.0 copy-done.13
  200.6 1.6 fusion.37
  202.2 1.6 fusion.11
  203.8 4.0 %convolution_convert_fusion.1 = bf16[768,3584]{1,0:T(8,128)(2,1)} fusion(bf16[768,256]{1,0:T(8,128)(2,1)S(1)} %fusion.11, bf16[1,256,3584]{2,1,0:T(8,128)(2,1)S(1)} %copy-done), kind=kOutput, calls=%fused_computation.1 | convolution fusion | flops 1412038656 | bytes 7733248 | tf_op jit(solution)/shard_map/dot_general | solution.py:42
  207.8 4.8 %convolution_convert_fusion = bf16[768,3584]{1,0:T(8,128)(2,1)} fusion(bf16[3584,256]{1,0:T(8,128)(2,1)S(1)} %bitcast.82, bf16[3584,256]{1,0:T(8,128)(2,1)S(1)} %bitcast.81, bf16[768,256]{1,0:T(8,128)(2,1)S(1)} %get-tuple-element.10, bf16[768,256]{1,0:T(8,128)(2,1)S(1)} %get-tuple-element.9), kind=kOutput, calls=%fused_computation | convolution fusion | flops 2830237696 | bytes 9961472 | tf_op jit(solution)/shard_map/dot_general | solution.py:61
  212.6 100.8 %shard_map.158 = bf16[2,8,24,3584]{3,2,1,0:T(8,128)(2,1)} custom-call(bf16[2,2,8,24,3584]{4,3,2,1,0:T(8,128)(2,1)} %bitcast.59, bf16[2,2,8,24,3584]{4,3,2,1,0:T(8,128)(2,1)} %bitcast.61), custom_call_target="tpu_custom_call" | custom-call | tf_op jit(solution)/shard_map/pallas_call | solution.py:304
  313.4 1.9 fusion.39
  315.4 1.4 fusion.1
  316.8 0.5 multiply_reduce_fusion
  317.3 0.6 copy-done.2
  318.0 2.6 fusion.12
  (35 shorter events, 0.1 us)
Async XLA Ops:
  0.6 194.1 %copy-start = (bf16[1,256,3584]{2,1,0:T(8,128)(2,1)S(1)}, bf16[1,256,3584]{2,1,0:T(8,128)(2,1)}, u32[]{:S(2)}) copy-start(bf16[1,256,3584]{2,1,0:T(8,128)(2,1)} %param.26) | copy-start | bytes 5505028
  0.6 18.5 %copy-start.3 = (f32[1,3584]{1,0:T(1,128)S(1)}, f32[1,3584]{1,0:T(1,128)}, u32[]{:S(2)}) copy-start(f32[1,3584]{1,0:T(1,128)} %param.27) | copy-start | bytes 43012
  0.7 18.5 %copy-start.4 = (s32[1,128,1]{1,2,0:T(1,128)S(1)}, s32[1,128,1]{1,2,0:T(1,128)}, u32[]{:S(2)}) copy-start(s32[1,128,1]{1,2,0:T(1,128)} %param.20) | copy-start | bytes 1540
  0.7 18.3 %copy-start.5 = (s32[1,128,1]{1,2,0:T(1,128)S(1)}, s32[1,128,1]{1,2,0:T(1,128)}, u32[]{:S(2)}) copy-start(s32[1,128,1]{1,2,0:T(1,128)} %param.16) | copy-start | bytes 1540
  0.7 50.2 %collective-permute-start.1 = (bf16[1,128,3584]{2,1,0:T(8,128)(2,1)}, bf16[1,128,3584]{2,1,0:T(8,128)(2,1)}, u32[]{:S(2)}, u32[]{:S(2)}) collective-permute-start(bf16[1,128,3584]{2,1,0:T(8,128)(2,1)} %param.19), channel_id=1, source_target_pairs={{32,0},{64,32},{96,64},{128,96},{160,128},{192,160},{224,192},{33,... | collective-permute-start | bytes 2752520 | tf_op jit(solution)/shard_map/ppermute | solution.py:22
  10.1 59.3 %collective-permute-start = (bf16[1,128,3584]{2,1,0:T(8,128)(2,1)}, bf16[1,128,3584]{2,1,0:T(8,128)(2,1)}, u32[]{:S(2)}, u32[]{:S(2)}) collective-permute-start(bf16[1,128,3584]{2,1,0:T(8,128)(2,1)} %param.15), channel_id=1, source_target_pairs={{0,32},{32,64},{64,96},{96,128},{128,160},{160,192},{192,224},{1,3... | collective-permute-start | bytes 2752520 | tf_op jit(solution)/shard_map/ppermute | solution.py:22
  19.1 33.4 %copy-start.9 = (s32[128]{0:T(128)}, s32[128]{0:T(128)S(1)}, u32[]{:S(2)}) copy-start(s32[128]{0:T(128)S(1)} %multiply_add_fusion) | copy-start | bytes 1540
  19.2 50.3 %copy-start.6 = (s32[128]{0:T(128)}, s32[128]{0:T(128)S(1)}, u32[]{:S(2)}) copy-start(s32[128]{0:T(128)S(1)} %multiply_add_fusion.1) | copy-start | bytes 1540
  19.2 33.3 %copy-start.11 = (f32[1,128]{1,0:T(1,128)S(1)}, f32[1,128]{1,0:T(1,128)}, u32[]{:S(2)}) copy-start(f32[1,128]{1,0:T(1,128)} %param.21) | copy-start | bytes 1540
  52.5 16.9 %copy-start.1 = (bf16[128,3584]{1,0:T(8,128)(2,1)S(1)}, bf16[128,3584]{1,0:T(8,128)(2,1)}, u32[]{:S(2)}) copy-start(bf16[128,3584]{1,0:T(8,128)(2,1)} %param.14) | copy-start | bytes 2752516
  194.7 4.8 %slice-start = ((s8[5505024]{0:T(1024)(128)(4,1)}), s8[4194304]{0:T(1024)(128)(4,1)S(1)}, s32[]{:S(2)}) async-start(s8[5505024]{0:T(1024)(128)(4,1)} %bitcast.76), calls=%async_computation | async-start | bytes 8388608
  194.8 4.8 %slice-start.1 = ((s8[5505024]{0:T(1024)(128)(4,1)}), s8[1310720]{0:T(1024)(128)(4,1)S(1)}, s32[]{:S(2)}) async-start(s8[5505024]{0:T(1024)(128)(4,1)} %bitcast.76), calls=%async_computation.1 | async-start | bytes 2621440
  199.1 1.5 copy-start.13
  200.6 1.6 copy-start.14
  313.4 2.0 copy-start.10
  315.4 1.4 copy-start.7
  315.4 1.4 copy-start.12
  316.8 1.2 copy-start.2
  317.3 3.2 copy-start.8
